TPU v7x, 32 devices: a whole 2x2x4 slice. The times are simulated.
32 devices in a mesh: wide: 16 (over z, x, core), narrow: 2 (over y).
Axes of the slice: x: 2, y: 2, z: 4, core: 2. Of those that a mesh axis runs over, the one named last changes fastest.
Arguments:
- query_rows: bfloat16 [640, 6144], P('wide', 'narrow'), may hold values from -30 to 30
- key_rows: bfloat16 [640, 6144], P('wide', 'narrow'), may hold values from -10 to 10
- value_rows: bfloat16 [640, 6144], P('wide', 'narrow'), may hold values from -6 to 6
- mid_grad: bfloat16 [5120, 2048], P(('wide', 'narrow')), may hold values from -6 to 6
- link_weight: bfloat16 [768, 2048], replicated, may hold values from -0.21875 to 0.21875
Outputs:
- query_grad: bfloat16 [640, 6144], P('wide', 'narrow')
- key_grad: bfloat16 [640, 6144], P('wide', 'narrow')
- value_grad: bfloat16 [640, 6144], P('wide', 'narrow')
All inputs are finite; a program needn't handle non-finite values.
Results may differ from a plain program's by a relative error of at most 0.0066.
Values may be sent and summed in bfloat16 or wider, within the bound.
No kernel may reach another device: no remote copies, remote signals or barrier semaphores. Data moves between devices by JAX's collectives and lax.ppermute only.
A program may use at most 64 MiB of HBM per device.

v0:
```python
import math

import jax
import jax.numpy as jnp
from jax import lax
from jax.sharding import PartitionSpec as P

HD = 128
PATCH = 8


lowest = -1e30


def on_device(query_rows, key_rows, value_rows, mid_grad, link_weight):
    groups = lax.axis_size("narrow")
    patches = query_rows.shape[0]
    columns = query_rows.shape[1]
    heads_here = columns // HD
    scaling = 1.0 / math.sqrt(HD)
    local_patches = mid_grad.shape[0] // PATCH
    grouped = mid_grad.reshape(local_patches, groups, PATCH // groups, mid_grad.shape[1])
    moved = jnp.einsum(
        "abcm,pm->abcp",
        lax.all_to_all(grouped, "narrow", split_axis=1, concat_axis=0, tiled=True),
        link_weight,
        preferred_element_type=jnp.float32,
    ).astype(jnp.bfloat16)
    incoming = moved.reshape(patches, columns)
    incoming_heads = incoming.reshape(patches, heads_here, HD)
    query_heads = query_rows.reshape(patches, heads_here, HD)
    key_heads = key_rows.reshape(patches, heads_here, HD)
    value_heads = value_rows.reshape(patches, heads_here, HD)
    own_pos = lax.axis_index("wide") * patches + jnp.arange(patches, dtype=jnp.int32)
    total_rows = patches * lax.axis_size("wide")
    empty_store = jnp.zeros((total_rows, columns), jnp.bfloat16)
    fold_start = (
        jnp.full((heads_here, patches), lowest, jnp.float32),
        jnp.zeros((heads_here, patches), jnp.float32),
        jnp.zeros((heads_here, patches), jnp.float32),
        empty_store,
        empty_store,
    )
    pieces = (
        lax.all_gather(key_rows, "wide", axis=0, tiled=True),
        lax.all_gather(value_rows, "wide", axis=0, tiled=True),
    )
    key_piece, value_piece = pieces
    piece_rows = key_piece.shape[0]
    key_split = key_piece.reshape(piece_rows, heads_here, HD)
    value_split = value_piece.reshape(piece_rows, heads_here, HD)
    piece_pos = jnp.arange(piece_rows, dtype=jnp.int32)
    allowed = piece_pos[None, None, :] <= own_pos[None, :, None]
    scores = (
        jnp.einsum("qhd,khd->hqk", query_heads, key_split, preferred_element_type=jnp.float32)
        * scaling
    )
    scores = jnp.where(allowed, scores, lowest)
    products = jnp.einsum(
        "qhd,khd->hqk", incoming_heads, value_split, preferred_element_type=jnp.float32
    )
    old_max, old_total, old_tilt = fold_start[:3]
    new_max = jnp.maximum(old_max, jnp.max(scores, axis=2))
    expo = jnp.where(allowed, jnp.exp(scores - new_max[:, :, None]), 0.0)
    stats = (new_max, jnp.sum(expo, axis=2), jnp.sum(expo * products, axis=2))
    key_store = pieces[0]
    value_store = pieces[1]
    folded = stats + (key_store, value_store)
    run_max, run_total, run_tilt = (folded[0], folded[1], folded[2])
    log_total = run_max + jnp.log(run_total)
    row_delta = run_tilt / run_total
    key_all = folded[3].reshape(total_rows, heads_here, HD)
    value_all = folded[4].reshape(total_rows, heads_here, HD)
    every_pos = jnp.arange(total_rows, dtype=jnp.int32)
    allowed_q = every_pos[None, None, :] <= own_pos[None, :, None]
    scores_q = (
        jnp.einsum("qhd,khd->hqk", query_heads, key_all, preferred_element_type=jnp.float32)
        * scaling
    )
    products_q = jnp.einsum(
        "qhd,khd->hqk", incoming_heads, value_all, preferred_element_type=jnp.float32
    )
    weights_q = jnp.where(
        allowed_q, jnp.exp(jnp.where(allowed_q, scores_q, lowest) - log_total[:, :, None]), 0.0
    )
    score_grad_q = (weights_q * (products_q - row_delta[:, :, None])).astype(jnp.bfloat16)
    query_accum = jnp.einsum(
        "hqk,khd->qhd", score_grad_q, key_all, preferred_element_type=jnp.float32
    )
    query_grad = (query_accum * scaling).astype(jnp.bfloat16).reshape(patches, columns)
    total_all, delta_all = (
        lax.all_gather(log_total, "wide", axis=1, tiled=True),
        lax.all_gather(row_delta, "wide", axis=1, tiled=True),
    )
    query_piece = lax.all_gather(query_rows, "wide", axis=0, tiled=True)
    grad_piece = lax.all_gather(incoming, "wide", axis=0, tiled=True)
    piece_rows = query_piece.shape[0]
    query_split = query_piece.reshape(piece_rows, heads_here, HD)
    grad_split = grad_piece.reshape(piece_rows, heads_here, HD)
    piece_pos = jnp.arange(piece_rows, dtype=jnp.int32)
    allowed = own_pos[None, None, :] <= piece_pos[None, :, None]
    scores = (
        jnp.einsum("qhd,khd->hqk", query_split, key_heads, preferred_element_type=jnp.float32)
        * scaling
    )
    scores = jnp.where(allowed, scores, lowest)
    products = jnp.einsum(
        "qhd,khd->hqk", grad_split, value_heads, preferred_element_type=jnp.float32
    )
    weights = jnp.where(allowed, jnp.exp(scores - total_all[:, :, None]), 0.0)
    score_grad = (weights * (products - delta_all[:, :, None])).astype(jnp.bfloat16)
    key_accum = jnp.einsum(
        "hqk,qhd->khd", score_grad, query_split, preferred_element_type=jnp.float32
    )
    value_accum = jnp.einsum(
        "hqk,qhd->khd", weights.astype(jnp.bfloat16), grad_split, preferred_element_type=jnp.float32
    )
    key_accum, value_accum = (key_accum, value_accum)
    key_grad = (key_accum * scaling).astype(jnp.bfloat16).reshape(patches, columns)
    value_grad = value_accum.astype(jnp.bfloat16).reshape(patches, columns)
    return (query_grad, key_grad, value_grad)


def solution(mesh):
    in_specs = (
        P("wide", "narrow"),
        P("wide", "narrow"),
        P("wide", "narrow"),
        P(("wide", "narrow"), None),
        P(),
    )
    out_specs = (P("wide", "narrow"), P("wide", "narrow"), P("wide", "narrow"))
    return jax.shard_map(
        on_device, mesh=mesh, in_specs=in_specs, out_specs=out_specs, check_vma=False
    )
```

profile of v0, /device:TPU:0, one launch (start us, length us, event | category | flops | bytes accessed | tf_op | source)
XLA Modules:
  0.0 240.6 jit_solution(15646590345335519802)
XLA Ops:
  7.2 0.7 all-gather.7.cloned.1.call-update
  8.0 0.7 all-gather.9.cloned.1.call-update
  8.7 0.7 all-gather.11.cloned.1.call-update
  9.4 2.3 reshape.125
  11.7 1.4 copy.35
  13.1 13.4 %all_to_all.15 = bf16[20,2,4,2048]{3,2,0,1:T(4,128)(2,1)S(1)} all-to-all(bf16[20,2,4,2048]{3,2,0,1:T(4,128)(2,1)S(1)} %copy.35), channel_id=1, replica_groups=mesh['wide'=16,'narrow'=2] {'narrow'}, dimensions={1} | all-to-all | bytes 1310720 | tf_op jit(solution)/shard_map/all_to_all | solution.py:25
  26.6 1.5 fusion.25
  28.0 0.7 copy.67
  28.8 0.1 iota_compare_fusion.1
  29.0 0.8 copy.37
  29.8 1.7 reshape_reshape.3
  31.5 30.6 %all-gather.7.cloned.1.call-done = bf16[640,3072]{1,0:T(8,128)(2,1)} async-done(((bf16[40,3072]{1,0:T(8,128)(2,1)}), bf16[640,3072]{1,0:T(8,128)(2,1)}) %all-gather.7.cloned.1.call-update) | async-done | bytes 3932176 | tf_op jit(solution)/shard_map/all_gather | solution.py:45
  62.1 6.3 %copy.32 = bf16[640,3072]{0,1:T(8,128)(2,1)} copy(bf16[640,3072]{1,0:T(8,128)(2,1)} %all-gather.7.cloned.1.call-done) | data formatting | bytes 7864320 | tf_op jit(solution)/shard_map/all_gather | solution.py:45
  68.4 43.6 %all-gather.9.cloned.1.call-done = bf16[640,3072]{1,0:T(8,128)(2,1)} async-done(((bf16[40,3072]{1,0:T(8,128)(2,1)}), bf16[640,3072]{1,0:T(8,128)(2,1)}) %all-gather.9.cloned.1.call-update) | async-done | bytes 3932176 | tf_op jit(solution)/shard_map/all_gather | solution.py:46
  112.0 6.2 %copy.38 = bf16[640,3072]{0,1:T(8,128)(2,1)} copy(bf16[640,3072]{1,0:T(8,128)(2,1)} %all-gather.9.cloned.1.call-done) | data formatting | bytes 7864320 | tf_op jit(solution)/shard_map/all_gather | solution.py:46
  118.3 3.3 %fusion.57 = (f32[24,40]{1,0:T(8,128)S(1)}, f32[24,40,640]{2,1,0:T(8,128)S(1)}) fusion(bf16[640,24,128]{0,2,1:T(8,128)(2,1)} %bitcast.76, pred[40,640]{1,0:T(8,128)(4,1)S(1)} %iota_compare_fusion.1, bf16[40,3072]{1,0:T(8,128)(2,1)S(1)} %copy-done.3), kind=kOutput, calls=%fused_computation.62 | convolution fusion | flops 159128640 | bytes 6664960 | tf_op jit(solution)/shard_map/qhd,khd->hqk/dot_general | solution.py:77
  121.6 0.2 copy-done.2
  121.8 1.4 fusion.2
  123.2 0.7 copy-done.1
  123.9 1.8 fusion.33
  125.7 0.7 copy.94
  126.4 19.6 %all-gather = f32[16,40,24]{1,2,0:T(8,128)S(1)} all-gather(f32[1,40,24]{1,2,0:T(8,128)S(1)} %bitcast.88), channel_id=1, replica_groups=mesh['wide'=16,'narrow'=2] {'wide'}, dimensions={0}, use_global_device_ids=true | all-gather | bytes 65280 | tf_op jit(solution)/shard_map/all_gather | solution.py:92
  146.1 0.1 reshape.137
  146.2 18.5 %all-gather.1 = f32[16,40,24]{1,2,0:T(8,128)S(1)} all-gather(f32[1,40,24]{1,2,0:T(8,128)S(1)} %bitcast.87), channel_id=1, replica_groups=mesh['wide'=16,'narrow'=2] {'wide'}, dimensions={0}, use_global_device_ids=true | all-gather | bytes 65280 | tf_op jit(solution)/shard_map/all_gather | solution.py:93
  164.7 0.1 reshape.139
  164.9 6.4 %copy.43 = bf16[640,3072]{0,1:T(8,128)(2,1)} copy(bf16[640,3072]{1,0:T(8,128)(2,1)} %all-gather.11.cloned.1.call-done) | data formatting | bytes 7864320 | tf_op jit(solution)/shard_map/all_gather | solution.py:95
  171.4 4.5 %fusion.43 = f32[24,640,40]{1,2,0:T(8,128)} fusion(bf16[640,24,128]{0,2,1:T(8,128)(2,1)} %bitcast.78, bf16[40,3072]{1,0:T(8,128)(2,1)S(1)} %copy-done.4), kind=kOutput, calls=%fused_computation.43 | convolution fusion | flops 157286400 | bytes 6635520 | tf_op jit(solution)/shard_map/qhd,khd->hqk/dot_general | solution.py:103
  175.9 37.4 %all-gather.13.cloned.1.call-done = bf16[640,3072]{1,0:T(8,128)(2,1)} async-done(((bf16[40,3072]{1,0:T(8,128)(2,1)}), bf16[640,3072]{1,0:T(8,128)(2,1)}) %all-gather.13.cloned.1.call-update) | async-done | bytes 3932176 | tf_op jit(solution)/shard_map/all_gather | solution.py:96
  213.3 6.3 %copy.48 = bf16[640,3072]{0,1:T(8,128)(2,1)} copy(bf16[640,3072]{1,0:T(8,128)(2,1)} %all-gather.13.cloned.1.call-done) | data formatting | bytes 7864320 | tf_op jit(solution)/shard_map/all_gather | solution.py:96
  219.6 5.3 %fusion.35 = bf16[24,5,8,128]{3,2,1,0:T(8,128)(2,1)} fusion(bf16[640,24,128]{0,2,1:T(8,128)(2,1)} %bitcast.81, f32[24,640,40]{1,2,0:T(8,128)} %fusion.43, f32[24,640]{1,0:T(8,128)S(1)} %bitcast.89, pred[640,40]{0,1:T(8,128)(4,1)S(1)} %iota_compare_fusion), kind=kOutput, calls=%fused_computation.36 | convolution fusion | flops 160481280 | bytes 6722560 | tf_op jit(solution)/shard_map/hqk,qhd->khd/dot_general | solution.py:115
  224.9 7.3 %fusion.34 = bf16[24,5,8,128]{3,2,1,0:T(8,128)(2,1)} fusion(bf16[640,24,128]{0,2,1:T(8,128)(2,1)} %bitcast.79, f32[24,640,40]{1,2,0:T(8,128)} %fusion.43, bf16[640,24,128]{0,2,1:T(8,128)(2,1)} %bitcast.82, f32[24,640]{1,0:T(8,128)S(1)} %bitcast.91, f32[24,640]{1,0:T(8,128)S(1)} %bitcast.90, pred[640,40]{0,1:T(8,128)(4,1)S(1)} %iota_compare_fusion, ...), kind=kOutput, calls=%fused_computation.35 | convolution fusion | flops 319119360 | bytes 10961920 | tf_op jit(solution)/shard_map/hqk,qhd->khd/dot_general | solution.py:112
  232.1 1.9 copy_bitcast_fusion
  (24 shorter events, 0.4 us)
Async XLA Ops:
  7.2 19.4 %copy-start = (bf16[768,2048]{1,0:T(8,128)(2,1)S(1)}, bf16[768,2048]{1,0:T(8,128)(2,1)}, u32[]{:S(2)}) copy-start(bf16[768,2048]{1,0:T(8,128)(2,1)} %param.9) | copy-start | bytes 9437188
  7.2 54.9 %all-gather.7.cloned.1.call-start = ((), (), s32[]{:S(2)}) async-start(), calls=%async_computation.1 | async-start | bytes 4177920 | tf_op jit(solution)/shard_map/all_gather | solution.py:45
  7.9 104.1 %all-gather.9.cloned.1.call-start = ((), (), s32[]{:S(2)}) async-start(), calls=%async_computation.2 | async-start | bytes 4177920 | tf_op jit(solution)/shard_map/all_gather | solution.py:46
  8.7 156.2 %all-gather.11.cloned.1.call-start = ((), (), s32[]{:S(2)}) async-start(), calls=%async_computation.3 | async-start | bytes 4177920 | tf_op jit(solution)/shard_map/all_gather | solution.py:95
  9.4 203.9 %all-gather.13.cloned.1.call-start = ((), (), s32[]{:S(2)}) async-start(), calls=%async_computation.4 | async-start | bytes 4177920 | tf_op jit(solution)/shard_map/all_gather | solution.py:96
  68.4 49.9 %copy-start.3 = (bf16[40,3072]{1,0:T(8,128)(2,1)S(1)}, bf16[40,3072]{1,0:T(8,128)(2,1)}, u32[]{:S(2)}) copy-start(bf16[40,3072]{1,0:T(8,128)(2,1)} %param.5) | copy-start | bytes 737284
  118.3 3.5 %copy-start.2 = (bf16[640,3072]{0,1:T(8,128)(2,1)S(1)}, bf16[640,3072]{0,1:T(8,128)(2,1)}, u32[]{:S(2)}) copy-start(bf16[640,3072]{0,1:T(8,128)(2,1)} %copy.38) | copy-start | bytes 11796484
  118.3 3.5 %copy-start.5 = (bf16[40,24,128]{2,1,0:T(8,128)(2,1)S(1)}, bf16[40,24,128]{2,1,0:T(8,128)(2,1)}, u32[]{:S(2)}) copy-start(bf16[40,24,128]{2,1,0:T(8,128)(2,1)} %reshape_reshape.3) | copy-start | bytes 737284
  121.8 2.1 copy-start.1
  164.9 6.5 %copy-start.4 = (bf16[40,3072]{1,0:T(8,128)(2,1)S(1)}, bf16[40,3072]{1,0:T(8,128)(2,1)}, u32[]{:S(2)}) copy-start(bf16[40,3072]{1,0:T(8,128)(2,1)} %param.6) | copy-start | bytes 737284
  219.6 5.3 %copy-start.6 = (bf16[40,3072]{1,0:T(8,128)(2,1)S(1)}, bf16[40,3072]{1,0:T(8,128)(2,1)}, u32[]{:S(2)}) copy-start(bf16[40,3072]{1,0:T(8,128)(2,1)} %param.7) | copy-start | bytes 737284
Sparse Core Ops, SparseCore 0:
  10.3 51.7 all-gather.6
  64.3 47.6 all-gather.8
  114.3 48.4 all-gather.10
  164.9 48.3 all-gather.12
where the time goes:
time: 241 us
  waiting for transfers between devices  114 us (47%)
  blocking collectives  51.5 us (21%)
  local copies, waits for them, and re-layouts  36.1 us (15%)
  matrix products  25 us (10%)
  between operations  13.9 us (6%)
    all_gather x1, waiting for transfers between devices, on_device(): lax.all_gather(value_rows, 'wide', axis=0, tiled=True)  43.6 us
    all_gather x1, waiting for transfers between devices, on_device(): grad_piece = lax.all_gather(incoming, 'wide', axis=0, tiled=True)  37.4 us
    all_gather x1, waiting for transfers between devices, on_device(): lax.all_gather(key_rows, 'wide', axis=0, tiled=True)  30.6 us
    all_gather x1, blocking collectives, on_device(): lax.all_gather(log_total, 'wide', axis=1, tiled=True)  19.6 us
    all_gather x1, blocking collectives, on_device(): lax.all_gather(row_delta, 'wide', axis=1, tiled=True)  18.5 us
    all_to_all x1, blocking collectives, on_device(): lax.all_to_all(grouped, 'narrow', split_axis=1, concat_axis=0, tiled=True)  13.4 us
    dot_general x1, matrix products, on_device(): jnp.einsum('hqk,qhd->khd', score_grad, query_split, preferred_element_typ...  7.27 us
    all_gather x1, local copies, waits for them, and re-layouts, on_device(): query_piece = lax.all_gather(query_rows, 'wide', axis=0, tiled=True)  6.45 us
  transfers between devices with their start and end apart: 4, of which 3 were waited for; matrix products, arithmetic and copies ran while one was open for 16% of the time, Pallas kernels for 0%

commit v1 on v0

--- a/solution.py
+++ b/solution.py
@@ -3,16 +3,290 @@
 import jax
 import jax.numpy as jnp
 from jax import lax
+from jax.experimental import pallas as pl
+from jax.experimental.pallas import tpu as pltpu
 from jax.sharding import PartitionSpec as P
+
 
 HD = 128
 PATCH = 8
+TILE = 128
+ROOM = 24 << 20
 
 
 lowest = -1e30
 
 
+def in_order(chips):
+    far = list(range(chips // 2, chips))
+    near = list(range(1, chips // 2))[::-1]
+    return far[:2], far[2:] + near
+
+
+def local(kernel, ins, shapes, scratch=(), flops=0, final=False):
+    vmem = pl.BlockSpec(memory_space=pltpu.VMEM)
+    outs = [
+        jax.ShapeDtypeStruct(shape, jnp.bfloat16) if final else pltpu.VMEM(shape, jnp.bfloat16)
+        for shape in shapes
+    ]
+    moved = 2 * (sum(array.size for array in ins) + sum(math.prod(shape) for shape in shapes))
+    return pl.pallas_call(
+        kernel,
+        in_specs=[vmem] * len(ins),
+        out_specs=[vmem] * len(shapes),
+        out_shape=outs,
+        scratch_shapes=list(scratch),
+        compiler_params=pltpu.CompilerParams(vmem_limit_bytes=ROOM),
+        cost_estimate=pl.CostEstimate(flops=flops, bytes_accessed=moved, transcendentals=0),
+    )(*ins)
+
+
+def held(array):
+    return pltpu.with_memory_space_constraint(array, pltpu.VMEM)
+
+
+def where_am_i():
+    me = lax.axis_index("wide")
+    return me // 2, me % 2, lax.axis_index("narrow")
+
+
+def project(mid_grad, link_weight, groups):
+    rows, depth = mid_grad.shape
+    features = link_weight.shape[0]
+    patches, each = rows // PATCH, PATCH // groups
+
+    def kernel(grad_ref, link_ref, stay_ref, leave_ref, product):
+        side = where_am_i()[2]
+        for low in range(0, features, 256):
+            result = lax.dot_general(
+                grad_ref[...],
+                link_ref[low : low + 256],
+                (((1,), (1,)), ((), ())),
+                preferred_element_type=jnp.float32,
+            )
+            for slab in range(result.shape[1] // HD):
+                product[low // HD + slab] = result[:, slab * HD : (slab + 1) * HD]
+        for out, group in ((stay_ref, side), (leave_ref, 1 - side)):
+            for index in range(each):
+                for slab in range(features // HD):
+                    at = index * features + slab * HD
+                    picked = product[slab, pl.ds(group * each + index, patches, stride=PATCH), :]
+                    out[:, at : at + HD] = picked.astype(jnp.bfloat16)
+
+    return local(
+        kernel,
+        [mid_grad, link_weight],
+        [(patches, each * features)] * 2,
+        [pltpu.VMEM((features // HD, rows, HD), jnp.float32)],
+        2 * rows * depth * features,
+    )
+
+
+def pack(arrays, chips, steps):
+    rows, columns = arrays[0].shape
+    wide = columns // chips
+
+    def kernel(*refs):
+        ins, outs = refs[: len(arrays)], refs[len(arrays) :]
+        chip = where_am_i()[0]
+        for out, step in zip(outs, steps):
+            start = pl.multiple_of((chip ^ step) * wide, HD)
+            for which, ref in enumerate(ins):
+                out[:, which * wide : (which + 1) * wide] = ref[:, pl.ds(start, wide)]
+
+    return local(kernel, arrays, [(rows, len(arrays) * wide)] * len(steps))
+
+
+def pack_grads(arrays, stay, came, chips, steps, early):
+    rows, columns = arrays[0].shape
+    wide = columns // chips
+    half = stay.shape[0]
+    count = len(arrays)
+
+    def kernel(*refs):
+        ins, (stay_ref, came_ref) = refs[:count], refs[count : count + 2]
+        outs, ordered = refs[count + 2 : -1], refs[-1]
+        chip, _, side = where_am_i()
+        mine, others = stay_ref[...].astype(jnp.float32), came_ref[...].astype(jnp.float32)
+        ordered[:half] = jnp.where(side == 0, mine, others)
+        ordered[half:] = jnp.where(side == 0, others, mine)
+        for out, step in zip(outs, tuple(steps) + tuple(early)):
+            start = pl.multiple_of((chip ^ step) * wide, HD)
+            taken = ins if step in steps else ()
+            for which, ref in enumerate(taken):
+                out[:, which * wide : (which + 1) * wide] = ref[:, pl.ds(start, wide)]
+            low = len(taken) * wide
+            out[:, low : low + wide] = ordered[:, pl.ds(start, wide)].astype(jnp.bfloat16)
+
+    return local(
+        kernel,
+        [*arrays, stay, came],
+        [(rows, (count + 1) * wide)] * len(steps) + [(rows, wide)] * len(early),
+        [pltpu.VMEM((rows, columns), jnp.float32)],
+    )
+
+
+def attend(own, other, rows):
+    chips = len(own)
+    total = 2 * chips * rows
+    scaling = 1.0 / math.sqrt(HD)
+    operands = [block for part in (own, other) for blocks in part for block in blocks]
+    inputs = len(operands)
+
+    def kernel(*refs):
+        taken = iter(refs)
+        own_refs, other_refs = (
+            [[next(taken) for _ in blocks] for blocks in part] for part in (own, other)
+        )
+        outs = refs[inputs : inputs + chips]
+        gathered, query_sum, key_sum, value_sum = refs[inputs + chips :]
+        chip, core, _ = where_am_i()
+
+        def piece(blocks, which, head):
+            at = which * 3 + head
+            if len(blocks) == 2 and which == 3:
+                blocks, at = blocks[1:], head
+            return blocks[0][:, pl.ds(pl.multiple_of(at * HD, HD), HD)].astype(jnp.float32)
+
+        def spots(step):
+            start = (chip ^ step) * (2 * rows)
+            return (
+                pl.ds(pl.multiple_of(start + core * rows, 8), rows),
+                pl.ds(pl.multiple_of(start + (1 - core) * rows, 8), rows),
+            )
+
+        for index in range(2):
+            head = core + index
+            for which in range(4):
+                for step in range(chips):
+                    mine, others = spots(step)
+                    gathered[which, mine, :] = piece(own_refs[step], which, head)
+                    gathered[which, others, :] = piece(other_refs[step], which, head)
+            query, keys, values, grads = (
+                gathered[which].astype(jnp.bfloat16) for which in range(4)
+            )
+            for low in range(0, total, TILE):
+                high = min(low + TILE, total)
+                q, g = query[low:high], grads[low:high]
+                k, v = keys[:high], values[:high]
+                last = (((1,), (1,)), ((), ()))
+                first = (((0,), (0,)), ((), ()))
+                scores = scaling * lax.dot_general(q, k, last, preferred_element_type=jnp.float32)
+                row = lax.broadcasted_iota(jnp.int32, scores.shape, 0) + low
+                col = lax.broadcasted_iota(jnp.int32, scores.shape, 1)
+                scores = jnp.where(col <= row, scores, lowest)
+                expo = jnp.exp(scores - jnp.max(scores, axis=1, keepdims=True))
+                products = lax.dot_general(g, v, last, preferred_element_type=jnp.float32)
+                scale = 1.0 / jnp.sum(expo, axis=1, keepdims=True)
+                delta = jnp.sum(expo * products, axis=1, keepdims=True) * scale
+                weights = expo * scale
+                score_grad = (weights * (products - delta)).astype(jnp.bfloat16)
+                half = weights.astype(jnp.bfloat16)
+                query_sum[low:high] = lax.dot_general(
+                    score_grad, k, (((1,), (0,)), ((), ())), preferred_element_type=jnp.float32
+                )
+                key_part = lax.dot_general(score_grad, q, first, preferred_element_type=jnp.float32)
+                value_part = lax.dot_general(half, g, first, preferred_element_type=jnp.float32)
+                if low:
+                    key_sum[:low] += key_part[:low]
+                    value_sum[:low] += value_part[:low]
+                key_sum[low:high] = key_part[low:]
+                value_sum[low:high] = value_part[low:]
+            for which, (store, factor) in enumerate(
+                ((query_sum, scaling), (key_sum, scaling), (value_sum, 1.0))
+            ):
+                lanes = slice(which * HD, (which + 1) * HD)
+                for step in range(chips):
+                    mine, others = spots(step)
+
+                    def rounded(spot):
+                        return (store[spot] * factor).astype(jnp.bfloat16)
+
+                    outs[step][pl.ds(jnp.where(head == 1, 1, 0), 1), :, lanes] = rounded(mine)[None]
+
+                    @pl.when(head != 1)
+                    def _():
+                        outs[step][2, :, lanes] = rounded(others)
+
+    big = pltpu.VMEM((total, HD), jnp.float32)
+    return local(
+        kernel,
+        operands,
+        [(3, rows, 3 * HD)] * chips,
+        [pltpu.VMEM((4, total, HD), jnp.float32), big, big, big],
+        10 * total * total * HD,
+    )
+
+
+def unpack(own, other, rows, columns):
+    chips = len(own)
+    wide = columns // chips
+
+    def kernel(*refs):
+        own_refs, other_refs, outs = refs[:chips], refs[chips : 2 * chips], refs[2 * chips :]
+        chip, core, _ = where_am_i()
+        for step in range(chips):
+            start = (chip ^ step) * wide
+            for which, out in enumerate(outs):
+                lanes = slice(which * HD, (which + 1) * HD)
+
+                def put(head, block):
+                    out[:, pl.ds(pl.multiple_of(start + head * HD, HD), HD)] = block
+
+                put(2 * core, own_refs[step][0, :, lanes])
+                put(1, own_refs[step][1, :, lanes])
+                put(2 - 2 * core, other_refs[step][2, :, lanes])
+
+    return local(kernel, [*own, *other], [(rows, columns)] * 3, final=True)
+
+
+def by_heads(query_rows, key_rows, value_rows, mid_grad, link_weight):
+    rows, columns = query_rows.shape
+    size = lax.axis_size("wide")
+    chips = size // 2
+
+    def cross(block, step):
+        return held(lax.ppermute(block, "wide", [(i, i ^ step) for i in range(size)]))
+
+    early, late = in_order(chips)
+    arrays = [held(query_rows), held(key_rows), held(value_rows)]
+    own = {}
+    ahead = pack(arrays, chips, early) if early else []
+    for step, block in zip(early, ahead):
+        own[step] = [cross(block, 2 * step)]
+    stay, leave = project(held(mid_grad), held(link_weight), 2)
+    came = held(lax.ppermute(leave, "narrow", [(0, 1), (1, 0)]))
+    rest = pack_grads(arrays, stay, came, chips, [0] + late, early)
+    own[0] = [rest[0]]
+    for step, block in zip(late, rest[1:]):
+        own[step] = [cross(block, 2 * step)]
+    for step, block in zip(early, rest[1 + len(late) :]):
+        own[step].append(cross(block, 2 * step))
+    own = [own[step] for step in range(chips)]
+    other = [[cross(block, 1) for block in blocks] for blocks in own]
+    done = attend(own, other, rows)
+    own = [done[0]] + [cross(done[step], 2 * step) for step in range(1, chips)]
+    other = [cross(block, 1) for block in own]
+    return tuple(unpack(own, other, rows, columns))
+
+
 def on_device(query_rows, key_rows, value_rows, mid_grad, link_weight):
+    size = lax.axis_size("wide")
+    rows, columns = query_rows.shape
+    chips = size // 2
+    fits = (
+        size > 1
+        and size & (size - 1) == 0
+        and lax.axis_size("narrow") == 2
+        and columns == chips * 3 * HD
+        and (size * rows) % TILE == 0
+        and rows % 8 == 0
+    )
+    plan = by_heads if fits else by_rows
+    return plan(query_rows, key_rows, value_rows, mid_grad, link_weight)
+
+
+def by_rows(query_rows, key_rows, value_rows, mid_grad, link_weight):
     groups = lax.axis_size("narrow")
     patches = query_rows.shape[0]
     columns = query_rows.shape[1]
@@ -59,7 +333,7 @@
     products = jnp.einsum(
         "qhd,khd->hqk", incoming_heads, value_split, preferred_element_type=jnp.float32
     )
-    old_max, old_total, old_tilt = fold_start[:3]
+    old_max, _, _ = fold_start[:3]
     new_max = jnp.maximum(old_max, jnp.max(scores, axis=2))
     expo = jnp.where(allowed, jnp.exp(scores - new_max[:, :, None]), 0.0)
     stats = (new_max, jnp.sum(expo, axis=2), jnp.sum(expo * products, axis=2))

time: 241 us -> 75 us (0.31)
  waiting for transfers between devices: 114 us -> 27.1 us
  blocking collectives: 51.5 us -> 0 us
  starting transfers between devices: 0.15 us -> 34.8 us
  local copies, waits for them, and re-layouts: 36.1 us -> 2.98 us
  matrix products: 25 us -> 0 us
  between operations: 13.9 us -> 0.71 us
  Pallas kernels: 0 us -> 8.01 us
    all_gather x4 -> x0, waiting for transfers between devices: 112 us -> none  [the longest x1 43.6 us: on_device(): lax.all_gather(value_rows, 'wide', axis=0, tiled=True)]
    all_gather x2 -> x0, blocking collectives: 38.1 us -> none  [the longest x1 19.6 us: on_device(): lax.all_gather(log_total, 'wide', axis=1, tiled=True)]
    ppermute x0 -> x35, starting transfers between devices: none -> 34.8 us  [the longest x34 31.8 us: cross(): lax.ppermute(block, 'wide', [(i, i ^ step) for i in range(size)])]
    ppermute x0 -> x35, waiting for transfers between devices: none -> 27.1 us  [the longest x34 27.1 us: cross(): lax.ppermute(block, 'wide', [(i, i ^ step) for i in range(size)])]
    all_gather x6 -> x0, local copies, waits for them, and re-layouts: 25.4 us -> none  [the longest x1 6.45 us: on_device(): query_piece = lax.all_gather(query_rows, 'wide', axis=0, tiled=True)]
    dot_general x7 -> x0, matrix products: 25 us -> none  [the longest x1 7.27 us: on_device(): jnp.einsum('hqk,qhd->khd', score_grad, query_split, preferred_element_typ...]
    all_to_all x1 -> x0, blocking collectives: 13.4 us -> none  [on_device(): lax.all_to_all(grouped, 'narrow', split_axis=1, concat_axis=0, tiled=True)]
    pallas_call x0 -> x5, Pallas kernels: none -> 8.01 us  [local(): pl.pallas_call(kernel, in_specs=[vmem] * len(ins), out_specs=[vmem] * len...]
  transfers between devices with their start and end apart: 4 -> 35, of which waited for: 3 -> 16; matrix products, arithmetic and copies ran while one was open for 16% -> 0% of each run, Pallas kernels for 0% -> 0%
where the time goes in v1:
time: 75 us; the launch traced here: 73.7 us
  starting transfers between devices  34.8 us (46%)
  waiting for transfers between devices  27.1 us (36%)
  Pallas kernels  8.01 us (11%)
  local copies, waits for them, and re-layouts  2.98 us (4%)
    ppermute x34, starting transfers between devices, cross(): lax.ppermute(block, 'wide', [(i, i ^ step) for i in range(size)])  31.8 us
    ppermute x34, waiting for transfers between devices, cross(): lax.ppermute(block, 'wide', [(i, i ^ step) for i in range(size)])  27.1 us
    pallas_call x5, Pallas kernels, local(): pl.pallas_call(kernel, in_specs=[vmem] * len(ins), out_specs=[vmem] * len...  8.01 us
    ppermute x1, starting transfers between devices, by_heads(): came = held(lax.ppermute(leave, 'narrow', [(0, 1), (1, 0)]))  3.06 us
    unnamed x10, local copies, waits for them, and re-layouts  2.98 us
  transfers between devices with their start and end apart: 35, of which 16 were waited for; matrix products, arithmetic and copies ran while one was open for 0% of the time, Pallas kernels for 0%

profile of v1, /device:TPU:0, one launch (start us, length us, event | category | flops | bytes accessed | tf_op | source)
XLA Modules:
  0.0 73.7 jit_solution(1508078944428765296)
XLA Ops:
  0.6 1.9 %copy-done = bf16[768,2048]{1,0:T(8,128)(2,1)S(1)} copy-done((bf16[768,2048]{1,0:T(8,128)(2,1)S(1)}, bf16[768,2048]{1,0:T(8,128)(2,1)}, u32[]{:S(2)}) %copy-start) | copy-done | bytes 3145752
  2.5 1.1 %copy-done.4 = bf16[160,2048]{1,0:T(8,128)(2,1)S(1)} copy-done((bf16[160,2048]{1,0:T(8,128)(2,1)S(1)}, bf16[160,2048]{1,0:T(8,128)(2,1)}, u32[]{:S(2)}) %copy-start.4) | copy-done | bytes 655384
  3.6 1.3 %shard_map.76 = (bf16[20,3072]{1,0:T(8,128)(2,1)S(1)}, bf16[20,3072]{1,0:T(8,128)(2,1)S(1)}) custom-call(bf16[160,2048]{1,0:T(8,128)(2,1)S(1)} %copy-done.4, bf16[768,2048]{1,0:T(8,128)(2,1)S(1)} %copy-done), custom_call_target="tpu_custom_call" | custom-call | flops 503316480 | bytes 4046848 | tf_op jit(solution)/shard_map/pallas_call | solution.py:33
  4.9 3.1 %collective-permute-start = (bf16[20,3072]{1,0:T(8,128)(2,1)S(1)}, bf16[20,3072]{1,0:T(8,128)(2,1)S(1)}, u32[]{:S(2)}, u32[]{:S(2)}) collective-permute-start(bf16[20,3072]{1,0:T(8,128)(2,1)S(1)} %get-tuple-element.24), channel_id=1, source_target_pairs={{0,1},{1,0},{2,3},{3,2},{4,5},{5,4},{6,7},{7,6},{8,9},{9,8},{10,11... | collective-permute-start | bytes 368648 | tf_op jit(solution)/shard_map/ppermute | solution.py:258
  8.0 2.7 %collective-permute-start.4 = (bf16[40,1152]{1,0:T(8,128)(2,1)S(1)}, bf16[40,1152]{1,0:T(8,128)(2,1)S(1)}, u32[]{:S(2)}, u32[]{:S(2)}) collective-permute-start(bf16[40,1152]{1,0:T(8,128)(2,1)S(1)} %get-tuple-element.29), channel_id=1, source_target_pairs={{0,16},{2,18},{4,20},{6,22},{8,24},{10,26},{12,28},{14,30},{16,0},... | collective-permute-start | bytes 276488 | tf_op jit(solution)/shard_map/ppermute | solution.py:249
  10.7 1.3 %collective-permute-start.6 = (bf16[40,1152]{1,0:T(8,128)(2,1)S(1)}, bf16[40,1152]{1,0:T(8,128)(2,1)S(1)}, u32[]{:S(2)}, u32[]{:S(2)}) collective-permute-start(bf16[40,1152]{1,0:T(8,128)(2,1)S(1)} %get-tuple-element.31), channel_id=1, source_target_pairs={{0,20},{2,22},{4,16},{6,18},{8,28},{10,30},{12,24},{14,26},{16,4},... | collective-permute-start | bytes 276488 | tf_op jit(solution)/shard_map/ppermute | solution.py:249
  12.1 1.7 %collective-permute-start.1 = (bf16[40,1536]{1,0:T(8,128)(2,1)S(1)}, bf16[40,1536]{1,0:T(8,128)(2,1)S(1)}, u32[]{:S(2)}, u32[]{:S(2)}) collective-permute-start(bf16[40,1536]{1,0:T(8,128)(2,1)S(1)} %get-tuple-element.26), channel_id=1, source_target_pairs={{0,4},{2,6},{4,0},{6,2},{8,12},{10,14},{12,8},{14,10},{16,20},{18,... | collective-permute-start | bytes 368648 | tf_op jit(solution)/shard_map/ppermute | solution.py:249
  13.7 2.9 %collective-permute-done.4.refs_4_ = bf16[40,1152]{1,0:T(8,128)(2,1)S(1)} collective-permute-done((bf16[40,1152]{1,0:T(8,128)(2,1)S(1)}, bf16[40,1152]{1,0:T(8,128)(2,1)S(1)}, u32[]{:S(2)}, u32[]{:S(2)}) %collective-permute-start.4) | collective-permute-done | bytes 92192 | tf_op jit(solution)/shard_map/ppermute | solution.py:249
  16.6 3.3 %collective-permute-done.6.refs_6_ = bf16[40,1152]{1,0:T(8,128)(2,1)S(1)} collective-permute-done((bf16[40,1152]{1,0:T(8,128)(2,1)S(1)}, bf16[40,1152]{1,0:T(8,128)(2,1)S(1)}, u32[]{:S(2)}, u32[]{:S(2)}) %collective-permute-start.6) | collective-permute-done | bytes 92192 | tf_op jit(solution)/shard_map/ppermute | solution.py:249
  20.0 2.9 %collective-permute-start.7 = (bf16[40,384]{1,0:T(8,128)(2,1)S(1)}, bf16[40,384]{1,0:T(8,128)(2,1)S(1)}, u32[]{:S(2)}, u32[]{:S(2)}) collective-permute-start(bf16[40,384]{1,0:T(8,128)(2,1)S(1)} %get-tuple-element.32), channel_id=1, source_target_pairs={{0,20},{2,22},{4,16},{6,18},{8,28},{10,30},{12,24},{14,26},{16,4},... | collective-permute-start | bytes 92168 | tf_op jit(solution)/shard_map/ppermute | solution.py:249
  22.9 2.7 %collective-permute-done.5.refs_5_ = bf16[40,384]{1,0:T(8,128)(2,1)S(1)} collective-permute-done((bf16[40,384]{1,0:T(8,128)(2,1)S(1)}, bf16[40,384]{1,0:T(8,128)(2,1)S(1)}, u32[]{:S(2)}, u32[]{:S(2)}) %collective-permute-start.5) | collective-permute-done | bytes 30752 | tf_op jit(solution)/shard_map/ppermute | solution.py:249
  25.6 0.6 collective-permute-done.7.refs_7_
  26.3 3.5 %collective-permute-start.2 = (bf16[40,1536]{1,0:T(8,128)(2,1)S(1)}, bf16[40,1536]{1,0:T(8,128)(2,1)S(1)}, u32[]{:S(2)}, u32[]{:S(2)}) collective-permute-start(bf16[40,1536]{1,0:T(8,128)(2,1)S(1)} %get-tuple-element.27), channel_id=1, source_target_pairs={{0,8},{2,10},{4,12},{6,14},{8,0},{10,2},{12,4},{14,6},{16,24},{18,... | collective-permute-start | bytes 368648 | tf_op jit(solution)/shard_map/ppermute | solution.py:249
  29.9 2.5 %collective-permute-start.8 = (bf16[40,1536]{1,0:T(8,128)(2,1)S(1)}, bf16[40,1536]{1,0:T(8,128)(2,1)S(1)}, u32[]{:S(2)}, u32[]{:S(2)}) collective-permute-start(bf16[40,1536]{1,0:T(8,128)(2,1)S(1)} %get-tuple-element.33), channel_id=1, source_target_pairs={{0,24},{2,26},{4,28},{6,30},{8,16},{10,18},{12,20},{14,22},{16,8},... | collective-permute-start | bytes 368648 | tf_op jit(solution)/shard_map/ppermute | solution.py:249
  32.4 2.2 %collective-permute-start.9 = (bf16[40,1536]{1,0:T(8,128)(2,1)S(1)}, bf16[40,1536]{1,0:T(8,128)(2,1)S(1)}, u32[]{:S(2)}, u32[]{:S(2)}) collective-permute-start(bf16[40,1536]{1,0:T(8,128)(2,1)S(1)} %get-tuple-element.34), channel_id=1, source_target_pairs={{0,28},{2,30},{4,24},{6,26},{8,20},{10,22},{12,16},{14,18},{16,12}... | collective-permute-start | bytes 368648 | tf_op jit(solution)/shard_map/ppermute | solution.py:249
  35.0 1.4 %collective-permute-done.3.refs_3_ = bf16[40,1536]{1,0:T(8,128)(2,1)S(1)} collective-permute-done((bf16[40,1536]{1,0:T(8,128)(2,1)S(1)}, bf16[40,1536]{1,0:T(8,128)(2,1)S(1)}, u32[]{:S(2)}, u32[]{:S(2)}) %collective-permute-start.3) | collective-permute-done | bytes 122912 | tf_op jit(solution)/shard_map/ppermute | solution.py:249
  36.4 3.2 %collective-permute-done.8.refs_8_ = bf16[40,1536]{1,0:T(8,128)(2,1)S(1)} collective-permute-done((bf16[40,1536]{1,0:T(8,128)(2,1)S(1)}, bf16[40,1536]{1,0:T(8,128)(2,1)S(1)}, u32[]{:S(2)}, u32[]{:S(2)}) %collective-permute-start.8) | collective-permute-done | bytes 122912 | tf_op jit(solution)/shard_map/ppermute | solution.py:249
  39.6 2.7 %collective-permute-done.9.refs_9_ = bf16[40,1536]{1,0:T(8,128)(2,1)S(1)} collective-permute-done((bf16[40,1536]{1,0:T(8,128)(2,1)S(1)}, bf16[40,1536]{1,0:T(8,128)(2,1)S(1)}, u32[]{:S(2)}, u32[]{:S(2)}) %collective-permute-start.9) | collective-permute-done | bytes 122912 | tf_op jit(solution)/shard_map/ppermute | solution.py:249
  42.3 0.5 collective-permute-start.19
  42.8 0.8 %collective-permute-done.18.refs_18_ = bf16[40,1536]{1,0:T(8,128)(2,1)S(1)} collective-permute-done((bf16[40,1536]{1,0:T(8,128)(2,1)S(1)}, bf16[40,1536]{1,0:T(8,128)(2,1)S(1)}, u32[]{:S(2)}, u32[]{:S(2)}) %collective-permute-start.18) | collective-permute-done | bytes 122912 | tf_op jit(solution)/shard_map/ppermute | solution.py:249
  43.8 5.5 %shard_map.79 = (bf16[3,40,384]{2,1,0:T(8,128)(2,1)S(1)}, bf16[3,40,384]{2,1,0:T(8,128)(2,1)S(1)}, bf16[3,40,384]{2,1,0:T(8,128)(2,1)S(1)}, bf16[3,40,384]{2,1,0...) custom-call(bf16[40,1536]{1,0:T(8,128)(2,1)S(1)} %get-tuple-element., ...), custom_call_target="tpu_custom_call" | custom-call | flops 524288000 | bytes 2703360 | tf_op jit(solution)/shard_map/pallas_call | solution.py:33
  49.3 1.0 %collective-permute-start.20 = (bf16[3,40,384]{2,1,0:T(8,128)(2,1)S(1)}, bf16[3,40,384]{2,1,0:T(8,128)(2,1)S(1)}, u32[]{:S(2)}, u32[]{:S(2)}) collective-permute-start(bf16[3,40,384]{2,1,0:T(8,128)(2,1)S(1)} %get-tuple-element.36), channel_id=1, source_target_pairs={{0,4},{2,6},{4,0},{6,2},{8,12},{10,14},{12,8},{14,10},{16,20},{18,... | collective-permute-start | bytes 276488 | tf_op jit(solution)/shard_map/ppermute | solution.py:249
  50.3 3.1 %collective-permute-start.21 = (bf16[3,40,384]{2,1,0:T(8,128)(2,1)S(1)}, bf16[3,40,384]{2,1,0:T(8,128)(2,1)S(1)}, u32[]{:S(2)}, u32[]{:S(2)}) collective-permute-start(bf16[3,40,384]{2,1,0:T(8,128)(2,1)S(1)} %get-tuple-element.37), channel_id=1, source_target_pairs={{0,8},{2,10},{4,12},{6,14},{8,0},{10,2},{12,4},{14,6},{16,24},{18,... | collective-permute-start | bytes 276488 | tf_op jit(solution)/shard_map/ppermute | solution.py:249
  53.4 0.8 %collective-permute-start.22 = (bf16[3,40,384]{2,1,0:T(8,128)(2,1)S(1)}, bf16[3,40,384]{2,1,0:T(8,128)(2,1)S(1)}, u32[]{:S(2)}, u32[]{:S(2)}) collective-permute-start(bf16[3,40,384]{2,1,0:T(8,128)(2,1)S(1)} %get-tuple-element.38), channel_id=1, source_target_pairs={{0,12},{2,14},{4,8},{6,10},{8,4},{10,6},{12,0},{14,2},{16,28},{18,... | collective-permute-start | bytes 276488 | tf_op jit(solution)/shard_map/ppermute | solution.py:249
  54.3 1.7 %collective-permute-start.23 = (bf16[3,40,384]{2,1,0:T(8,128)(2,1)S(1)}, bf16[3,40,384]{2,1,0:T(8,128)(2,1)S(1)}, u32[]{:S(2)}, u32[]{:S(2)}) collective-permute-start(bf16[3,40,384]{2,1,0:T(8,128)(2,1)S(1)} %get-tuple-element.39), channel_id=1, source_target_pairs={{0,16},{2,18},{4,20},{6,22},{8,24},{10,26},{12,28},{14,30},{16,0},... | collective-permute-start | bytes 276488 | tf_op jit(solution)/shard_map/ppermute | solution.py:249
  56.0 1.2 %collective-permute-start.24 = (bf16[3,40,384]{2,1,0:T(8,128)(2,1)S(1)}, bf16[3,40,384]{2,1,0:T(8,128)(2,1)S(1)}, u32[]{:S(2)}, u32[]{:S(2)}) collective-permute-start(bf16[3,40,384]{2,1,0:T(8,128)(2,1)S(1)} %get-tuple-element.40), channel_id=1, source_target_pairs={{0,20},{2,22},{4,16},{6,18},{8,28},{10,30},{12,24},{14,26},{16,4},... | collective-permute-start | bytes 276488 | tf_op jit(solution)/shard_map/ppermute | solution.py:249
  57.3 2.7 %collective-permute-start.25 = (bf16[3,40,384]{2,1,0:T(8,128)(2,1)S(1)}, bf16[3,40,384]{2,1,0:T(8,128)(2,1)S(1)}, u32[]{:S(2)}, u32[]{:S(2)}) collective-permute-start(bf16[3,40,384]{2,1,0:T(8,128)(2,1)S(1)} %get-tuple-element.41), channel_id=1, source_target_pairs={{0,24},{2,26},{4,28},{6,30},{8,16},{10,18},{12,20},{14,22},{16,8},... | collective-permute-start | bytes 276488 | tf_op jit(solution)/shard_map/ppermute | solution.py:249
  59.9 2.0 %collective-permute-start.26 = (bf16[3,40,384]{2,1,0:T(8,128)(2,1)S(1)}, bf16[3,40,384]{2,1,0:T(8,128)(2,1)S(1)}, u32[]{:S(2)}, u32[]{:S(2)}) collective-permute-start(bf16[3,40,384]{2,1,0:T(8,128)(2,1)S(1)} %get-tuple-element.42), channel_id=1, source_target_pairs={{0,28},{2,30},{4,24},{6,26},{8,20},{10,22},{12,16},{14,18},{16,12}... | collective-permute-start | bytes 276488 | tf_op jit(solution)/shard_map/ppermute | solution.py:249
  61.9 6.5 %collective-permute-done.23.refs_4_ = bf16[3,40,384]{2,1,0:T(8,128)(2,1)S(1)} collective-permute-done((bf16[3,40,384]{2,1,0:T(8,128)(2,1)S(1)}, bf16[3,40,384]{2,1,0:T(8,128)(2,1)S(1)}, u32[]{:S(2)}, u32[]{:S(2)}) %collective-permute-start.23) | collective-permute-done | bytes 92192 | tf_op jit(solution)/shard_map/ppermute | solution.py:249
  68.5 1.6 %collective-permute-done.24.refs_5_ = bf16[3,40,384]{2,1,0:T(8,128)(2,1)S(1)} collective-permute-done((bf16[3,40,384]{2,1,0:T(8,128)(2,1)S(1)}, bf16[3,40,384]{2,1,0:T(8,128)(2,1)S(1)}, u32[]{:S(2)}, u32[]{:S(2)}) %collective-permute-start.24) | collective-permute-done | bytes 92192 | tf_op jit(solution)/shard_map/ppermute | solution.py:249
  70.1 0.5 collective-permute-start.30
  72.6 1.0 %shard_map.80 = (bf16[40,3072]{1,0:T(8,128)(2,1)}, bf16[40,3072]{1,0:T(8,128)(2,1)}, bf16[40,3072]{1,0:T(8,128)(2,1)}) custom-call(bf16[3,40,384]{2,1,0:T(8,128)(2,1)S(1)} %get-tuple-element.35.refs_0_, bf16[3,40,384]{2,1,0:T(8,128)(2,1)S(1)} %collective-permute-done.20.refs_1_, bf16[3,40,384]{2,1,0:T(8,128)(2,1)S(1)} %collective-permute-done.21.refs_2_, ...), custom_call_target="tpu_custom_call" | custom-call | bytes 2211840 | tf_op jit(solution)/shard_map/pallas_call | solution.py:33
  (53 shorter events, 3.2 us)
Async XLA Ops:
  4.9 7.0 %collective-permute-start = (bf16[20,3072]{1,0:T(8,128)(2,1)S(1)}, bf16[20,3072]{1,0:T(8,128)(2,1)S(1)}, u32[]{:S(2)}, u32[]{:S(2)}) collective-permute-start(bf16[20,3072]{1,0:T(8,128)(2,1)S(1)} %get-tuple-element.24), channel_id=1, source_target_pairs={{0,1},{1,0},{2,3},{3,2},{4,5},{5,4},{6,7},{7,6},{8,9},{9,8},{10,11... | collective-permute-start | bytes 368648 | tf_op jit(solution)/shard_map/ppermute | solution.py:258
  8.0 8.6 %collective-permute-start.4 = (bf16[40,1152]{1,0:T(8,128)(2,1)S(1)}, bf16[40,1152]{1,0:T(8,128)(2,1)S(1)}, u32[]{:S(2)}, u32[]{:S(2)}) collective-permute-start(bf16[40,1152]{1,0:T(8,128)(2,1)S(1)} %get-tuple-element.29), channel_id=1, source_target_pairs={{0,16},{2,18},{4,20},{6,22},{8,24},{10,26},{12,28},{14,30},{16,0},... | collective-permute-start | bytes 276488 | tf_op jit(solution)/shard_map/ppermute | solution.py:249
  10.7 9.3 %collective-permute-start.6 = (bf16[40,1152]{1,0:T(8,128)(2,1)S(1)}, bf16[40,1152]{1,0:T(8,128)(2,1)S(1)}, u32[]{:S(2)}, u32[]{:S(2)}) collective-permute-start(bf16[40,1152]{1,0:T(8,128)(2,1)S(1)} %get-tuple-element.31), channel_id=1, source_target_pairs={{0,20},{2,22},{4,16},{6,18},{8,28},{10,30},{12,24},{14,26},{16,4},... | collective-permute-start | bytes 276488 | tf_op jit(solution)/shard_map/ppermute | solution.py:249
  12.1 22.4 %collective-permute-start.1 = (bf16[40,1536]{1,0:T(8,128)(2,1)S(1)}, bf16[40,1536]{1,0:T(8,128)(2,1)S(1)}, u32[]{:S(2)}, u32[]{:S(2)}) collective-permute-start(bf16[40,1536]{1,0:T(8,128)(2,1)S(1)} %get-tuple-element.26), channel_id=1, source_target_pairs={{0,4},{2,6},{4,0},{6,2},{8,12},{10,14},{12,8},{14,10},{16,20},{18,... | collective-permute-start | bytes 368648 | tf_op jit(solution)/shard_map/ppermute | solution.py:249
  16.6 9.6 %collective-permute-start.14 = (bf16[40,1152]{1,0:T(8,128)(2,1)S(1)}, bf16[40,1152]{1,0:T(8,128)(2,1)S(1)}, u32[]{:S(2)}, u32[]{:S(2)}) collective-permute-start(bf16[40,1152]{1,0:T(8,128)(2,1)S(1)} %collective-permute-done.4.refs_4_), channel_id=1, source_target_pairs={{0,2},{2,0},{4,6},{6,4},{8,10},{10,8},{12,14},{14,12},{16,18},{18,... | collective-permute-start | bytes 276488 | tf_op jit(solution)/shard_map/ppermute | solution.py:249
  20.0 9.7 %collective-permute-start.16 = (bf16[40,1152]{1,0:T(8,128)(2,1)S(1)}, bf16[40,1152]{1,0:T(8,128)(2,1)S(1)}, u32[]{:S(2)}, u32[]{:S(2)}) collective-permute-start(bf16[40,1152]{1,0:T(8,128)(2,1)S(1)} %collective-permute-done.6.refs_6_), channel_id=1, source_target_pairs={{0,2},{2,0},{4,6},{6,4},{8,10},{10,8},{12,14},{14,12},{16,18},{18,... | collective-permute-start | bytes 276488 | tf_op jit(solution)/shard_map/ppermute | solution.py:249
  20.0 5.6 %collective-permute-start.5 = (bf16[40,384]{1,0:T(8,128)(2,1)S(1)}, bf16[40,384]{1,0:T(8,128)(2,1)S(1)}, u32[]{:S(2)}, u32[]{:S(2)}) collective-permute-start(bf16[40,384]{1,0:T(8,128)(2,1)S(1)} %get-tuple-element.30), channel_id=1, source_target_pairs={{0,16},{2,18},{4,20},{6,22},{8,24},{10,26},{12,28},{14,30},{16,0},... | collective-permute-start | bytes 92168 | tf_op jit(solution)/shard_map/ppermute | solution.py:249
  20.0 6.2 %collective-permute-start.7 = (bf16[40,384]{1,0:T(8,128)(2,1)S(1)}, bf16[40,384]{1,0:T(8,128)(2,1)S(1)}, u32[]{:S(2)}, u32[]{:S(2)}) collective-permute-start(bf16[40,384]{1,0:T(8,128)(2,1)S(1)} %get-tuple-element.32), channel_id=1, source_target_pairs={{0,20},{2,22},{4,16},{6,18},{8,28},{10,30},{12,24},{14,26},{16,4},... | collective-permute-start | bytes 92168 | tf_op jit(solution)/shard_map/ppermute | solution.py:249
  25.6 4.2 %collective-permute-start.15 = (bf16[40,384]{1,0:T(8,128)(2,1)S(1)}, bf16[40,384]{1,0:T(8,128)(2,1)S(1)}, u32[]{:S(2)}, u32[]{:S(2)}) collective-permute-start(bf16[40,384]{1,0:T(8,128)(2,1)S(1)} %collective-permute-done.5.refs_5_), channel_id=1, source_target_pairs={{0,2},{2,0},{4,6},{6,4},{8,10},{10,8},{12,14},{14,12},{16,18},{18,... | collective-permute-start | bytes 92168 | tf_op jit(solution)/shard_map/ppermute | solution.py:249
  26.2 6.2 %collective-permute-start.17 = (bf16[40,384]{1,0:T(8,128)(2,1)S(1)}, bf16[40,384]{1,0:T(8,128)(2,1)S(1)}, u32[]{:S(2)}, u32[]{:S(2)}) collective-permute-start(bf16[40,384]{1,0:T(8,128)(2,1)S(1)} %collective-permute-done.7.refs_7_), channel_id=1, source_target_pairs={{0,2},{2,0},{4,6},{6,4},{8,10},{10,8},{12,14},{14,12},{16,18},{18,... | collective-permute-start | bytes 92168 | tf_op jit(solution)/shard_map/ppermute | solution.py:249
  26.3 8.3 %collective-permute-start.2 = (bf16[40,1536]{1,0:T(8,128)(2,1)S(1)}, bf16[40,1536]{1,0:T(8,128)(2,1)S(1)}, u32[]{:S(2)}, u32[]{:S(2)}) collective-permute-start(bf16[40,1536]{1,0:T(8,128)(2,1)S(1)} %get-tuple-element.27), channel_id=1, source_target_pairs={{0,8},{2,10},{4,12},{6,14},{8,0},{10,2},{12,4},{14,6},{16,24},{18,... | collective-permute-start | bytes 368648 | tf_op jit(solution)/shard_map/ppermute | solution.py:249
  29.7 6.7 %collective-permute-start.3 = (bf16[40,1536]{1,0:T(8,128)(2,1)S(1)}, bf16[40,1536]{1,0:T(8,128)(2,1)S(1)}, u32[]{:S(2)}, u32[]{:S(2)}) collective-permute-start(bf16[40,1536]{1,0:T(8,128)(2,1)S(1)} %get-tuple-element.28), channel_id=1, source_target_pairs={{0,12},{2,14},{4,8},{6,10},{8,4},{10,6},{12,0},{14,2},{16,28},{18,... | collective-permute-start | bytes 368648 | tf_op jit(solution)/shard_map/ppermute | solution.py:249
  29.9 9.7 %collective-permute-start.8 = (bf16[40,1536]{1,0:T(8,128)(2,1)S(1)}, bf16[40,1536]{1,0:T(8,128)(2,1)S(1)}, u32[]{:S(2)}, u32[]{:S(2)}) collective-permute-start(bf16[40,1536]{1,0:T(8,128)(2,1)S(1)} %get-tuple-element.33), channel_id=1, source_target_pairs={{0,24},{2,26},{4,28},{6,30},{8,16},{10,18},{12,20},{14,22},{16,8},... | collective-permute-start | bytes 368648 | tf_op jit(solution)/shard_map/ppermute | solution.py:249
  32.4 10.0 %collective-permute-start.9 = (bf16[40,1536]{1,0:T(8,128)(2,1)S(1)}, bf16[40,1536]{1,0:T(8,128)(2,1)S(1)}, u32[]{:S(2)}, u32[]{:S(2)}) collective-permute-start(bf16[40,1536]{1,0:T(8,128)(2,1)S(1)} %get-tuple-element.34), channel_id=1, source_target_pairs={{0,28},{2,30},{4,24},{6,26},{8,20},{10,22},{12,16},{14,18},{16,12}... | collective-permute-start | bytes 368648 | tf_op jit(solution)/shard_map/ppermute | solution.py:249
  34.5 7.8 %collective-permute-start.10 = (bf16[40,1536]{1,0:T(8,128)(2,1)S(1)}, bf16[40,1536]{1,0:T(8,128)(2,1)S(1)}, u32[]{:S(2)}, u32[]{:S(2)}) collective-permute-start(bf16[40,1536]{1,0:T(8,128)(2,1)S(1)} %get-tuple-element.25.refs_0_), channel_id=1, source_target_pairs={{0,2},{2,0},{4,6},{6,4},{8,10},{10,8},{12,14},{14,12},{16,18},{18,... | collective-permute-start | bytes 368648 | tf_op jit(solution)/shard_map/ppermute | solution.py:249
  34.5 8.3 %collective-permute-start.11 = (bf16[40,1536]{1,0:T(8,128)(2,1)S(1)}, bf16[40,1536]{1,0:T(8,128)(2,1)S(1)}, u32[]{:S(2)}, u32[]{:S(2)}) collective-permute-start(bf16[40,1536]{1,0:T(8,128)(2,1)S(1)} %collective-permute-done.1.refs_1_), channel_id=1, source_target_pairs={{0,2},{2,0},{4,6},{6,4},{8,10},{10,8},{12,14},{14,12},{16,18},{18,... | collective-permute-start | bytes 368648 | tf_op jit(solution)/shard_map/ppermute | solution.py:249
  36.4 6.4 %collective-permute-start.12 = (bf16[40,1536]{1,0:T(8,128)(2,1)S(1)}, bf16[40,1536]{1,0:T(8,128)(2,1)S(1)}, u32[]{:S(2)}, u32[]{:S(2)}) collective-permute-start(bf16[40,1536]{1,0:T(8,128)(2,1)S(1)} %collective-permute-done.2.refs_2_), channel_id=1, source_target_pairs={{0,2},{2,0},{4,6},{6,4},{8,10},{10,8},{12,14},{14,12},{16,18},{18,... | collective-permute-start | bytes 368648 | tf_op jit(solution)/shard_map/ppermute | solution.py:249
  39.6 3.2 %collective-permute-start.13 = (bf16[40,1536]{1,0:T(8,128)(2,1)S(1)}, bf16[40,1536]{1,0:T(8,128)(2,1)S(1)}, u32[]{:S(2)}, u32[]{:S(2)}) collective-permute-start(bf16[40,1536]{1,0:T(8,128)(2,1)S(1)} %collective-permute-done.3.refs_3_), channel_id=1, source_target_pairs={{0,2},{2,0},{4,6},{6,4},{8,10},{10,8},{12,14},{14,12},{16,18},{18,... | collective-permute-start | bytes 368648 | tf_op jit(solution)/shard_map/ppermute | solution.py:249
  42.3 1.3 %collective-permute-start.18 = (bf16[40,1536]{1,0:T(8,128)(2,1)S(1)}, bf16[40,1536]{1,0:T(8,128)(2,1)S(1)}, u32[]{:S(2)}, u32[]{:S(2)}) collective-permute-start(bf16[40,1536]{1,0:T(8,128)(2,1)S(1)} %collective-permute-done.8.refs_8_), channel_id=1, source_target_pairs={{0,2},{2,0},{4,6},{6,4},{8,10},{10,8},{12,14},{14,12},{16,18},{18,... | collective-permute-start | bytes 368648 | tf_op jit(solution)/shard_map/ppermute | solution.py:249
  42.3 1.5 %collective-permute-start.19 = (bf16[40,1536]{1,0:T(8,128)(2,1)S(1)}, bf16[40,1536]{1,0:T(8,128)(2,1)S(1)}, u32[]{:S(2)}, u32[]{:S(2)}) collective-permute-start(bf16[40,1536]{1,0:T(8,128)(2,1)S(1)} %collective-permute-done.9.refs_9_), channel_id=1, source_target_pairs={{0,2},{2,0},{4,6},{6,4},{8,10},{10,8},{12,14},{14,12},{16,18},{18,... | collective-permute-start | bytes 368648 | tf_op jit(solution)/shard_map/ppermute | solution.py:249
  49.3 7.9 %collective-permute-start.20 = (bf16[3,40,384]{2,1,0:T(8,128)(2,1)S(1)}, bf16[3,40,384]{2,1,0:T(8,128)(2,1)S(1)}, u32[]{:S(2)}, u32[]{:S(2)}) collective-permute-start(bf16[3,40,384]{2,1,0:T(8,128)(2,1)S(1)} %get-tuple-element.36), channel_id=1, source_target_pairs={{0,4},{2,6},{4,0},{6,2},{8,12},{10,14},{12,8},{14,10},{16,20},{18,... | collective-permute-start | bytes 276488 | tf_op jit(solution)/shard_map/ppermute | solution.py:249
  50.3 9.6 %collective-permute-start.21 = (bf16[3,40,384]{2,1,0:T(8,128)(2,1)S(1)}, bf16[3,40,384]{2,1,0:T(8,128)(2,1)S(1)}, u32[]{:S(2)}, u32[]{:S(2)}) collective-permute-start(bf16[3,40,384]{2,1,0:T(8,128)(2,1)S(1)} %get-tuple-element.37), channel_id=1, source_target_pairs={{0,8},{2,10},{4,12},{6,14},{8,0},{10,2},{12,4},{14,6},{16,24},{18,... | collective-permute-start | bytes 276488 | tf_op jit(solution)/shard_map/ppermute | solution.py:249
  53.4 8.5 %collective-permute-start.22 = (bf16[3,40,384]{2,1,0:T(8,128)(2,1)S(1)}, bf16[3,40,384]{2,1,0:T(8,128)(2,1)S(1)}, u32[]{:S(2)}, u32[]{:S(2)}) collective-permute-start(bf16[3,40,384]{2,1,0:T(8,128)(2,1)S(1)} %get-tuple-element.38), channel_id=1, source_target_pairs={{0,12},{2,14},{4,8},{6,10},{8,4},{10,6},{12,0},{14,2},{16,28},{18,... | collective-permute-start | bytes 276488 | tf_op jit(solution)/shard_map/ppermute | solution.py:249
  54.3 14.2 %collective-permute-start.23 = (bf16[3,40,384]{2,1,0:T(8,128)(2,1)S(1)}, bf16[3,40,384]{2,1,0:T(8,128)(2,1)S(1)}, u32[]{:S(2)}, u32[]{:S(2)}) collective-permute-start(bf16[3,40,384]{2,1,0:T(8,128)(2,1)S(1)} %get-tuple-element.39), channel_id=1, source_target_pairs={{0,16},{2,18},{4,20},{6,22},{8,24},{10,26},{12,28},{14,30},{16,0},... | collective-permute-start | bytes 276488 | tf_op jit(solution)/shard_map/ppermute | solution.py:249
  56.0 14.0 %collective-permute-start.24 = (bf16[3,40,384]{2,1,0:T(8,128)(2,1)S(1)}, bf16[3,40,384]{2,1,0:T(8,128)(2,1)S(1)}, u32[]{:S(2)}, u32[]{:S(2)}) collective-permute-start(bf16[3,40,384]{2,1,0:T(8,128)(2,1)S(1)} %get-tuple-element.40), channel_id=1, source_target_pairs={{0,20},{2,22},{4,16},{6,18},{8,28},{10,30},{12,24},{14,26},{16,4},... | collective-permute-start | bytes 276488 | tf_op jit(solution)/shard_map/ppermute | solution.py:249
  57.3 12.8 %collective-permute-start.25 = (bf16[3,40,384]{2,1,0:T(8,128)(2,1)S(1)}, bf16[3,40,384]{2,1,0:T(8,128)(2,1)S(1)}, u32[]{:S(2)}, u32[]{:S(2)}) collective-permute-start(bf16[3,40,384]{2,1,0:T(8,128)(2,1)S(1)} %get-tuple-element.41), channel_id=1, source_target_pairs={{0,24},{2,26},{4,28},{6,30},{8,16},{10,18},{12,20},{14,22},{16,8},... | collective-permute-start | bytes 276488 | tf_op jit(solution)/shard_map/ppermute | solution.py:249
  59.9 10.6 %collective-permute-start.26 = (bf16[3,40,384]{2,1,0:T(8,128)(2,1)S(1)}, bf16[3,40,384]{2,1,0:T(8,128)(2,1)S(1)}, u32[]{:S(2)}, u32[]{:S(2)}) collective-permute-start(bf16[3,40,384]{2,1,0:T(8,128)(2,1)S(1)} %get-tuple-element.42), channel_id=1, source_target_pairs={{0,28},{2,30},{4,24},{6,26},{8,20},{10,22},{12,16},{14,18},{16,12}... | collective-permute-start | bytes 276488 | tf_op jit(solution)/shard_map/ppermute | solution.py:249
  61.9 8.7 %collective-permute-start.27 = (bf16[3,40,384]{2,1,0:T(8,128)(2,1)S(1)}, bf16[3,40,384]{2,1,0:T(8,128)(2,1)S(1)}, u32[]{:S(2)}, u32[]{:S(2)}) collective-permute-start(bf16[3,40,384]{2,1,0:T(8,128)(2,1)S(1)} %get-tuple-element.35.refs_0_), channel_id=1, source_target_pairs={{0,2},{2,0},{4,6},{6,4},{8,10},{10,8},{12,14},{14,12},{16,18},{18,... | collective-permute-start | bytes 276488 | tf_op jit(solution)/shard_map/ppermute | solution.py:249
  68.5 2.6 %collective-permute-start.28 = (bf16[3,40,384]{2,1,0:T(8,128)(2,1)S(1)}, bf16[3,40,384]{2,1,0:T(8,128)(2,1)S(1)}, u32[]{:S(2)}, u32[]{:S(2)}) collective-permute-start(bf16[3,40,384]{2,1,0:T(8,128)(2,1)S(1)} %collective-permute-done.20.refs_1_), channel_id=1, source_target_pairs={{0,2},{2,0},{4,6},{6,4},{8,10},{10,8},{12,14},{14,12},{16,18},{18,... | collective-permute-start | bytes 276488 | tf_op jit(solution)/shard_map/ppermute | solution.py:249
  70.1 1.5 %collective-permute-start.30 = (bf16[3,40,384]{2,1,0:T(8,128)(2,1)S(1)}, bf16[3,40,384]{2,1,0:T(8,128)(2,1)S(1)}, u32[]{:S(2)}, u32[]{:S(2)}) collective-permute-start(bf16[3,40,384]{2,1,0:T(8,128)(2,1)S(1)} %collective-permute-done.22.refs_3_), channel_id=1, source_target_pairs={{0,2},{2,0},{4,6},{6,4},{8,10},{10,8},{12,14},{14,12},{16,18},{18,... | collective-permute-start | bytes 276488 | tf_op jit(solution)/shard_map/ppermute | solution.py:249
  70.6 1.3 %collective-permute-start.31 = (bf16[3,40,384]{2,1,0:T(8,128)(2,1)S(1)}, bf16[3,40,384]{2,1,0:T(8,128)(2,1)S(1)}, u32[]{:S(2)}, u32[]{:S(2)}) collective-permute-start(bf16[3,40,384]{2,1,0:T(8,128)(2,1)S(1)} %collective-permute-done.23.refs_4_), channel_id=1, source_target_pairs={{0,2},{2,0},{4,6},{6,4},{8,10},{10,8},{12,14},{14,12},{16,18},{18,... | collective-permute-start | bytes 276488 | tf_op jit(solution)/shard_map/ppermute | solution.py:249
  70.6 1.4 %collective-permute-start.32 = (bf16[3,40,384]{2,1,0:T(8,128)(2,1)S(1)}, bf16[3,40,384]{2,1,0:T(8,128)(2,1)S(1)}, u32[]{:S(2)}, u32[]{:S(2)}) collective-permute-start(bf16[3,40,384]{2,1,0:T(8,128)(2,1)S(1)} %collective-permute-done.24.refs_5_), channel_id=1, source_target_pairs={{0,2},{2,0},{4,6},{6,4},{8,10},{10,8},{12,14},{14,12},{16,18},{18,... | collective-permute-start | bytes 276488 | tf_op jit(solution)/shard_map/ppermute | solution.py:249
  (8 other events, 19.9 us)

commit v2 on v1

--- a/solution.py
+++ b/solution.py
@@ -10,7 +10,7 @@
 
 HD = 128
 PATCH = 8
-TILE = 128
+TILE = 320
 ROOM = 24 << 20
 
 
@@ -23,8 +23,8 @@
     return far[:2], far[2:] + near
 
 
-def local(kernel, ins, shapes, scratch=(), flops=0, final=False):
-    vmem = pl.BlockSpec(memory_space=pltpu.VMEM)
+def local(kernel, ins, shapes, scratch=(), flops=0, final=False, afar=()):
+    vmem, anywhere = (pl.BlockSpec(memory_space=space) for space in (pltpu.VMEM, pltpu.HBM))
     outs = [
         jax.ShapeDtypeStruct(shape, jnp.bfloat16) if final else pltpu.VMEM(shape, jnp.bfloat16)
         for shape in shapes
@@ -32,13 +32,13 @@
     moved = 2 * (sum(array.size for array in ins) + sum(math.prod(shape) for shape in shapes))
     return pl.pallas_call(
         kernel,
-        in_specs=[vmem] * len(ins),
+        in_specs=[anywhere if i in afar else vmem for i in range(len(ins))],
         out_specs=[vmem] * len(shapes),
         out_shape=outs,
         scratch_shapes=list(scratch),
         compiler_params=pltpu.CompilerParams(vmem_limit_bytes=ROOM),
         cost_estimate=pl.CostEstimate(flops=flops, bytes_accessed=moved, transcendentals=0),
-    )(*ins)
+    )(*(pltpu.with_memory_space_constraint(x, pltpu.HBM) if i in afar else x for i, x in enumerate(ins)))
 
 
 def held(array):
@@ -82,19 +82,36 @@
     )
 
 
-def pack(arrays, chips, steps):
+def pack(arrays, others, chips, steps):
     rows, columns = arrays[0].shape
     wide = columns // chips
+    whole = [*arrays, *others]
+    count = len(whole)
 
     def kernel(*refs):
-        ins, outs = refs[: len(arrays)], refs[len(arrays) :]
+        ins, kept, outs, arrived = refs[:count], refs[count : 2 * count], refs[2 * count : -1], refs[-1]
+        copies = [
+            pltpu.make_async_copy(ref, keep, arrived.at[which])
+            for which, (ref, keep) in enumerate(zip(ins, kept))
+        ]
+        for copy in copies:
+            copy.start()
+        for copy in copies:
+            copy.wait()
         chip = where_am_i()[0]
         for out, step in zip(outs, steps):
             start = pl.multiple_of((chip ^ step) * wide, HD)
-            for which, ref in enumerate(ins):
-                out[:, which * wide : (which + 1) * wide] = ref[:, pl.ds(start, wide)]
-
-    return local(kernel, arrays, [(rows, len(arrays) * wide)] * len(steps))
+            for which in range(len(arrays)):
+                out[:, which * wide : (which + 1) * wide] = kept[which][:, pl.ds(start, wide)]
+
+    return local(
+        kernel,
+        whole,
+        [array.shape for array in whole] + [(rows, len(arrays) * wide)] * len(steps),
+        [pltpu.SemaphoreType.DMA((count,))],
+        flops=5 * 10**9,
+        afar=range(count),
+    )
 
 
 def pack_grads(arrays, stay, came, chips, steps, early):
@@ -249,12 +266,12 @@
         return held(lax.ppermute(block, "wide", [(i, i ^ step) for i in range(size)]))
 
     early, late = in_order(chips)
-    arrays = [held(query_rows), held(key_rows), held(value_rows)]
     own = {}
-    ahead = pack(arrays, chips, early) if early else []
+    ahead = pack([query_rows, key_rows, value_rows], [], chips, early)
+    arrays, ahead = ahead[:3], ahead[3:]
     for step, block in zip(early, ahead):
         own[step] = [cross(block, 2 * step)]
-    stay, leave = project(held(mid_grad), held(link_weight), 2)
+    stay, leave = project(mid_grad, link_weight, 2)
     came = held(lax.ppermute(leave, "narrow", [(0, 1), (1, 0)]))
     rest = pack_grads(arrays, stay, came, chips, [0] + late, early)
     own[0] = [rest[0]]

time: 75 us -> 74.7 us (level)
    unnamed x10 -> x4, local copies, waits for them, and re-layouts: 2.98 us -> 2.97 us
  transfers between devices with their start and end apart: 35 -> 35, of which waited for: 16 -> 17; matrix products, arithmetic and copies ran while one was open for 0% -> 0% of each run, Pallas kernels for 0% -> 2%
where the time goes in v2:
time: 74.7 us; the launch traced here: 73.3 us
  starting transfers between devices  34.3 us (46%)
  waiting for transfers between devices  27.6 us (37%)
  Pallas kernels  7.62 us (10%)
  local copies, waits for them, and re-layouts  2.97 us (4%)
    ppermute x34, starting transfers between devices, cross(): lax.ppermute(block, 'wide', [(i, i ^ step) for i in range(size)])  31.3 us
    ppermute x34, waiting for transfers between devices, cross(): lax.ppermute(block, 'wide', [(i, i ^ step) for i in range(size)])  27.6 us
    pallas_call x5, Pallas kernels, local(): pl.pallas_call(kernel, in_specs=[anywhere if i in afar else vmem for i in...  7.62 us
    ppermute x1, starting transfers between devices, by_heads(): came = held(lax.ppermute(leave, 'narrow', [(0, 1), (1, 0)]))  3.06 us
    unnamed x4, local copies, waits for them, and re-layouts  2.97 us
  transfers between devices with their start and end apart: 35, of which 17 were waited for; matrix products, arithmetic and copies ran while one was open for 0% of the time, Pallas kernels for 2%

profile of v2, /device:TPU:0, one launch (start us, length us, event | category | flops | bytes accessed | tf_op | source)
XLA Modules:
  0.0 73.3 jit_solution(15186496556113738452)
XLA Ops:
  0.6 1.9 %copy-done = bf16[768,2048]{1,0:T(8,128)(2,1)S(1)} copy-done((bf16[768,2048]{1,0:T(8,128)(2,1)S(1)}, bf16[768,2048]{1,0:T(8,128)(2,1)}, u32[]{:S(2)}) %copy-start) | copy-done | bytes 3145752
  2.5 1.1 %copy-done.1 = bf16[160,2048]{1,0:T(8,128)(2,1)S(1)} copy-done((bf16[160,2048]{1,0:T(8,128)(2,1)S(1)}, bf16[160,2048]{1,0:T(8,128)(2,1)}, u32[]{:S(2)}) %copy-start.1) | copy-done | bytes 655384
  3.6 1.3 %shard_map.77 = (bf16[20,3072]{1,0:T(8,128)(2,1)S(1)}, bf16[20,3072]{1,0:T(8,128)(2,1)S(1)}) custom-call(bf16[160,2048]{1,0:T(8,128)(2,1)S(1)} %copy-done.1, bf16[768,2048]{1,0:T(8,128)(2,1)S(1)} %copy-done), custom_call_target="tpu_custom_call" | custom-call | flops 503316480 | bytes 4046848 | tf_op jit(solution)/shard_map/pallas_call | solution.py:33
  4.9 3.1 %collective-permute-start = (bf16[20,3072]{1,0:T(8,128)(2,1)S(1)}, bf16[20,3072]{1,0:T(8,128)(2,1)S(1)}, u32[]{:S(2)}, u32[]{:S(2)}) collective-permute-start(bf16[20,3072]{1,0:T(8,128)(2,1)S(1)} %get-tuple-element.30), channel_id=1, source_target_pairs={{0,1},{1,0},{2,3},{3,2},{4,5},{5,4},{6,7},{7,6},{8,9},{9,8},{10,11... | collective-permute-start | bytes 368648 | tf_op jit(solution)/shard_map/ppermute | solution.py:275
  7.9 1.2 %shard_map.76 = (bf16[40,3072]{1,0:T(8,128)(2,1)S(1)}, bf16[40,3072]{1,0:T(8,128)(2,1)S(1)}, bf16[40,3072]{1,0:T(8,128)(2,1)S(1)}, bf16[40,1152]{1,0:T(8,128)(2,1)S(1)}, bf16[40,1152]{1,0:T(8,128)(2,1)S(1)}) custom-call(bf16[40,3072]{1,0:T(8,128)(2,1)} %refs_0_.1, bf16[40,3072]{1,0:T(8,128)(2,1)} %refs_1_.1, bf16[40,3072]{1,0:T(8,128)(2,1)} %refs_2_.1), custom_call_target="tpu_custom_call" | custom-call | flops 5000000000 | bytes 1658880 | tf_op jit(solution)/shard_map/pallas_call | solution.py:33
  9.2 2.7 %collective-permute-start.4 = (bf16[40,1152]{1,0:T(8,128)(2,1)S(1)}, bf16[40,1152]{1,0:T(8,128)(2,1)S(1)}, u32[]{:S(2)}, u32[]{:S(2)}) collective-permute-start(bf16[40,1152]{1,0:T(8,128)(2,1)S(1)} %get-tuple-element.35), channel_id=1, source_target_pairs={{0,16},{2,18},{4,20},{6,22},{8,24},{10,26},{12,28},{14,30},{16,0},... | collective-permute-start | bytes 276488 | tf_op jit(solution)/shard_map/ppermute | solution.py:266
  11.8 1.3 %collective-permute-start.6 = (bf16[40,1152]{1,0:T(8,128)(2,1)S(1)}, bf16[40,1152]{1,0:T(8,128)(2,1)S(1)}, u32[]{:S(2)}, u32[]{:S(2)}) collective-permute-start(bf16[40,1152]{1,0:T(8,128)(2,1)S(1)} %get-tuple-element.37), channel_id=1, source_target_pairs={{0,20},{2,22},{4,16},{6,18},{8,28},{10,30},{12,24},{14,26},{16,4},... | collective-permute-start | bytes 276488 | tf_op jit(solution)/shard_map/ppermute | solution.py:266
  13.3 0.6 collective-permute-start.1
  13.9 4.0 %collective-permute-done.4.refs_4_ = bf16[40,1152]{1,0:T(8,128)(2,1)S(1)} collective-permute-done((bf16[40,1152]{1,0:T(8,128)(2,1)S(1)}, bf16[40,1152]{1,0:T(8,128)(2,1)S(1)}, u32[]{:S(2)}, u32[]{:S(2)}) %collective-permute-start.4) | collective-permute-done | bytes 92192 | tf_op jit(solution)/shard_map/ppermute | solution.py:266
  17.8 3.3 %collective-permute-done.6.refs_6_ = bf16[40,1152]{1,0:T(8,128)(2,1)S(1)} collective-permute-done((bf16[40,1152]{1,0:T(8,128)(2,1)S(1)}, bf16[40,1152]{1,0:T(8,128)(2,1)S(1)}, u32[]{:S(2)}, u32[]{:S(2)}) %collective-permute-start.6) | collective-permute-done | bytes 92192 | tf_op jit(solution)/shard_map/ppermute | solution.py:266
  21.1 2.9 %collective-permute-start.7 = (bf16[40,384]{1,0:T(8,128)(2,1)S(1)}, bf16[40,384]{1,0:T(8,128)(2,1)S(1)}, u32[]{:S(2)}, u32[]{:S(2)}) collective-permute-start(bf16[40,384]{1,0:T(8,128)(2,1)S(1)} %get-tuple-element.38), channel_id=1, source_target_pairs={{0,20},{2,22},{4,16},{6,18},{8,28},{10,30},{12,24},{14,26},{16,4},... | collective-permute-start | bytes 92168 | tf_op jit(solution)/shard_map/ppermute | solution.py:266
  24.0 2.7 %collective-permute-done.5.refs_5_ = bf16[40,384]{1,0:T(8,128)(2,1)S(1)} collective-permute-done((bf16[40,384]{1,0:T(8,128)(2,1)S(1)}, bf16[40,384]{1,0:T(8,128)(2,1)S(1)}, u32[]{:S(2)}, u32[]{:S(2)}) %collective-permute-start.5) | collective-permute-done | bytes 30752 | tf_op jit(solution)/shard_map/ppermute | solution.py:266
  27.3 0.7 collective-permute-done.15.refs_15_
  28.0 2.9 %collective-permute-start.2 = (bf16[40,1536]{1,0:T(8,128)(2,1)S(1)}, bf16[40,1536]{1,0:T(8,128)(2,1)S(1)}, u32[]{:S(2)}, u32[]{:S(2)}) collective-permute-start(bf16[40,1536]{1,0:T(8,128)(2,1)S(1)} %get-tuple-element.33), channel_id=1, source_target_pairs={{0,8},{2,10},{4,12},{6,14},{8,0},{10,2},{12,4},{14,6},{16,24},{18,... | collective-permute-start | bytes 368648 | tf_op jit(solution)/shard_map/ppermute | solution.py:266
  30.9 1.2 %collective-permute-start.3 = (bf16[40,1536]{1,0:T(8,128)(2,1)S(1)}, bf16[40,1536]{1,0:T(8,128)(2,1)S(1)}, u32[]{:S(2)}, u32[]{:S(2)}) collective-permute-start(bf16[40,1536]{1,0:T(8,128)(2,1)S(1)} %get-tuple-element.34), channel_id=1, source_target_pairs={{0,12},{2,14},{4,8},{6,10},{8,4},{10,6},{12,0},{14,2},{16,28},{18,... | collective-permute-start | bytes 368648 | tf_op jit(solution)/shard_map/ppermute | solution.py:266
  32.1 1.5 %collective-permute-start.8 = (bf16[40,1536]{1,0:T(8,128)(2,1)S(1)}, bf16[40,1536]{1,0:T(8,128)(2,1)S(1)}, u32[]{:S(2)}, u32[]{:S(2)}) collective-permute-start(bf16[40,1536]{1,0:T(8,128)(2,1)S(1)} %get-tuple-element.39), channel_id=1, source_target_pairs={{0,24},{2,26},{4,28},{6,30},{8,16},{10,18},{12,20},{14,22},{16,8},... | collective-permute-start | bytes 368648 | tf_op jit(solution)/shard_map/ppermute | solution.py:266
  33.5 3.3 %collective-permute-start.9 = (bf16[40,1536]{1,0:T(8,128)(2,1)S(1)}, bf16[40,1536]{1,0:T(8,128)(2,1)S(1)}, u32[]{:S(2)}, u32[]{:S(2)}) collective-permute-start(bf16[40,1536]{1,0:T(8,128)(2,1)S(1)} %get-tuple-element.40), channel_id=1, source_target_pairs={{0,28},{2,30},{4,24},{6,26},{8,20},{10,22},{12,16},{14,18},{16,12}... | collective-permute-start | bytes 368648 | tf_op jit(solution)/shard_map/ppermute | solution.py:266
  37.5 3.3 %collective-permute-done.8.refs_8_ = bf16[40,1536]{1,0:T(8,128)(2,1)S(1)} collective-permute-done((bf16[40,1536]{1,0:T(8,128)(2,1)S(1)}, bf16[40,1536]{1,0:T(8,128)(2,1)S(1)}, u32[]{:S(2)}, u32[]{:S(2)}) %collective-permute-start.8) | collective-permute-done | bytes 122912 | tf_op jit(solution)/shard_map/ppermute | solution.py:266
  40.8 2.7 %collective-permute-done.9.refs_9_ = bf16[40,1536]{1,0:T(8,128)(2,1)S(1)} collective-permute-done((bf16[40,1536]{1,0:T(8,128)(2,1)S(1)}, bf16[40,1536]{1,0:T(8,128)(2,1)S(1)}, u32[]{:S(2)}, u32[]{:S(2)}) %collective-permute-start.9) | collective-permute-done | bytes 122912 | tf_op jit(solution)/shard_map/ppermute | solution.py:266
  43.5 0.5 collective-permute-start.19
  44.0 0.8 %collective-permute-done.18.refs_18_ = bf16[40,1536]{1,0:T(8,128)(2,1)S(1)} collective-permute-done((bf16[40,1536]{1,0:T(8,128)(2,1)S(1)}, bf16[40,1536]{1,0:T(8,128)(2,1)S(1)}, u32[]{:S(2)}, u32[]{:S(2)}) %collective-permute-start.18) | collective-permute-done | bytes 122912 | tf_op jit(solution)/shard_map/ppermute | solution.py:266
  45.0 3.9 %shard_map.79 = (bf16[3,40,384]{2,1,0:T(8,128)(2,1)S(1)}, bf16[3,40,384]{2,1,0:T(8,128)(2,1)S(1)}, bf16[3,40,384]{2,1,0:T(8,128)(2,1)S(1)}, bf16[3,40,384]{2,1,0...) custom-call(bf16[40,1536]{1,0:T(8,128)(2,1)S(1)} %get-tuple-element., ...), custom_call_target="tpu_custom_call" | custom-call | flops 524288000 | bytes 2703360 | tf_op jit(solution)/shard_map/pallas_call | solution.py:33
  48.9 1.0 %collective-permute-start.20 = (bf16[3,40,384]{2,1,0:T(8,128)(2,1)S(1)}, bf16[3,40,384]{2,1,0:T(8,128)(2,1)S(1)}, u32[]{:S(2)}, u32[]{:S(2)}) collective-permute-start(bf16[3,40,384]{2,1,0:T(8,128)(2,1)S(1)} %get-tuple-element.42), channel_id=1, source_target_pairs={{0,4},{2,6},{4,0},{6,2},{8,12},{10,14},{12,8},{14,10},{16,20},{18,... | collective-permute-start | bytes 276488 | tf_op jit(solution)/shard_map/ppermute | solution.py:266
  49.9 3.0 %collective-permute-start.21 = (bf16[3,40,384]{2,1,0:T(8,128)(2,1)S(1)}, bf16[3,40,384]{2,1,0:T(8,128)(2,1)S(1)}, u32[]{:S(2)}, u32[]{:S(2)}) collective-permute-start(bf16[3,40,384]{2,1,0:T(8,128)(2,1)S(1)} %get-tuple-element.43), channel_id=1, source_target_pairs={{0,8},{2,10},{4,12},{6,14},{8,0},{10,2},{12,4},{14,6},{16,24},{18,... | collective-permute-start | bytes 276488 | tf_op jit(solution)/shard_map/ppermute | solution.py:266
  52.9 0.9 %collective-permute-start.22 = (bf16[3,40,384]{2,1,0:T(8,128)(2,1)S(1)}, bf16[3,40,384]{2,1,0:T(8,128)(2,1)S(1)}, u32[]{:S(2)}, u32[]{:S(2)}) collective-permute-start(bf16[3,40,384]{2,1,0:T(8,128)(2,1)S(1)} %get-tuple-element.44), channel_id=1, source_target_pairs={{0,12},{2,14},{4,8},{6,10},{8,4},{10,6},{12,0},{14,2},{16,28},{18,... | collective-permute-start | bytes 276488 | tf_op jit(solution)/shard_map/ppermute | solution.py:266
  53.9 1.7 %collective-permute-start.23 = (bf16[3,40,384]{2,1,0:T(8,128)(2,1)S(1)}, bf16[3,40,384]{2,1,0:T(8,128)(2,1)S(1)}, u32[]{:S(2)}, u32[]{:S(2)}) collective-permute-start(bf16[3,40,384]{2,1,0:T(8,128)(2,1)S(1)} %get-tuple-element.45), channel_id=1, source_target_pairs={{0,16},{2,18},{4,20},{6,22},{8,24},{10,26},{12,28},{14,30},{16,0},... | collective-permute-start | bytes 276488 | tf_op jit(solution)/shard_map/ppermute | solution.py:266
  55.6 1.2 %collective-permute-start.24 = (bf16[3,40,384]{2,1,0:T(8,128)(2,1)S(1)}, bf16[3,40,384]{2,1,0:T(8,128)(2,1)S(1)}, u32[]{:S(2)}, u32[]{:S(2)}) collective-permute-start(bf16[3,40,384]{2,1,0:T(8,128)(2,1)S(1)} %get-tuple-element.46), channel_id=1, source_target_pairs={{0,20},{2,22},{4,16},{6,18},{8,28},{10,30},{12,24},{14,26},{16,4},... | collective-permute-start | bytes 276488 | tf_op jit(solution)/shard_map/ppermute | solution.py:266
  56.8 2.7 %collective-permute-start.25 = (bf16[3,40,384]{2,1,0:T(8,128)(2,1)S(1)}, bf16[3,40,384]{2,1,0:T(8,128)(2,1)S(1)}, u32[]{:S(2)}, u32[]{:S(2)}) collective-permute-start(bf16[3,40,384]{2,1,0:T(8,128)(2,1)S(1)} %get-tuple-element.47), channel_id=1, source_target_pairs={{0,24},{2,26},{4,28},{6,30},{8,16},{10,18},{12,20},{14,22},{16,8},... | collective-permute-start | bytes 276488 | tf_op jit(solution)/shard_map/ppermute | solution.py:266
  59.5 2.0 %collective-permute-start.26 = (bf16[3,40,384]{2,1,0:T(8,128)(2,1)S(1)}, bf16[3,40,384]{2,1,0:T(8,128)(2,1)S(1)}, u32[]{:S(2)}, u32[]{:S(2)}) collective-permute-start(bf16[3,40,384]{2,1,0:T(8,128)(2,1)S(1)} %get-tuple-element.48), channel_id=1, source_target_pairs={{0,28},{2,30},{4,24},{6,26},{8,20},{10,22},{12,16},{14,18},{16,12}... | collective-permute-start | bytes 276488 | tf_op jit(solution)/shard_map/ppermute | solution.py:266
  61.5 6.3 %collective-permute-done.23.refs_4_ = bf16[3,40,384]{2,1,0:T(8,128)(2,1)S(1)} collective-permute-done((bf16[3,40,384]{2,1,0:T(8,128)(2,1)S(1)}, bf16[3,40,384]{2,1,0:T(8,128)(2,1)S(1)}, u32[]{:S(2)}, u32[]{:S(2)}) %collective-permute-start.23) | collective-permute-done | bytes 92192 | tf_op jit(solution)/shard_map/ppermute | solution.py:266
  67.9 1.8 %collective-permute-done.24.refs_5_ = bf16[3,40,384]{2,1,0:T(8,128)(2,1)S(1)} collective-permute-done((bf16[3,40,384]{2,1,0:T(8,128)(2,1)S(1)}, bf16[3,40,384]{2,1,0:T(8,128)(2,1)S(1)}, u32[]{:S(2)}, u32[]{:S(2)}) %collective-permute-start.24) | collective-permute-done | bytes 92192 | tf_op jit(solution)/shard_map/ppermute | solution.py:266
  72.2 1.0 %shard_map.80 = (bf16[40,3072]{1,0:T(8,128)(2,1)}, bf16[40,3072]{1,0:T(8,128)(2,1)}, bf16[40,3072]{1,0:T(8,128)(2,1)}) custom-call(bf16[3,40,384]{2,1,0:T(8,128)(2,1)S(1)} %get-tuple-element.41.refs_0_, bf16[3,40,384]{2,1,0:T(8,128)(2,1)S(1)} %collective-permute-done.20.refs_1_, bf16[3,40,384]{2,1,0:T(8,128)(2,1)S(1)} %collective-permute-done.21.refs_2_, ...), custom_call_target="tpu_custom_call" | custom-call | bytes 2211840 | tf_op jit(solution)/shard_map/pallas_call | solution.py:33
  (47 shorter events, 4.2 us)
Async XLA Ops:
  4.9 8.2 %collective-permute-start = (bf16[20,3072]{1,0:T(8,128)(2,1)S(1)}, bf16[20,3072]{1,0:T(8,128)(2,1)S(1)}, u32[]{:S(2)}, u32[]{:S(2)}) collective-permute-start(bf16[20,3072]{1,0:T(8,128)(2,1)S(1)} %get-tuple-element.30), channel_id=1, source_target_pairs={{0,1},{1,0},{2,3},{3,2},{4,5},{5,4},{6,7},{7,6},{8,9},{9,8},{10,11... | collective-permute-start | bytes 368648 | tf_op jit(solution)/shard_map/ppermute | solution.py:275
  9.2 8.6 %collective-permute-start.4 = (bf16[40,1152]{1,0:T(8,128)(2,1)S(1)}, bf16[40,1152]{1,0:T(8,128)(2,1)S(1)}, u32[]{:S(2)}, u32[]{:S(2)}) collective-permute-start(bf16[40,1152]{1,0:T(8,128)(2,1)S(1)} %get-tuple-element.35), channel_id=1, source_target_pairs={{0,16},{2,18},{4,20},{6,22},{8,24},{10,26},{12,28},{14,30},{16,0},... | collective-permute-start | bytes 276488 | tf_op jit(solution)/shard_map/ppermute | solution.py:266
  11.8 9.3 %collective-permute-start.6 = (bf16[40,1152]{1,0:T(8,128)(2,1)S(1)}, bf16[40,1152]{1,0:T(8,128)(2,1)S(1)}, u32[]{:S(2)}, u32[]{:S(2)}) collective-permute-start(bf16[40,1152]{1,0:T(8,128)(2,1)S(1)} %get-tuple-element.37), channel_id=1, source_target_pairs={{0,20},{2,22},{4,16},{6,18},{8,28},{10,30},{12,24},{14,26},{16,4},... | collective-permute-start | bytes 276488 | tf_op jit(solution)/shard_map/ppermute | solution.py:266
  13.3 23.5 %collective-permute-start.1 = (bf16[40,1536]{1,0:T(8,128)(2,1)S(1)}, bf16[40,1536]{1,0:T(8,128)(2,1)S(1)}, u32[]{:S(2)}, u32[]{:S(2)}) collective-permute-start(bf16[40,1536]{1,0:T(8,128)(2,1)S(1)} %get-tuple-element.32), channel_id=1, source_target_pairs={{0,4},{2,6},{4,0},{6,2},{8,12},{10,14},{12,8},{14,10},{16,20},{18,... | collective-permute-start | bytes 368648 | tf_op jit(solution)/shard_map/ppermute | solution.py:266
  17.8 14.2 %collective-permute-start.14 = (bf16[40,1152]{1,0:T(8,128)(2,1)S(1)}, bf16[40,1152]{1,0:T(8,128)(2,1)S(1)}, u32[]{:S(2)}, u32[]{:S(2)}) collective-permute-start(bf16[40,1152]{1,0:T(8,128)(2,1)S(1)} %collective-permute-done.4.refs_4_), channel_id=1, source_target_pairs={{0,2},{2,0},{4,6},{6,4},{8,10},{10,8},{12,14},{14,12},{16,18},{18,... | collective-permute-start | bytes 276488 | tf_op jit(solution)/shard_map/ppermute | solution.py:266
  21.1 12.4 %collective-permute-start.16 = (bf16[40,1152]{1,0:T(8,128)(2,1)S(1)}, bf16[40,1152]{1,0:T(8,128)(2,1)S(1)}, u32[]{:S(2)}, u32[]{:S(2)}) collective-permute-start(bf16[40,1152]{1,0:T(8,128)(2,1)S(1)} %collective-permute-done.6.refs_6_), channel_id=1, source_target_pairs={{0,2},{2,0},{4,6},{6,4},{8,10},{10,8},{12,14},{14,12},{16,18},{18,... | collective-permute-start | bytes 276488 | tf_op jit(solution)/shard_map/ppermute | solution.py:266
  21.1 5.6 %collective-permute-start.5 = (bf16[40,384]{1,0:T(8,128)(2,1)S(1)}, bf16[40,384]{1,0:T(8,128)(2,1)S(1)}, u32[]{:S(2)}, u32[]{:S(2)}) collective-permute-start(bf16[40,384]{1,0:T(8,128)(2,1)S(1)} %get-tuple-element.36), channel_id=1, source_target_pairs={{0,16},{2,18},{4,20},{6,22},{8,24},{10,26},{12,28},{14,30},{16,0},... | collective-permute-start | bytes 92168 | tf_op jit(solution)/shard_map/ppermute | solution.py:266
  21.1 6.1 %collective-permute-start.7 = (bf16[40,384]{1,0:T(8,128)(2,1)S(1)}, bf16[40,384]{1,0:T(8,128)(2,1)S(1)}, u32[]{:S(2)}, u32[]{:S(2)}) collective-permute-start(bf16[40,384]{1,0:T(8,128)(2,1)S(1)} %get-tuple-element.38), channel_id=1, source_target_pairs={{0,20},{2,22},{4,16},{6,18},{8,28},{10,30},{12,24},{14,26},{16,4},... | collective-permute-start | bytes 92168 | tf_op jit(solution)/shard_map/ppermute | solution.py:266
  27.3 3.6 %collective-permute-start.17 = (bf16[40,384]{1,0:T(8,128)(2,1)S(1)}, bf16[40,384]{1,0:T(8,128)(2,1)S(1)}, u32[]{:S(2)}, u32[]{:S(2)}) collective-permute-start(bf16[40,384]{1,0:T(8,128)(2,1)S(1)} %collective-permute-done.7.refs_7_), channel_id=1, source_target_pairs={{0,2},{2,0},{4,6},{6,4},{8,10},{10,8},{12,14},{14,12},{16,18},{18,... | collective-permute-start | bytes 92168 | tf_op jit(solution)/shard_map/ppermute | solution.py:266
  28.0 8.8 %collective-permute-start.2 = (bf16[40,1536]{1,0:T(8,128)(2,1)S(1)}, bf16[40,1536]{1,0:T(8,128)(2,1)S(1)}, u32[]{:S(2)}, u32[]{:S(2)}) collective-permute-start(bf16[40,1536]{1,0:T(8,128)(2,1)S(1)} %get-tuple-element.33), channel_id=1, source_target_pairs={{0,8},{2,10},{4,12},{6,14},{8,0},{10,2},{12,4},{14,6},{16,24},{18,... | collective-permute-start | bytes 368648 | tf_op jit(solution)/shard_map/ppermute | solution.py:266
  30.9 6.6 %collective-permute-start.3 = (bf16[40,1536]{1,0:T(8,128)(2,1)S(1)}, bf16[40,1536]{1,0:T(8,128)(2,1)S(1)}, u32[]{:S(2)}, u32[]{:S(2)}) collective-permute-start(bf16[40,1536]{1,0:T(8,128)(2,1)S(1)} %get-tuple-element.34), channel_id=1, source_target_pairs={{0,12},{2,14},{4,8},{6,10},{8,4},{10,6},{12,0},{14,2},{16,28},{18,... | collective-permute-start | bytes 368648 | tf_op jit(solution)/shard_map/ppermute | solution.py:266
  32.1 8.8 %collective-permute-start.8 = (bf16[40,1536]{1,0:T(8,128)(2,1)S(1)}, bf16[40,1536]{1,0:T(8,128)(2,1)S(1)}, u32[]{:S(2)}, u32[]{:S(2)}) collective-permute-start(bf16[40,1536]{1,0:T(8,128)(2,1)S(1)} %get-tuple-element.39), channel_id=1, source_target_pairs={{0,24},{2,26},{4,28},{6,30},{8,16},{10,18},{12,20},{14,22},{16,8},... | collective-permute-start | bytes 368648 | tf_op jit(solution)/shard_map/ppermute | solution.py:266
  33.5 10.0 %collective-permute-start.9 = (bf16[40,1536]{1,0:T(8,128)(2,1)S(1)}, bf16[40,1536]{1,0:T(8,128)(2,1)S(1)}, u32[]{:S(2)}, u32[]{:S(2)}) collective-permute-start(bf16[40,1536]{1,0:T(8,128)(2,1)S(1)} %get-tuple-element.40), channel_id=1, source_target_pairs={{0,28},{2,30},{4,24},{6,26},{8,20},{10,22},{12,16},{14,18},{16,12}... | collective-permute-start | bytes 368648 | tf_op jit(solution)/shard_map/ppermute | solution.py:266
  36.8 6.7 %collective-permute-start.10 = (bf16[40,1536]{1,0:T(8,128)(2,1)S(1)}, bf16[40,1536]{1,0:T(8,128)(2,1)S(1)}, u32[]{:S(2)}, u32[]{:S(2)}) collective-permute-start(bf16[40,1536]{1,0:T(8,128)(2,1)S(1)} %get-tuple-element.31.refs_0_), channel_id=1, source_target_pairs={{0,2},{2,0},{4,6},{6,4},{8,10},{10,8},{12,14},{14,12},{16,18},{18,... | collective-permute-start | bytes 368648 | tf_op jit(solution)/shard_map/ppermute | solution.py:266
  36.8 7.2 %collective-permute-start.11 = (bf16[40,1536]{1,0:T(8,128)(2,1)S(1)}, bf16[40,1536]{1,0:T(8,128)(2,1)S(1)}, u32[]{:S(2)}, u32[]{:S(2)}) collective-permute-start(bf16[40,1536]{1,0:T(8,128)(2,1)S(1)} %collective-permute-done.1.refs_1_), channel_id=1, source_target_pairs={{0,2},{2,0},{4,6},{6,4},{8,10},{10,8},{12,14},{14,12},{16,18},{18,... | collective-permute-start | bytes 368648 | tf_op jit(solution)/shard_map/ppermute | solution.py:266
  37.5 6.5 %collective-permute-start.12 = (bf16[40,1536]{1,0:T(8,128)(2,1)S(1)}, bf16[40,1536]{1,0:T(8,128)(2,1)S(1)}, u32[]{:S(2)}, u32[]{:S(2)}) collective-permute-start(bf16[40,1536]{1,0:T(8,128)(2,1)S(1)} %collective-permute-done.2.refs_2_), channel_id=1, source_target_pairs={{0,2},{2,0},{4,6},{6,4},{8,10},{10,8},{12,14},{14,12},{16,18},{18,... | collective-permute-start | bytes 368648 | tf_op jit(solution)/shard_map/ppermute | solution.py:266
  40.8 3.2 %collective-permute-start.13 = (bf16[40,1536]{1,0:T(8,128)(2,1)S(1)}, bf16[40,1536]{1,0:T(8,128)(2,1)S(1)}, u32[]{:S(2)}, u32[]{:S(2)}) collective-permute-start(bf16[40,1536]{1,0:T(8,128)(2,1)S(1)} %collective-permute-done.3.refs_3_), channel_id=1, source_target_pairs={{0,2},{2,0},{4,6},{6,4},{8,10},{10,8},{12,14},{14,12},{16,18},{18,... | collective-permute-start | bytes 368648 | tf_op jit(solution)/shard_map/ppermute | solution.py:266
  43.5 1.3 %collective-permute-start.18 = (bf16[40,1536]{1,0:T(8,128)(2,1)S(1)}, bf16[40,1536]{1,0:T(8,128)(2,1)S(1)}, u32[]{:S(2)}, u32[]{:S(2)}) collective-permute-start(bf16[40,1536]{1,0:T(8,128)(2,1)S(1)} %collective-permute-done.8.refs_8_), channel_id=1, source_target_pairs={{0,2},{2,0},{4,6},{6,4},{8,10},{10,8},{12,14},{14,12},{16,18},{18,... | collective-permute-start | bytes 368648 | tf_op jit(solution)/shard_map/ppermute | solution.py:266
  43.5 1.5 %collective-permute-start.19 = (bf16[40,1536]{1,0:T(8,128)(2,1)S(1)}, bf16[40,1536]{1,0:T(8,128)(2,1)S(1)}, u32[]{:S(2)}, u32[]{:S(2)}) collective-permute-start(bf16[40,1536]{1,0:T(8,128)(2,1)S(1)} %collective-permute-done.9.refs_9_), channel_id=1, source_target_pairs={{0,2},{2,0},{4,6},{6,4},{8,10},{10,8},{12,14},{14,12},{16,18},{18,... | collective-permute-start | bytes 368648 | tf_op jit(solution)/shard_map/ppermute | solution.py:266
  48.9 7.9 %collective-permute-start.20 = (bf16[3,40,384]{2,1,0:T(8,128)(2,1)S(1)}, bf16[3,40,384]{2,1,0:T(8,128)(2,1)S(1)}, u32[]{:S(2)}, u32[]{:S(2)}) collective-permute-start(bf16[3,40,384]{2,1,0:T(8,128)(2,1)S(1)} %get-tuple-element.42), channel_id=1, source_target_pairs={{0,4},{2,6},{4,0},{6,2},{8,12},{10,14},{12,8},{14,10},{16,20},{18,... | collective-permute-start | bytes 276488 | tf_op jit(solution)/shard_map/ppermute | solution.py:266
  49.9 9.6 %collective-permute-start.21 = (bf16[3,40,384]{2,1,0:T(8,128)(2,1)S(1)}, bf16[3,40,384]{2,1,0:T(8,128)(2,1)S(1)}, u32[]{:S(2)}, u32[]{:S(2)}) collective-permute-start(bf16[3,40,384]{2,1,0:T(8,128)(2,1)S(1)} %get-tuple-element.43), channel_id=1, source_target_pairs={{0,8},{2,10},{4,12},{6,14},{8,0},{10,2},{12,4},{14,6},{16,24},{18,... | collective-permute-start | bytes 276488 | tf_op jit(solution)/shard_map/ppermute | solution.py:266
  52.9 8.6 %collective-permute-start.22 = (bf16[3,40,384]{2,1,0:T(8,128)(2,1)S(1)}, bf16[3,40,384]{2,1,0:T(8,128)(2,1)S(1)}, u32[]{:S(2)}, u32[]{:S(2)}) collective-permute-start(bf16[3,40,384]{2,1,0:T(8,128)(2,1)S(1)} %get-tuple-element.44), channel_id=1, source_target_pairs={{0,12},{2,14},{4,8},{6,10},{8,4},{10,6},{12,0},{14,2},{16,28},{18,... | collective-permute-start | bytes 276488 | tf_op jit(solution)/shard_map/ppermute | solution.py:266
  53.9 14.0 %collective-permute-start.23 = (bf16[3,40,384]{2,1,0:T(8,128)(2,1)S(1)}, bf16[3,40,384]{2,1,0:T(8,128)(2,1)S(1)}, u32[]{:S(2)}, u32[]{:S(2)}) collective-permute-start(bf16[3,40,384]{2,1,0:T(8,128)(2,1)S(1)} %get-tuple-element.45), channel_id=1, source_target_pairs={{0,16},{2,18},{4,20},{6,22},{8,24},{10,26},{12,28},{14,30},{16,0},... | collective-permute-start | bytes 276488 | tf_op jit(solution)/shard_map/ppermute | solution.py:266
  55.6 14.0 %collective-permute-start.24 = (bf16[3,40,384]{2,1,0:T(8,128)(2,1)S(1)}, bf16[3,40,384]{2,1,0:T(8,128)(2,1)S(1)}, u32[]{:S(2)}, u32[]{:S(2)}) collective-permute-start(bf16[3,40,384]{2,1,0:T(8,128)(2,1)S(1)} %get-tuple-element.46), channel_id=1, source_target_pairs={{0,20},{2,22},{4,16},{6,18},{8,28},{10,30},{12,24},{14,26},{16,4},... | collective-permute-start | bytes 276488 | tf_op jit(solution)/shard_map/ppermute | solution.py:266
  56.8 12.8 %collective-permute-start.25 = (bf16[3,40,384]{2,1,0:T(8,128)(2,1)S(1)}, bf16[3,40,384]{2,1,0:T(8,128)(2,1)S(1)}, u32[]{:S(2)}, u32[]{:S(2)}) collective-permute-start(bf16[3,40,384]{2,1,0:T(8,128)(2,1)S(1)} %get-tuple-element.47), channel_id=1, source_target_pairs={{0,24},{2,26},{4,28},{6,30},{8,16},{10,18},{12,20},{14,22},{16,8},... | collective-permute-start | bytes 276488 | tf_op jit(solution)/shard_map/ppermute | solution.py:266
  59.5 10.6 %collective-permute-start.26 = (bf16[3,40,384]{2,1,0:T(8,128)(2,1)S(1)}, bf16[3,40,384]{2,1,0:T(8,128)(2,1)S(1)}, u32[]{:S(2)}, u32[]{:S(2)}) collective-permute-start(bf16[3,40,384]{2,1,0:T(8,128)(2,1)S(1)} %get-tuple-element.48), channel_id=1, source_target_pairs={{0,28},{2,30},{4,24},{6,26},{8,20},{10,22},{12,16},{14,18},{16,12}... | collective-permute-start | bytes 276488 | tf_op jit(solution)/shard_map/ppermute | solution.py:266
  61.5 8.7 %collective-permute-start.27 = (bf16[3,40,384]{2,1,0:T(8,128)(2,1)S(1)}, bf16[3,40,384]{2,1,0:T(8,128)(2,1)S(1)}, u32[]{:S(2)}, u32[]{:S(2)}) collective-permute-start(bf16[3,40,384]{2,1,0:T(8,128)(2,1)S(1)} %get-tuple-element.41.refs_0_), channel_id=1, source_target_pairs={{0,2},{2,0},{4,6},{6,4},{8,10},{10,8},{12,14},{14,12},{16,18},{18,... | collective-permute-start | bytes 276488 | tf_op jit(solution)/shard_map/ppermute | solution.py:266
  67.9 2.8 %collective-permute-start.28 = (bf16[3,40,384]{2,1,0:T(8,128)(2,1)S(1)}, bf16[3,40,384]{2,1,0:T(8,128)(2,1)S(1)}, u32[]{:S(2)}, u32[]{:S(2)}) collective-permute-start(bf16[3,40,384]{2,1,0:T(8,128)(2,1)S(1)} %collective-permute-done.20.refs_1_), channel_id=1, source_target_pairs={{0,2},{2,0},{4,6},{6,4},{8,10},{10,8},{12,14},{14,12},{16,18},{18,... | collective-permute-start | bytes 276488 | tf_op jit(solution)/shard_map/ppermute | solution.py:266
  69.6 1.5 %collective-permute-start.30 = (bf16[3,40,384]{2,1,0:T(8,128)(2,1)S(1)}, bf16[3,40,384]{2,1,0:T(8,128)(2,1)S(1)}, u32[]{:S(2)}, u32[]{:S(2)}) collective-permute-start(bf16[3,40,384]{2,1,0:T(8,128)(2,1)S(1)} %collective-permute-done.22.refs_3_), channel_id=1, source_target_pairs={{0,2},{2,0},{4,6},{6,4},{8,10},{10,8},{12,14},{14,12},{16,18},{18,... | collective-permute-start | bytes 276488 | tf_op jit(solution)/shard_map/ppermute | solution.py:266
  70.2 1.3 %collective-permute-start.31 = (bf16[3,40,384]{2,1,0:T(8,128)(2,1)S(1)}, bf16[3,40,384]{2,1,0:T(8,128)(2,1)S(1)}, u32[]{:S(2)}, u32[]{:S(2)}) collective-permute-start(bf16[3,40,384]{2,1,0:T(8,128)(2,1)S(1)} %collective-permute-done.23.refs_4_), channel_id=1, source_target_pairs={{0,2},{2,0},{4,6},{6,4},{8,10},{10,8},{12,14},{14,12},{16,18},{18,... | collective-permute-start | bytes 276488 | tf_op jit(solution)/shard_map/ppermute | solution.py:266
  70.2 1.4 %collective-permute-start.32 = (bf16[3,40,384]{2,1,0:T(8,128)(2,1)S(1)}, bf16[3,40,384]{2,1,0:T(8,128)(2,1)S(1)}, u32[]{:S(2)}, u32[]{:S(2)}) collective-permute-start(bf16[3,40,384]{2,1,0:T(8,128)(2,1)S(1)} %collective-permute-done.24.refs_5_), channel_id=1, source_target_pairs={{0,2},{2,0},{4,6},{6,4},{8,10},{10,8},{12,14},{14,12},{16,18},{18,... | collective-permute-start | bytes 276488 | tf_op jit(solution)/shard_map/ppermute | solution.py:266
  70.7 1.3 %collective-permute-start.33 = (bf16[3,40,384]{2,1,0:T(8,128)(2,1)S(1)}, bf16[3,40,384]{2,1,0:T(8,128)(2,1)S(1)}, u32[]{:S(2)}, u32[]{:S(2)}) collective-permute-start(bf16[3,40,384]{2,1,0:T(8,128)(2,1)S(1)} %collective-permute-done.25.refs_6_), channel_id=1, source_target_pairs={{0,2},{2,0},{4,6},{6,4},{8,10},{10,8},{12,14},{14,12},{16,18},{18,... | collective-permute-start | bytes 276488 | tf_op jit(solution)/shard_map/ppermute | solution.py:266
  (5 other events, 6.8 us)

commit v3 on v1

--- a/solution.py
+++ b/solution.py
@@ -10,7 +10,7 @@
 
 HD = 128
 PATCH = 8
-TILE = 128
+TILE = 320
 ROOM = 24 << 20
 
 
@@ -18,13 +18,16 @@
 
 
 def in_order(chips):
-    far = list(range(chips // 2, chips))
-    near = list(range(1, chips // 2))[::-1]
-    return far[:2], far[2:] + near
-
-
-def local(kernel, ins, shapes, scratch=(), flops=0, final=False):
-    vmem = pl.BlockSpec(memory_space=pltpu.VMEM)
+    far, near = far_and_near(chips)
+    return far[:3], far[3:] + near
+
+
+def far_and_near(chips):
+    return list(range(chips // 2, chips)), list(range(1, chips // 2))[::-1]
+
+
+def local(kernel, ins, shapes, scratch=(), flops=0, final=False, afar=()):
+    vmem, anywhere = (pl.BlockSpec(memory_space=space) for space in (pltpu.VMEM, pltpu.HBM))
     outs = [
         jax.ShapeDtypeStruct(shape, jnp.bfloat16) if final else pltpu.VMEM(shape, jnp.bfloat16)
         for shape in shapes
@@ -32,13 +35,13 @@
     moved = 2 * (sum(array.size for array in ins) + sum(math.prod(shape) for shape in shapes))
     return pl.pallas_call(
         kernel,
-        in_specs=[vmem] * len(ins),
+        in_specs=[anywhere if i in afar else vmem for i in range(len(ins))],
         out_specs=[vmem] * len(shapes),
         out_shape=outs,
         scratch_shapes=list(scratch),
         compiler_params=pltpu.CompilerParams(vmem_limit_bytes=ROOM),
         cost_estimate=pl.CostEstimate(flops=flops, bytes_accessed=moved, transcendentals=0),
-    )(*ins)
+    )(*(pltpu.with_memory_space_constraint(x, pltpu.HBM) if i in afar else x for i, x in enumerate(ins)))
 
 
 def held(array):
@@ -82,19 +85,36 @@
     )
 
 
-def pack(arrays, chips, steps):
+def pack(arrays, chips, steps, first=False):
     rows, columns = arrays[0].shape
     wide = columns // chips
+    count = len(arrays)
 
     def kernel(*refs):
-        ins, outs = refs[: len(arrays)], refs[len(arrays) :]
+        ins, outs = refs[:count], refs[count : count + len(steps)]
         chip = where_am_i()[0]
-        for out, step in zip(outs, steps):
+        copies = []
+        for at, (out, step) in enumerate(zip(outs, steps)):
             start = pl.multiple_of((chip ^ step) * wide, HD)
             for which, ref in enumerate(ins):
-                out[:, which * wide : (which + 1) * wide] = ref[:, pl.ds(start, wide)]
-
-    return local(kernel, arrays, [(rows, len(arrays) * wide)] * len(steps))
+                source, target = ref.at[:, pl.ds(start, wide)], out.at[:, which * wide : (which + 1) * wide]
+                if first:
+                    arrived = refs[-1].at[at * count + which]
+                    copies.append(pltpu.make_async_copy(source, target, arrived))
+                    copies[-1].start()
+                else:
+                    target[...] = source[...]
+        for copy in copies:
+            copy.wait()
+
+    return local(
+        kernel,
+        arrays,
+        [(rows, count * wide)] * len(steps),
+        [pltpu.SemaphoreType.DMA((count * len(steps),))] if first else (),
+        flops=5 * 10**9 if first else 0,
+        afar=range(count) if first else (),
+    )
 
 
 def pack_grads(arrays, stay, came, chips, steps, early):
@@ -249,12 +269,13 @@
         return held(lax.ppermute(block, "wide", [(i, i ^ step) for i in range(size)]))
 
     early, late = in_order(chips)
-    arrays = [held(query_rows), held(key_rows), held(value_rows)]
     own = {}
-    ahead = pack(arrays, chips, early) if early else []
+    arrays = [query_rows, key_rows, value_rows]
+    ahead = pack(arrays, chips, early[:1], first=True)
+    ahead += pack(arrays, chips, early[1:]) if early[1:] else []
     for step, block in zip(early, ahead):
         own[step] = [cross(block, 2 * step)]
-    stay, leave = project(held(mid_grad), held(link_weight), 2)
+    stay, leave = project(mid_grad, link_weight, 2)
     came = held(lax.ppermute(leave, "narrow", [(0, 1), (1, 0)]))
     rest = pack_grads(arrays, stay, came, chips, [0] + late, early)
     own[0] = [rest[0]]

time: 75 us -> 76.3 us (1.017)
  starting transfers between devices: 34.8 us -> 40.7 us
  waiting for transfers between devices: 27.1 us -> 23.5 us
  Pallas kernels: 8.01 us -> 7.23 us
    ppermute x34 -> x36, starting transfers between devices: 31.8 us -> 37.6 us  [cross(): lax.ppermute(block, 'wide', [(i, i ^ step) for i in range(size)])]
    ppermute x34 -> x36, waiting for transfers between devices: 27.1 us -> 23.5 us  [cross(): lax.ppermute(block, 'wide', [(i, i ^ step) for i in range(size)])]
    pallas_call x5 -> x6, Pallas kernels: 8.01 us -> 7.23 us  [local(): pl.pallas_call(kernel, in_specs=[anywhere if i in afar else vmem for i in...]
  transfers between devices with their start and end apart: 35 -> 37, of which waited for: 16 -> 19; matrix products, arithmetic and copies ran while one was open for 0% -> 0% of each run, Pallas kernels for 0% -> 1%
where the time goes in v3:
time: 76.3 us; the launch traced here: 75.2 us
  starting transfers between devices  40.7 us (53%)
  waiting for transfers between devices  23.5 us (31%)
  Pallas kernels  7.23 us (9%)
  local copies, waits for them, and re-layouts  2.99 us (4%)
    ppermute x36, starting transfers between devices, cross(): lax.ppermute(block, 'wide', [(i, i ^ step) for i in range(size)])  37.6 us
    ppermute x36, waiting for transfers between devices, cross(): lax.ppermute(block, 'wide', [(i, i ^ step) for i in range(size)])  23.5 us
    pallas_call x6, Pallas kernels, local(): pl.pallas_call(kernel, in_specs=[anywhere if i in afar else vmem for i in...  7.23 us
    ppermute x1, starting transfers between devices, by_heads(): came = held(lax.ppermute(leave, 'narrow', [(0, 1), (1, 0)]))  3.06 us
    unnamed x10, local copies, waits for them, and re-layouts  2.99 us
  transfers between devices with their start and end apart: 37, of which 19 were waited for; matrix products, arithmetic and copies ran while one was open for 0% of the time, Pallas kernels for 1%

profile of v3, /device:TPU:0, one launch (start us, length us, event | category | flops | bytes accessed | tf_op | source)
XLA Modules:
  0.0 75.2 jit_solution(4511206205442122445)
XLA Ops:
  0.6 1.9 %copy-done = bf16[768,2048]{1,0:T(8,128)(2,1)S(1)} copy-done((bf16[768,2048]{1,0:T(8,128)(2,1)S(1)}, bf16[768,2048]{1,0:T(8,128)(2,1)}, u32[]{:S(2)}) %copy-start) | copy-done | bytes 3145752
  2.5 1.1 %copy-done.4 = bf16[160,2048]{1,0:T(8,128)(2,1)S(1)} copy-done((bf16[160,2048]{1,0:T(8,128)(2,1)S(1)}, bf16[160,2048]{1,0:T(8,128)(2,1)}, u32[]{:S(2)}) %copy-start.4) | copy-done | bytes 655384
  3.6 1.3 %shard_map.76 = (bf16[20,3072]{1,0:T(8,128)(2,1)S(1)}, bf16[20,3072]{1,0:T(8,128)(2,1)S(1)}) custom-call(bf16[160,2048]{1,0:T(8,128)(2,1)S(1)} %copy-done.4, bf16[768,2048]{1,0:T(8,128)(2,1)S(1)} %copy-done), custom_call_target="tpu_custom_call" | custom-call | flops 503316480 | bytes 4046848 | tf_op jit(solution)/shard_map/pallas_call | solution.py:36
  4.9 3.1 %collective-permute-start = (bf16[20,3072]{1,0:T(8,128)(2,1)S(1)}, bf16[20,3072]{1,0:T(8,128)(2,1)S(1)}, u32[]{:S(2)}, u32[]{:S(2)}) collective-permute-start(bf16[20,3072]{1,0:T(8,128)(2,1)S(1)} %get-tuple-element.24), channel_id=1, source_target_pairs={{0,1},{1,0},{2,3},{3,2},{4,5},{5,4},{6,7},{7,6},{8,9},{9,8},{10,11... | collective-permute-start | bytes 368648 | tf_op jit(solution)/shard_map/ppermute | solution.py:279
  8.0 0.8 %shard_map.78 = bf16[40,1152]{1,0:T(8,128)(2,1)S(1)} custom-call(bf16[40,3072]{1,0:T(8,128)(2,1)} %refs_0_.5, bf16[40,3072]{1,0:T(8,128)(2,1)} %refs_1_.5, bf16[40,3072]{1,0:T(8,128)(2,1)} %refs_2_.5), custom_call_target="tpu_custom_call" | custom-call | flops 5000000000 | bytes 829440 | tf_op jit(solution)/shard_map/pallas_call | solution.py:36
  8.8 2.7 %collective-permute-start.4 = (bf16[40,1152]{1,0:T(8,128)(2,1)S(1)}, bf16[40,1152]{1,0:T(8,128)(2,1)S(1)}, u32[]{:S(2)}, u32[]{:S(2)}) collective-permute-start(bf16[40,1152]{1,0:T(8,128)(2,1)S(1)} %shard_map.78), channel_id=1, source_target_pairs={{0,16},{2,18},{4,20},{6,22},{8,24},{10,26},{12,28},{14,30},{16,0},... | collective-permute-start | bytes 276488 | tf_op jit(solution)/shard_map/ppermute | solution.py:269
  11.5 1.3 %collective-permute-start.6 = (bf16[40,1152]{1,0:T(8,128)(2,1)S(1)}, bf16[40,1152]{1,0:T(8,128)(2,1)S(1)}, u32[]{:S(2)}, u32[]{:S(2)}) collective-permute-start(bf16[40,1152]{1,0:T(8,128)(2,1)S(1)} %get-tuple-element.30), channel_id=1, source_target_pairs={{0,20},{2,22},{4,16},{6,18},{8,28},{10,30},{12,24},{14,26},{16,4},... | collective-permute-start | bytes 276488 | tf_op jit(solution)/shard_map/ppermute | solution.py:269
  12.8 3.6 %collective-permute-start.8 = (bf16[40,1152]{1,0:T(8,128)(2,1)S(1)}, bf16[40,1152]{1,0:T(8,128)(2,1)S(1)}, u32[]{:S(2)}, u32[]{:S(2)}) collective-permute-start(bf16[40,1152]{1,0:T(8,128)(2,1)S(1)} %get-tuple-element.32), channel_id=1, source_target_pairs={{0,24},{2,26},{4,28},{6,30},{8,16},{10,18},{12,20},{14,22},{16,8},... | collective-permute-start | bytes 276488 | tf_op jit(solution)/shard_map/ppermute | solution.py:269
  16.4 4.0 %collective-permute-done.4.refs_4_ = bf16[40,1152]{1,0:T(8,128)(2,1)S(1)} collective-permute-done((bf16[40,1152]{1,0:T(8,128)(2,1)S(1)}, bf16[40,1152]{1,0:T(8,128)(2,1)S(1)}, u32[]{:S(2)}, u32[]{:S(2)}) %collective-permute-start.4) | collective-permute-done | bytes 92192 | tf_op jit(solution)/shard_map/ppermute | solution.py:269
  20.4 2.9 %collective-permute-done.6.refs_6_ = bf16[40,1152]{1,0:T(8,128)(2,1)S(1)} collective-permute-done((bf16[40,1152]{1,0:T(8,128)(2,1)S(1)}, bf16[40,1152]{1,0:T(8,128)(2,1)S(1)}, u32[]{:S(2)}, u32[]{:S(2)}) %collective-permute-start.6) | collective-permute-done | bytes 92192 | tf_op jit(solution)/shard_map/ppermute | solution.py:269
  23.3 0.5 collective-permute-start.19
  24.0 2.6 %collective-permute-start.5 = (bf16[40,384]{1,0:T(8,128)(2,1)S(1)}, bf16[40,384]{1,0:T(8,128)(2,1)S(1)}, u32[]{:S(2)}, u32[]{:S(2)}) collective-permute-start(bf16[40,384]{1,0:T(8,128)(2,1)S(1)} %get-tuple-element.29), channel_id=1, source_target_pairs={{0,16},{2,18},{4,20},{6,22},{8,24},{10,26},{12,28},{14,30},{16,0},... | collective-permute-start | bytes 92168 | tf_op jit(solution)/shard_map/ppermute | solution.py:269
  26.6 1.0 %collective-permute-start.7 = (bf16[40,384]{1,0:T(8,128)(2,1)S(1)}, bf16[40,384]{1,0:T(8,128)(2,1)S(1)}, u32[]{:S(2)}, u32[]{:S(2)}) collective-permute-start(bf16[40,384]{1,0:T(8,128)(2,1)S(1)} %get-tuple-element.31), channel_id=1, source_target_pairs={{0,20},{2,22},{4,16},{6,18},{8,28},{10,30},{12,24},{14,26},{16,4},... | collective-permute-start | bytes 92168 | tf_op jit(solution)/shard_map/ppermute | solution.py:269
  27.6 1.6 %collective-permute-done.5.refs_5_ = bf16[40,384]{1,0:T(8,128)(2,1)S(1)} collective-permute-done((bf16[40,384]{1,0:T(8,128)(2,1)S(1)}, bf16[40,384]{1,0:T(8,128)(2,1)S(1)}, u32[]{:S(2)}, u32[]{:S(2)}) %collective-permute-start.5) | collective-permute-done | bytes 30752 | tf_op jit(solution)/shard_map/ppermute | solution.py:269
  29.3 4.2 %collective-permute-start.9 = (bf16[40,384]{1,0:T(8,128)(2,1)S(1)}, bf16[40,384]{1,0:T(8,128)(2,1)S(1)}, u32[]{:S(2)}, u32[]{:S(2)}) collective-permute-start(bf16[40,384]{1,0:T(8,128)(2,1)S(1)} %get-tuple-element.33), channel_id=1, source_target_pairs={{0,24},{2,26},{4,28},{6,30},{8,16},{10,18},{12,20},{14,22},{16,8},... | collective-permute-start | bytes 92168 | tf_op jit(solution)/shard_map/ppermute | solution.py:269
  33.4 0.6 collective-permute-start.1
  34.0 1.3 %collective-permute-done.9.refs_9_ = bf16[40,384]{1,0:T(8,128)(2,1)S(1)} collective-permute-done((bf16[40,384]{1,0:T(8,128)(2,1)S(1)}, bf16[40,384]{1,0:T(8,128)(2,1)S(1)}, u32[]{:S(2)}, u32[]{:S(2)}) %collective-permute-start.9) | collective-permute-done | bytes 30752 | tf_op jit(solution)/shard_map/ppermute | solution.py:269
  35.3 2.6 %collective-permute-start.3 = (bf16[40,1536]{1,0:T(8,128)(2,1)S(1)}, bf16[40,1536]{1,0:T(8,128)(2,1)S(1)}, u32[]{:S(2)}, u32[]{:S(2)}) collective-permute-start(bf16[40,1536]{1,0:T(8,128)(2,1)S(1)} %get-tuple-element.28), channel_id=1, source_target_pairs={{0,12},{2,14},{4,8},{6,10},{8,4},{10,6},{12,0},{14,2},{16,28},{18,... | collective-permute-start | bytes 368648 | tf_op jit(solution)/shard_map/ppermute | solution.py:269
  37.9 4.5 %collective-permute-start.10 = (bf16[40,1536]{1,0:T(8,128)(2,1)S(1)}, bf16[40,1536]{1,0:T(8,128)(2,1)S(1)}, u32[]{:S(2)}, u32[]{:S(2)}) collective-permute-start(bf16[40,1536]{1,0:T(8,128)(2,1)S(1)} %get-tuple-element.34), channel_id=1, source_target_pairs={{0,28},{2,30},{4,24},{6,26},{8,20},{10,22},{12,16},{14,18},{16,12}... | collective-permute-start | bytes 368648 | tf_op jit(solution)/shard_map/ppermute | solution.py:269
  42.4 1.2 %collective-permute-done.16.refs_16_ = bf16[40,384]{1,0:T(8,128)(2,1)S(1)} collective-permute-done((bf16[40,384]{1,0:T(8,128)(2,1)S(1)}, bf16[40,384]{1,0:T(8,128)(2,1)S(1)}, u32[]{:S(2)}, u32[]{:S(2)}) %collective-permute-start.16) | collective-permute-done | bytes 30752 | tf_op jit(solution)/shard_map/ppermute | solution.py:269
  43.8 1.0 %collective-permute-done.18.refs_18_ = bf16[40,384]{1,0:T(8,128)(2,1)S(1)} collective-permute-done((bf16[40,384]{1,0:T(8,128)(2,1)S(1)}, bf16[40,384]{1,0:T(8,128)(2,1)S(1)}, u32[]{:S(2)}, u32[]{:S(2)}) %collective-permute-start.18) | collective-permute-done | bytes 30752 | tf_op jit(solution)/shard_map/ppermute | solution.py:269
  45.0 1.0 %collective-permute-done.20.refs_20_ = bf16[40,384]{1,0:T(8,128)(2,1)S(1)} collective-permute-done((bf16[40,384]{1,0:T(8,128)(2,1)S(1)}, bf16[40,384]{1,0:T(8,128)(2,1)S(1)}, u32[]{:S(2)}, u32[]{:S(2)}) %collective-permute-start.20) | collective-permute-done | bytes 30752 | tf_op jit(solution)/shard_map/ppermute | solution.py:269
  48.4 3.9 %shard_map.80 = (bf16[3,40,384]{2,1,0:T(8,128)(2,1)S(1)}, bf16[3,40,384]{2,1,0:T(8,128)(2,1)S(1)}, bf16[3,40,384]{2,1,0:T(8,128)(2,1)S(1)}, bf16[3,40,384]{2,1,0...) custom-call(bf16[40,1536]{1,0:T(8,128)(2,1)S(1)} %get-tuple-element., ...), custom_call_target="tpu_custom_call" | custom-call | flops 524288000 | bytes 2703360 | tf_op jit(solution)/shard_map/pallas_call | solution.py:36
  52.5 3.4 %collective-permute-start.24 = (bf16[3,40,384]{2,1,0:T(8,128)(2,1)S(1)}, bf16[3,40,384]{2,1,0:T(8,128)(2,1)S(1)}, u32[]{:S(2)}, u32[]{:S(2)}) collective-permute-start(bf16[3,40,384]{2,1,0:T(8,128)(2,1)S(1)} %get-tuple-element.38), channel_id=1, source_target_pairs={{0,12},{2,14},{4,8},{6,10},{8,4},{10,6},{12,0},{14,2},{16,28},{18,... | collective-permute-start | bytes 276488 | tf_op jit(solution)/shard_map/ppermute | solution.py:269
  55.9 0.6 collective-permute-start.25
  56.5 1.9 %collective-permute-start.26 = (bf16[3,40,384]{2,1,0:T(8,128)(2,1)S(1)}, bf16[3,40,384]{2,1,0:T(8,128)(2,1)S(1)}, u32[]{:S(2)}, u32[]{:S(2)}) collective-permute-start(bf16[3,40,384]{2,1,0:T(8,128)(2,1)S(1)} %get-tuple-element.40), channel_id=1, source_target_pairs={{0,20},{2,22},{4,16},{6,18},{8,28},{10,30},{12,24},{14,26},{16,4},... | collective-permute-start | bytes 276488 | tf_op jit(solution)/shard_map/ppermute | solution.py:269
  58.4 3.4 %collective-permute-start.27 = (bf16[3,40,384]{2,1,0:T(8,128)(2,1)S(1)}, bf16[3,40,384]{2,1,0:T(8,128)(2,1)S(1)}, u32[]{:S(2)}, u32[]{:S(2)}) collective-permute-start(bf16[3,40,384]{2,1,0:T(8,128)(2,1)S(1)} %get-tuple-element.41), channel_id=1, source_target_pairs={{0,24},{2,26},{4,28},{6,30},{8,16},{10,18},{12,20},{14,22},{16,8},... | collective-permute-start | bytes 276488 | tf_op jit(solution)/shard_map/ppermute | solution.py:269
  61.7 1.8 %collective-permute-start.28 = (bf16[3,40,384]{2,1,0:T(8,128)(2,1)S(1)}, bf16[3,40,384]{2,1,0:T(8,128)(2,1)S(1)}, u32[]{:S(2)}, u32[]{:S(2)}) collective-permute-start(bf16[3,40,384]{2,1,0:T(8,128)(2,1)S(1)} %get-tuple-element.42), channel_id=1, source_target_pairs={{0,28},{2,30},{4,24},{6,26},{8,20},{10,22},{12,16},{14,18},{16,12}... | collective-permute-start | bytes 276488 | tf_op jit(solution)/shard_map/ppermute | solution.py:269
  63.5 6.4 %collective-permute-done.25.refs_4_ = bf16[3,40,384]{2,1,0:T(8,128)(2,1)S(1)} collective-permute-done((bf16[3,40,384]{2,1,0:T(8,128)(2,1)S(1)}, bf16[3,40,384]{2,1,0:T(8,128)(2,1)S(1)}, u32[]{:S(2)}, u32[]{:S(2)}) %collective-permute-start.25) | collective-permute-done | bytes 92192 | tf_op jit(solution)/shard_map/ppermute | solution.py:269
  70.0 1.6 %collective-permute-done.26.refs_5_ = bf16[3,40,384]{2,1,0:T(8,128)(2,1)S(1)} collective-permute-done((bf16[3,40,384]{2,1,0:T(8,128)(2,1)S(1)}, bf16[3,40,384]{2,1,0:T(8,128)(2,1)S(1)}, u32[]{:S(2)}, u32[]{:S(2)}) %collective-permute-start.26) | collective-permute-done | bytes 92192 | tf_op jit(solution)/shard_map/ppermute | solution.py:269
  71.5 0.5 collective-permute-start.32
  74.1 1.0 %shard_map.81 = (bf16[40,3072]{1,0:T(8,128)(2,1)}, bf16[40,3072]{1,0:T(8,128)(2,1)}, bf16[40,3072]{1,0:T(8,128)(2,1)}) custom-call(bf16[3,40,384]{2,1,0:T(8,128)(2,1)S(1)} %get-tuple-element.35.refs_0_, bf16[3,40,384]{2,1,0:T(8,128)(2,1)S(1)} %collective-permute-done.22.refs_1_, bf16[3,40,384]{2,1,0:T(8,128)(2,1)S(1)} %collective-permute-done.23.refs_2_, ...), custom_call_target="tpu_custom_call" | custom-call | bytes 2211840 | tf_op jit(solution)/shard_map/pallas_call | solution.py:36
  (58 shorter events, 5.2 us)
Async XLA Ops:
  4.9 18.9 %collective-permute-start = (bf16[20,3072]{1,0:T(8,128)(2,1)S(1)}, bf16[20,3072]{1,0:T(8,128)(2,1)S(1)}, u32[]{:S(2)}, u32[]{:S(2)}) collective-permute-start(bf16[20,3072]{1,0:T(8,128)(2,1)S(1)} %get-tuple-element.24), channel_id=1, source_target_pairs={{0,1},{1,0},{2,3},{3,2},{4,5},{5,4},{6,7},{7,6},{8,9},{9,8},{10,11... | collective-permute-start | bytes 368648 | tf_op jit(solution)/shard_map/ppermute | solution.py:279
  8.8 11.6 %collective-permute-start.4 = (bf16[40,1152]{1,0:T(8,128)(2,1)S(1)}, bf16[40,1152]{1,0:T(8,128)(2,1)S(1)}, u32[]{:S(2)}, u32[]{:S(2)}) collective-permute-start(bf16[40,1152]{1,0:T(8,128)(2,1)S(1)} %shard_map.78), channel_id=1, source_target_pairs={{0,16},{2,18},{4,20},{6,22},{8,24},{10,26},{12,28},{14,30},{16,0},... | collective-permute-start | bytes 276488 | tf_op jit(solution)/shard_map/ppermute | solution.py:269
  11.5 11.8 %collective-permute-start.6 = (bf16[40,1152]{1,0:T(8,128)(2,1)S(1)}, bf16[40,1152]{1,0:T(8,128)(2,1)S(1)}, u32[]{:S(2)}, u32[]{:S(2)}) collective-permute-start(bf16[40,1152]{1,0:T(8,128)(2,1)S(1)} %get-tuple-element.30), channel_id=1, source_target_pairs={{0,20},{2,22},{4,16},{6,18},{8,28},{10,30},{12,24},{14,26},{16,4},... | collective-permute-start | bytes 276488 | tf_op jit(solution)/shard_map/ppermute | solution.py:269
  12.8 10.5 %collective-permute-start.8 = (bf16[40,1152]{1,0:T(8,128)(2,1)S(1)}, bf16[40,1152]{1,0:T(8,128)(2,1)S(1)}, u32[]{:S(2)}, u32[]{:S(2)}) collective-permute-start(bf16[40,1152]{1,0:T(8,128)(2,1)S(1)} %get-tuple-element.32), channel_id=1, source_target_pairs={{0,24},{2,26},{4,28},{6,30},{8,16},{10,18},{12,20},{14,22},{16,8},... | collective-permute-start | bytes 276488 | tf_op jit(solution)/shard_map/ppermute | solution.py:269
  20.4 14.9 %collective-permute-start.15 = (bf16[40,1152]{1,0:T(8,128)(2,1)S(1)}, bf16[40,1152]{1,0:T(8,128)(2,1)S(1)}, u32[]{:S(2)}, u32[]{:S(2)}) collective-permute-start(bf16[40,1152]{1,0:T(8,128)(2,1)S(1)} %collective-permute-done.4.refs_4_), channel_id=1, source_target_pairs={{0,2},{2,0},{4,6},{6,4},{8,10},{10,8},{12,14},{14,12},{16,18},{18,... | collective-permute-start | bytes 276488 | tf_op jit(solution)/shard_map/ppermute | solution.py:269
  23.3 14.6 %collective-permute-start.17 = (bf16[40,1152]{1,0:T(8,128)(2,1)S(1)}, bf16[40,1152]{1,0:T(8,128)(2,1)S(1)}, u32[]{:S(2)}, u32[]{:S(2)}) collective-permute-start(bf16[40,1152]{1,0:T(8,128)(2,1)S(1)} %collective-permute-done.6.refs_6_), channel_id=1, source_target_pairs={{0,2},{2,0},{4,6},{6,4},{8,10},{10,8},{12,14},{14,12},{16,18},{18,... | collective-permute-start | bytes 276488 | tf_op jit(solution)/shard_map/ppermute | solution.py:269
  23.3 19.1 %collective-permute-start.19 = (bf16[40,1152]{1,0:T(8,128)(2,1)S(1)}, bf16[40,1152]{1,0:T(8,128)(2,1)S(1)}, u32[]{:S(2)}, u32[]{:S(2)}) collective-permute-start(bf16[40,1152]{1,0:T(8,128)(2,1)S(1)} %collective-permute-done.8.refs_8_), channel_id=1, source_target_pairs={{0,2},{2,0},{4,6},{6,4},{8,10},{10,8},{12,14},{14,12},{16,18},{18,... | collective-permute-start | bytes 276488 | tf_op jit(solution)/shard_map/ppermute | solution.py:269
  24.0 5.3 %collective-permute-start.5 = (bf16[40,384]{1,0:T(8,128)(2,1)S(1)}, bf16[40,384]{1,0:T(8,128)(2,1)S(1)}, u32[]{:S(2)}, u32[]{:S(2)}) collective-permute-start(bf16[40,384]{1,0:T(8,128)(2,1)S(1)} %get-tuple-element.29), channel_id=1, source_target_pairs={{0,16},{2,18},{4,20},{6,22},{8,24},{10,26},{12,28},{14,30},{16,0},... | collective-permute-start | bytes 92168 | tf_op jit(solution)/shard_map/ppermute | solution.py:269
  26.6 6.9 %collective-permute-start.7 = (bf16[40,384]{1,0:T(8,128)(2,1)S(1)}, bf16[40,384]{1,0:T(8,128)(2,1)S(1)}, u32[]{:S(2)}, u32[]{:S(2)}) collective-permute-start(bf16[40,384]{1,0:T(8,128)(2,1)S(1)} %get-tuple-element.31), channel_id=1, source_target_pairs={{0,20},{2,22},{4,16},{6,18},{8,28},{10,30},{12,24},{14,26},{16,4},... | collective-permute-start | bytes 92168 | tf_op jit(solution)/shard_map/ppermute | solution.py:269
  29.3 6.0 %collective-permute-start.9 = (bf16[40,384]{1,0:T(8,128)(2,1)S(1)}, bf16[40,384]{1,0:T(8,128)(2,1)S(1)}, u32[]{:S(2)}, u32[]{:S(2)}) collective-permute-start(bf16[40,384]{1,0:T(8,128)(2,1)S(1)} %get-tuple-element.33), channel_id=1, source_target_pairs={{0,24},{2,26},{4,28},{6,30},{8,16},{10,18},{12,20},{14,22},{16,8},... | collective-permute-start | bytes 92168 | tf_op jit(solution)/shard_map/ppermute | solution.py:269
  33.4 12.7 %collective-permute-start.1 = (bf16[40,1536]{1,0:T(8,128)(2,1)S(1)}, bf16[40,1536]{1,0:T(8,128)(2,1)S(1)}, u32[]{:S(2)}, u32[]{:S(2)}) collective-permute-start(bf16[40,1536]{1,0:T(8,128)(2,1)S(1)} %get-tuple-element.26), channel_id=1, source_target_pairs={{0,4},{2,6},{4,0},{6,2},{8,12},{10,14},{12,8},{14,10},{16,20},{18,... | collective-permute-start | bytes 368648 | tf_op jit(solution)/shard_map/ppermute | solution.py:269
  35.3 11.2 %collective-permute-start.2 = (bf16[40,1536]{1,0:T(8,128)(2,1)S(1)}, bf16[40,1536]{1,0:T(8,128)(2,1)S(1)}, u32[]{:S(2)}, u32[]{:S(2)}) collective-permute-start(bf16[40,1536]{1,0:T(8,128)(2,1)S(1)} %get-tuple-element.27), channel_id=1, source_target_pairs={{0,8},{2,10},{4,12},{6,14},{8,0},{10,2},{12,4},{14,6},{16,24},{18,... | collective-permute-start | bytes 368648 | tf_op jit(solution)/shard_map/ppermute | solution.py:269
  35.3 11.4 %collective-permute-start.3 = (bf16[40,1536]{1,0:T(8,128)(2,1)S(1)}, bf16[40,1536]{1,0:T(8,128)(2,1)S(1)}, u32[]{:S(2)}, u32[]{:S(2)}) collective-permute-start(bf16[40,1536]{1,0:T(8,128)(2,1)S(1)} %get-tuple-element.28), channel_id=1, source_target_pairs={{0,12},{2,14},{4,8},{6,10},{8,4},{10,6},{12,0},{14,2},{16,28},{18,... | collective-permute-start | bytes 368648 | tf_op jit(solution)/shard_map/ppermute | solution.py:269
  37.9 9.1 %collective-permute-start.10 = (bf16[40,1536]{1,0:T(8,128)(2,1)S(1)}, bf16[40,1536]{1,0:T(8,128)(2,1)S(1)}, u32[]{:S(2)}, u32[]{:S(2)}) collective-permute-start(bf16[40,1536]{1,0:T(8,128)(2,1)S(1)} %get-tuple-element.34), channel_id=1, source_target_pairs={{0,28},{2,30},{4,24},{6,26},{8,20},{10,22},{12,16},{14,18},{16,12}... | collective-permute-start | bytes 368648 | tf_op jit(solution)/shard_map/ppermute | solution.py:269
  46.0 1.3 %collective-permute-start.11 = (bf16[40,1536]{1,0:T(8,128)(2,1)S(1)}, bf16[40,1536]{1,0:T(8,128)(2,1)S(1)}, u32[]{:S(2)}, u32[]{:S(2)}) collective-permute-start(bf16[40,1536]{1,0:T(8,128)(2,1)S(1)} %get-tuple-element.25.refs_0_), channel_id=1, source_target_pairs={{0,2},{2,0},{4,6},{6,4},{8,10},{10,8},{12,14},{14,12},{16,18},{18,... | collective-permute-start | bytes 368648 | tf_op jit(solution)/shard_map/ppermute | solution.py:269
  46.2 1.3 %collective-permute-start.12 = (bf16[40,1536]{1,0:T(8,128)(2,1)S(1)}, bf16[40,1536]{1,0:T(8,128)(2,1)S(1)}, u32[]{:S(2)}, u32[]{:S(2)}) collective-permute-start(bf16[40,1536]{1,0:T(8,128)(2,1)S(1)} %collective-permute-done.1.refs_1_), channel_id=1, source_target_pairs={{0,2},{2,0},{4,6},{6,4},{8,10},{10,8},{12,14},{14,12},{16,18},{18,... | collective-permute-start | bytes 368648 | tf_op jit(solution)/shard_map/ppermute | solution.py:269
  46.5 1.3 %collective-permute-start.13 = (bf16[40,1536]{1,0:T(8,128)(2,1)S(1)}, bf16[40,1536]{1,0:T(8,128)(2,1)S(1)}, u32[]{:S(2)}, u32[]{:S(2)}) collective-permute-start(bf16[40,1536]{1,0:T(8,128)(2,1)S(1)} %collective-permute-done.2.refs_2_), channel_id=1, source_target_pairs={{0,2},{2,0},{4,6},{6,4},{8,10},{10,8},{12,14},{14,12},{16,18},{18,... | collective-permute-start | bytes 368648 | tf_op jit(solution)/shard_map/ppermute | solution.py:269
  46.7 1.3 %collective-permute-start.14 = (bf16[40,1536]{1,0:T(8,128)(2,1)S(1)}, bf16[40,1536]{1,0:T(8,128)(2,1)S(1)}, u32[]{:S(2)}, u32[]{:S(2)}) collective-permute-start(bf16[40,1536]{1,0:T(8,128)(2,1)S(1)} %collective-permute-done.3.refs_3_), channel_id=1, source_target_pairs={{0,2},{2,0},{4,6},{6,4},{8,10},{10,8},{12,14},{14,12},{16,18},{18,... | collective-permute-start | bytes 368648 | tf_op jit(solution)/shard_map/ppermute | solution.py:269
  47.0 1.3 %collective-permute-start.21 = (bf16[40,1536]{1,0:T(8,128)(2,1)S(1)}, bf16[40,1536]{1,0:T(8,128)(2,1)S(1)}, u32[]{:S(2)}, u32[]{:S(2)}) collective-permute-start(bf16[40,1536]{1,0:T(8,128)(2,1)S(1)} %collective-permute-done.10.refs_10_), channel_id=1, source_target_pairs={{0,2},{2,0},{4,6},{6,4},{8,10},{10,8},{12,14},{14,12},{16,18},{18,... | collective-permute-start | bytes 368648 | tf_op jit(solution)/shard_map/ppermute | solution.py:269
  52.3 6.0 %collective-permute-start.22 = (bf16[3,40,384]{2,1,0:T(8,128)(2,1)S(1)}, bf16[3,40,384]{2,1,0:T(8,128)(2,1)S(1)}, u32[]{:S(2)}, u32[]{:S(2)}) collective-permute-start(bf16[3,40,384]{2,1,0:T(8,128)(2,1)S(1)} %get-tuple-element.36), channel_id=1, source_target_pairs={{0,4},{2,6},{4,0},{6,2},{8,12},{10,14},{12,8},{14,10},{16,20},{18,... | collective-permute-start | bytes 276488 | tf_op jit(solution)/shard_map/ppermute | solution.py:269
  52.5 9.2 %collective-permute-start.23 = (bf16[3,40,384]{2,1,0:T(8,128)(2,1)S(1)}, bf16[3,40,384]{2,1,0:T(8,128)(2,1)S(1)}, u32[]{:S(2)}, u32[]{:S(2)}) collective-permute-start(bf16[3,40,384]{2,1,0:T(8,128)(2,1)S(1)} %get-tuple-element.37), channel_id=1, source_target_pairs={{0,8},{2,10},{4,12},{6,14},{8,0},{10,2},{12,4},{14,6},{16,24},{18,... | collective-permute-start | bytes 276488 | tf_op jit(solution)/shard_map/ppermute | solution.py:269
  52.5 11.0 %collective-permute-start.24 = (bf16[3,40,384]{2,1,0:T(8,128)(2,1)S(1)}, bf16[3,40,384]{2,1,0:T(8,128)(2,1)S(1)}, u32[]{:S(2)}, u32[]{:S(2)}) collective-permute-start(bf16[3,40,384]{2,1,0:T(8,128)(2,1)S(1)} %get-tuple-element.38), channel_id=1, source_target_pairs={{0,12},{2,14},{4,8},{6,10},{8,4},{10,6},{12,0},{14,2},{16,28},{18,... | collective-permute-start | bytes 276488 | tf_op jit(solution)/shard_map/ppermute | solution.py:269
  55.9 14.1 %collective-permute-start.25 = (bf16[3,40,384]{2,1,0:T(8,128)(2,1)S(1)}, bf16[3,40,384]{2,1,0:T(8,128)(2,1)S(1)}, u32[]{:S(2)}, u32[]{:S(2)}) collective-permute-start(bf16[3,40,384]{2,1,0:T(8,128)(2,1)S(1)} %get-tuple-element.39), channel_id=1, source_target_pairs={{0,16},{2,18},{4,20},{6,22},{8,24},{10,26},{12,28},{14,30},{16,0},... | collective-permute-start | bytes 276488 | tf_op jit(solution)/shard_map/ppermute | solution.py:269
  56.5 15.1 %collective-permute-start.26 = (bf16[3,40,384]{2,1,0:T(8,128)(2,1)S(1)}, bf16[3,40,384]{2,1,0:T(8,128)(2,1)S(1)}, u32[]{:S(2)}, u32[]{:S(2)}) collective-permute-start(bf16[3,40,384]{2,1,0:T(8,128)(2,1)S(1)} %get-tuple-element.40), channel_id=1, source_target_pairs={{0,20},{2,22},{4,16},{6,18},{8,28},{10,30},{12,24},{14,26},{16,4},... | collective-permute-start | bytes 276488 | tf_op jit(solution)/shard_map/ppermute | solution.py:269
  58.4 13.2 %collective-permute-start.27 = (bf16[3,40,384]{2,1,0:T(8,128)(2,1)S(1)}, bf16[3,40,384]{2,1,0:T(8,128)(2,1)S(1)}, u32[]{:S(2)}, u32[]{:S(2)}) collective-permute-start(bf16[3,40,384]{2,1,0:T(8,128)(2,1)S(1)} %get-tuple-element.41), channel_id=1, source_target_pairs={{0,24},{2,26},{4,28},{6,30},{8,16},{10,18},{12,20},{14,22},{16,8},... | collective-permute-start | bytes 276488 | tf_op jit(solution)/shard_map/ppermute | solution.py:269
  61.7 10.3 %collective-permute-start.28 = (bf16[3,40,384]{2,1,0:T(8,128)(2,1)S(1)}, bf16[3,40,384]{2,1,0:T(8,128)(2,1)S(1)}, u32[]{:S(2)}, u32[]{:S(2)}) collective-permute-start(bf16[3,40,384]{2,1,0:T(8,128)(2,1)S(1)} %get-tuple-element.42), channel_id=1, source_target_pairs={{0,28},{2,30},{4,24},{6,26},{8,20},{10,22},{12,16},{14,18},{16,12}... | collective-permute-start | bytes 276488 | tf_op jit(solution)/shard_map/ppermute | solution.py:269
  63.5 8.6 %collective-permute-start.29 = (bf16[3,40,384]{2,1,0:T(8,128)(2,1)S(1)}, bf16[3,40,384]{2,1,0:T(8,128)(2,1)S(1)}, u32[]{:S(2)}, u32[]{:S(2)}) collective-permute-start(bf16[3,40,384]{2,1,0:T(8,128)(2,1)S(1)} %get-tuple-element.35.refs_0_), channel_id=1, source_target_pairs={{0,2},{2,0},{4,6},{6,4},{8,10},{10,8},{12,14},{14,12},{16,18},{18,... | collective-permute-start | bytes 276488 | tf_op jit(solution)/shard_map/ppermute | solution.py:269
  70.0 2.6 %collective-permute-start.30 = (bf16[3,40,384]{2,1,0:T(8,128)(2,1)S(1)}, bf16[3,40,384]{2,1,0:T(8,128)(2,1)S(1)}, u32[]{:S(2)}, u32[]{:S(2)}) collective-permute-start(bf16[3,40,384]{2,1,0:T(8,128)(2,1)S(1)} %collective-permute-done.22.refs_1_), channel_id=1, source_target_pairs={{0,2},{2,0},{4,6},{6,4},{8,10},{10,8},{12,14},{14,12},{16,18},{18,... | collective-permute-start | bytes 276488 | tf_op jit(solution)/shard_map/ppermute | solution.py:269
  71.5 1.5 %collective-permute-start.32 = (bf16[3,40,384]{2,1,0:T(8,128)(2,1)S(1)}, bf16[3,40,384]{2,1,0:T(8,128)(2,1)S(1)}, u32[]{:S(2)}, u32[]{:S(2)}) collective-permute-start(bf16[3,40,384]{2,1,0:T(8,128)(2,1)S(1)} %collective-permute-done.24.refs_3_), channel_id=1, source_target_pairs={{0,2},{2,0},{4,6},{6,4},{8,10},{10,8},{12,14},{14,12},{16,18},{18,... | collective-permute-start | bytes 276488 | tf_op jit(solution)/shard_map/ppermute | solution.py:269
  72.1 1.3 %collective-permute-start.33 = (bf16[3,40,384]{2,1,0:T(8,128)(2,1)S(1)}, bf16[3,40,384]{2,1,0:T(8,128)(2,1)S(1)}, u32[]{:S(2)}, u32[]{:S(2)}) collective-permute-start(bf16[3,40,384]{2,1,0:T(8,128)(2,1)S(1)} %collective-permute-done.25.refs_4_), channel_id=1, source_target_pairs={{0,2},{2,0},{4,6},{6,4},{8,10},{10,8},{12,14},{14,12},{16,18},{18,... | collective-permute-start | bytes 276488 | tf_op jit(solution)/shard_map/ppermute | solution.py:269
  72.1 1.4 %collective-permute-start.34 = (bf16[3,40,384]{2,1,0:T(8,128)(2,1)S(1)}, bf16[3,40,384]{2,1,0:T(8,128)(2,1)S(1)}, u32[]{:S(2)}, u32[]{:S(2)}) collective-permute-start(bf16[3,40,384]{2,1,0:T(8,128)(2,1)S(1)} %collective-permute-done.26.refs_5_), channel_id=1, source_target_pairs={{0,2},{2,0},{4,6},{6,4},{8,10},{10,8},{12,14},{14,12},{16,18},{18,... | collective-permute-start | bytes 276488 | tf_op jit(solution)/shard_map/ppermute | solution.py:269
  72.6 1.3 %collective-permute-start.35 = (bf16[3,40,384]{2,1,0:T(8,128)(2,1)S(1)}, bf16[3,40,384]{2,1,0:T(8,128)(2,1)S(1)}, u32[]{:S(2)}, u32[]{:S(2)}) collective-permute-start(bf16[3,40,384]{2,1,0:T(8,128)(2,1)S(1)} %collective-permute-done.27.refs_6_), channel_id=1, source_target_pairs={{0,2},{2,0},{4,6},{6,4},{8,10},{10,8},{12,14},{14,12},{16,18},{18,... | collective-permute-start | bytes 276488 | tf_op jit(solution)/shard_map/ppermute | solution.py:269
  (10 other events, 28.9 us)

commit v4 on v3

--- a/solution.py
+++ b/solution.py
@@ -10,7 +10,6 @@
 
 HD = 128
 PATCH = 8
-TILE = 320
 ROOM = 24 << 20
 
 
@@ -149,7 +148,9 @@
 def attend(own, other, rows):
     chips = len(own)
     total = 2 * chips * rows
+    part = chips // 2 * rows
     scaling = 1.0 / math.sqrt(HD)
+    grade = scaling * math.log2(math.e)
     operands = [block for part in (own, other) for blocks in part for block in blocks]
     inputs = len(operands)
 
@@ -159,7 +160,7 @@
             [[next(taken) for _ in blocks] for blocks in part] for part in (own, other)
         )
         outs = refs[inputs : inputs + chips]
-        gathered, query_sum, key_sum, value_sum = refs[inputs + chips :]
+        gathered, query_sum, key_sum, value_sum, hidden = refs[inputs + chips :]
         chip, core, _ = where_am_i()
 
         def piece(blocks, which, head):
@@ -169,14 +170,25 @@
             return blocks[0][:, pl.ds(pl.multiple_of(at * HD, HD), HD)].astype(jnp.float32)
 
         def spots(step):
-            start = (chip ^ step) * (2 * rows)
+            late = jnp.where((chip ^ step) >= chips // 2, 1, 0)
+            start = late * (2 * part) + ((chip ^ step) - late * (chips // 2)) * rows
             return (
-                pl.ds(pl.multiple_of(start + core * rows, 8), rows),
-                pl.ds(pl.multiple_of(start + (1 - core) * rows, 8), rows),
+                pl.ds(pl.multiple_of(start, 8), rows),
+                pl.ds(pl.multiple_of(start + part, 8), rows),
             )
 
-        for index in range(2):
-            head = core + index
+        def place(shape, axis):
+            at = lax.broadcasted_iota(jnp.int32, shape, axis).astype(jnp.float32)
+            others = jnp.where(at < part, 0.0, 1.0)
+            inside = at - others * part
+            which = jnp.floor((inside + 0.5) * (1.0 / rows))
+            side = jnp.abs(others - jnp.where(core == 1, 1.0, 0.0))
+            return which * (2 * rows) + side * rows + (inside - which * rows)
+
+        square = hidden.shape
+        hidden[...] = jnp.where(place(square, 0) <= place(square, 1), 0.0, lowest)
+        last, first, plain = ((((x,), (y,)), ((), ())) for x, y in ((1, 1), (0, 0), (1, 0)))
+        for head in range(3):
             for which in range(4):
                 for step in range(chips):
                     mine, others = spots(step)
@@ -185,79 +197,66 @@
             query, keys, values, grads = (
                 gathered[which].astype(jnp.bfloat16) for which in range(4)
             )
-            for low in range(0, total, TILE):
-                high = min(low + TILE, total)
+            for low in range(0, total, 2 * part):
+                high = low + 2 * part
                 q, g = query[low:high], grads[low:high]
                 k, v = keys[:high], values[:high]
-                last = (((1,), (1,)), ((), ()))
-                first = (((0,), (0,)), ((), ()))
-                scores = scaling * lax.dot_general(q, k, last, preferred_element_type=jnp.float32)
-                row = lax.broadcasted_iota(jnp.int32, scores.shape, 0) + low
-                col = lax.broadcasted_iota(jnp.int32, scores.shape, 1)
-                scores = jnp.where(col <= row, scores, lowest)
-                expo = jnp.exp(scores - jnp.max(scores, axis=1, keepdims=True))
-                products = lax.dot_general(g, v, last, preferred_element_type=jnp.float32)
-                scale = 1.0 / jnp.sum(expo, axis=1, keepdims=True)
-                delta = jnp.sum(expo * products, axis=1, keepdims=True) * scale
+                scores = lax.dot_general(k, q, last, preferred_element_type=jnp.float32)
+                below = scores[low:] + hidden[...]
+                scores = jnp.concatenate([scores[:low], below]) if low else below
+                expo = jnp.exp2((scores - jnp.max(scores, axis=0, keepdims=True)) * grade)
+                products = lax.dot_general(v, g, last, preferred_element_type=jnp.float32)
+                scale = 1.0 / jnp.sum(expo, axis=0, keepdims=True)
+                delta = jnp.sum(expo * products, axis=0, keepdims=True) * scale
                 weights = expo * scale
                 score_grad = (weights * (products - delta)).astype(jnp.bfloat16)
                 half = weights.astype(jnp.bfloat16)
-                query_sum[low:high] = lax.dot_general(
-                    score_grad, k, (((1,), (0,)), ((), ())), preferred_element_type=jnp.float32
+                query_sum[low : low + part] = lax.dot_general(
+                    score_grad[:, :part], k, first, preferred_element_type=jnp.float32
                 )
-                key_part = lax.dot_general(score_grad, q, first, preferred_element_type=jnp.float32)
-                value_part = lax.dot_general(half, g, first, preferred_element_type=jnp.float32)
-                if low:
-                    key_sum[:low] += key_part[:low]
-                    value_sum[:low] += value_part[:low]
-                key_sum[low:high] = key_part[low:]
-                value_sum[low:high] = value_part[low:]
+                for start in range(0, high, 2 * part):
+                    mine = slice(start, start + part)
+                    for store, left, right in ((key_sum, score_grad, q), (value_sum, half, g)):
+                        added = lax.dot_general(
+                            left[mine], right, plain, preferred_element_type=jnp.float32
+                        )
+                        store[mine] = added if start == low else store[mine] + added
             for which, (store, factor) in enumerate(
                 ((query_sum, scaling), (key_sum, scaling), (value_sum, 1.0))
             ):
-                lanes = slice(which * HD, (which + 1) * HD)
+                at = (which * 3 + head) * HD
                 for step in range(chips):
-                    mine, others = spots(step)
-
-                    def rounded(spot):
-                        return (store[spot] * factor).astype(jnp.bfloat16)
-
-                    outs[step][pl.ds(jnp.where(head == 1, 1, 0), 1), :, lanes] = rounded(mine)[None]
-
-                    @pl.when(head != 1)
-                    def _():
-                        outs[step][2, :, lanes] = rounded(others)
+                    outs[step][:, at : at + HD] = (store[spots(step)[0]] * factor).astype(jnp.bfloat16)
 
     big = pltpu.VMEM((total, HD), jnp.float32)
     return local(
         kernel,
         operands,
-        [(3, rows, 3 * HD)] * chips,
-        [pltpu.VMEM((4, total, HD), jnp.float32), big, big, big],
+        [(rows, 9 * HD)] * chips,
+        [
+            pltpu.VMEM((4, total, HD), jnp.float32),
+            big,
+            big,
+            big,
+            pltpu.VMEM((2 * part, 2 * part), jnp.float32),
+        ],
         10 * total * total * HD,
     )
 
 
-def unpack(own, other, rows, columns):
-    chips = len(own)
+def unpack(blocks, rows, columns):
+    chips = len(blocks)
     wide = columns // chips
 
     def kernel(*refs):
-        own_refs, other_refs, outs = refs[:chips], refs[chips : 2 * chips], refs[2 * chips :]
-        chip, core, _ = where_am_i()
-        for step in range(chips):
-            start = (chip ^ step) * wide
+        ins, outs = refs[:chips], refs[chips:]
+        chip = where_am_i()[0]
+        for step, ref in enumerate(ins):
+            lanes = pl.ds(pl.multiple_of((chip ^ step) * wide, HD), wide)
             for which, out in enumerate(outs):
-                lanes = slice(which * HD, (which + 1) * HD)
-
-                def put(head, block):
-                    out[:, pl.ds(pl.multiple_of(start + head * HD, HD), HD)] = block
-
-                put(2 * core, own_refs[step][0, :, lanes])
-                put(1, own_refs[step][1, :, lanes])
-                put(2 - 2 * core, other_refs[step][2, :, lanes])
-
-    return local(kernel, [*own, *other], [(rows, columns)] * 3, final=True)
+                out[:, lanes] = ref[:, which * wide : (which + 1) * wide]
+
+    return local(kernel, blocks, [(rows, columns)] * 3, final=True)
 
 
 def by_heads(query_rows, key_rows, value_rows, mid_grad, link_weight):
@@ -287,8 +286,7 @@
     other = [[cross(block, 1) for block in blocks] for blocks in own]
     done = attend(own, other, rows)
     own = [done[0]] + [cross(done[step], 2 * step) for step in range(1, chips)]
-    other = [cross(block, 1) for block in own]
-    return tuple(unpack(own, other, rows, columns))
+    return tuple(unpack(own, rows, columns))
 
 
 def on_device(query_rows, key_rows, value_rows, mid_grad, link_weight):
@@ -300,7 +298,8 @@
         and size & (size - 1) == 0
         and lax.axis_size("narrow") == 2
         and columns == chips * 3 * HD
-        and (size * rows) % TILE == 0
+        and chips > 1
+        and (chips // 2 * rows) % 16 == 0
         and rows % 8 == 0
     )
     plan = by_heads if fits else by_rows

time: 76.3 us -> 74.3 us (0.974)
  starting transfers between devices: 40.7 us -> 39.3 us
  waiting for transfers between devices: 23.5 us -> 22.3 us
    ppermute x36 -> x28, starting transfers between devices: 37.6 us -> 36.3 us  [cross(): lax.ppermute(block, 'wide', [(i, i ^ step) for i in range(size)])]
    ppermute x36 -> x28, waiting for transfers between devices: 23.5 us -> 22.3 us  [cross(): lax.ppermute(block, 'wide', [(i, i ^ step) for i in range(size)])]
  transfers between devices with their start and end apart: 37 -> 29, of which waited for: 19 -> 14; matrix products, arithmetic and copies ran while one was open for 0% -> 0% of each run, Pallas kernels for 1% -> 1%
where the time goes in v4:
time: 74.3 us; the launch traced here: 73.1 us
  starting transfers between devices  39.3 us (53%)
  waiting for transfers between devices  22.3 us (30%)
  Pallas kernels  7.74 us (10%)
  local copies, waits for them, and re-layouts  2.99 us (4%)
    ppermute x28, starting transfers between devices, cross(): lax.ppermute(block, 'wide', [(i, i ^ step) for i in range(size)])  36.3 us
    ppermute x28, waiting for transfers between devices, cross(): lax.ppermute(block, 'wide', [(i, i ^ step) for i in range(size)])  22.3 us
    pallas_call x6, Pallas kernels, local(): pl.pallas_call(kernel, in_specs=[anywhere if i in afar else vmem for i in...  7.74 us
    ppermute x1, starting transfers between devices, by_heads(): came = held(lax.ppermute(leave, 'narrow', [(0, 1), (1, 0)]))  3.06 us
    unnamed x10, local copies, waits for them, and re-layouts  2.99 us
  transfers between devices with their start and end apart: 29, of which 14 were waited for; matrix products, arithmetic and copies ran while one was open for 0% of the time, Pallas kernels for 1%

profile of v4, /device:TPU:0, one launch (start us, length us, event | category | flops | bytes accessed | tf_op | source)
XLA Modules:
  0.0 73.1 jit_solution(3275195889380492478)
XLA Ops:
  0.6 1.9 %copy-done = bf16[768,2048]{1,0:T(8,128)(2,1)S(1)} copy-done((bf16[768,2048]{1,0:T(8,128)(2,1)S(1)}, bf16[768,2048]{1,0:T(8,128)(2,1)}, u32[]{:S(2)}) %copy-start) | copy-done | bytes 3145752
  2.5 1.1 %copy-done.4 = bf16[160,2048]{1,0:T(8,128)(2,1)S(1)} copy-done((bf16[160,2048]{1,0:T(8,128)(2,1)S(1)}, bf16[160,2048]{1,0:T(8,128)(2,1)}, u32[]{:S(2)}) %copy-start.4) | copy-done | bytes 655384
  3.6 1.3 %shard_map.76 = (bf16[20,3072]{1,0:T(8,128)(2,1)S(1)}, bf16[20,3072]{1,0:T(8,128)(2,1)S(1)}) custom-call(bf16[160,2048]{1,0:T(8,128)(2,1)S(1)} %copy-done.4, bf16[768,2048]{1,0:T(8,128)(2,1)S(1)} %copy-done), custom_call_target="tpu_custom_call" | custom-call | flops 503316480 | bytes 4046848 | tf_op jit(solution)/shard_map/pallas_call | solution.py:35
  4.9 3.1 %collective-permute-start = (bf16[20,3072]{1,0:T(8,128)(2,1)S(1)}, bf16[20,3072]{1,0:T(8,128)(2,1)S(1)}, u32[]{:S(2)}, u32[]{:S(2)}) collective-permute-start(bf16[20,3072]{1,0:T(8,128)(2,1)S(1)} %get-tuple-element.24), channel_id=1, source_target_pairs={{0,1},{1,0},{2,3},{3,2},{4,5},{5,4},{6,7},{7,6},{8,9},{9,8},{10,11... | collective-permute-start | bytes 368648 | tf_op jit(solution)/shard_map/ppermute | solution.py:278
  8.0 0.8 %shard_map.78 = bf16[40,1152]{1,0:T(8,128)(2,1)S(1)} custom-call(bf16[40,3072]{1,0:T(8,128)(2,1)} %refs_0_.5, bf16[40,3072]{1,0:T(8,128)(2,1)} %refs_1_.5, bf16[40,3072]{1,0:T(8,128)(2,1)} %refs_2_.5), custom_call_target="tpu_custom_call" | custom-call | flops 5000000000 | bytes 829440 | tf_op jit(solution)/shard_map/pallas_call | solution.py:35
  8.8 2.7 %collective-permute-start.4 = (bf16[40,1152]{1,0:T(8,128)(2,1)S(1)}, bf16[40,1152]{1,0:T(8,128)(2,1)S(1)}, u32[]{:S(2)}, u32[]{:S(2)}) collective-permute-start(bf16[40,1152]{1,0:T(8,128)(2,1)S(1)} %shard_map.78), channel_id=1, source_target_pairs={{0,16},{2,18},{4,20},{6,22},{8,24},{10,26},{12,28},{14,30},{16,0},... | collective-permute-start | bytes 276488 | tf_op jit(solution)/shard_map/ppermute | solution.py:268
  11.5 1.3 %collective-permute-start.6 = (bf16[40,1152]{1,0:T(8,128)(2,1)S(1)}, bf16[40,1152]{1,0:T(8,128)(2,1)S(1)}, u32[]{:S(2)}, u32[]{:S(2)}) collective-permute-start(bf16[40,1152]{1,0:T(8,128)(2,1)S(1)} %get-tuple-element.30), channel_id=1, source_target_pairs={{0,20},{2,22},{4,16},{6,18},{8,28},{10,30},{12,24},{14,26},{16,4},... | collective-permute-start | bytes 276488 | tf_op jit(solution)/shard_map/ppermute | solution.py:268
  12.8 3.6 %collective-permute-start.8 = (bf16[40,1152]{1,0:T(8,128)(2,1)S(1)}, bf16[40,1152]{1,0:T(8,128)(2,1)S(1)}, u32[]{:S(2)}, u32[]{:S(2)}) collective-permute-start(bf16[40,1152]{1,0:T(8,128)(2,1)S(1)} %get-tuple-element.32), channel_id=1, source_target_pairs={{0,24},{2,26},{4,28},{6,30},{8,16},{10,18},{12,20},{14,22},{16,8},... | collective-permute-start | bytes 276488 | tf_op jit(solution)/shard_map/ppermute | solution.py:268
  16.4 4.0 %collective-permute-done.4.refs_4_ = bf16[40,1152]{1,0:T(8,128)(2,1)S(1)} collective-permute-done((bf16[40,1152]{1,0:T(8,128)(2,1)S(1)}, bf16[40,1152]{1,0:T(8,128)(2,1)S(1)}, u32[]{:S(2)}, u32[]{:S(2)}) %collective-permute-start.4) | collective-permute-done | bytes 92192 | tf_op jit(solution)/shard_map/ppermute | solution.py:268
  20.4 2.9 %collective-permute-done.6.refs_6_ = bf16[40,1152]{1,0:T(8,128)(2,1)S(1)} collective-permute-done((bf16[40,1152]{1,0:T(8,128)(2,1)S(1)}, bf16[40,1152]{1,0:T(8,128)(2,1)S(1)}, u32[]{:S(2)}, u32[]{:S(2)}) %collective-permute-start.6) | collective-permute-done | bytes 92192 | tf_op jit(solution)/shard_map/ppermute | solution.py:268
  23.3 0.5 collective-permute-start.19
  24.0 2.6 %collective-permute-start.5 = (bf16[40,384]{1,0:T(8,128)(2,1)S(1)}, bf16[40,384]{1,0:T(8,128)(2,1)S(1)}, u32[]{:S(2)}, u32[]{:S(2)}) collective-permute-start(bf16[40,384]{1,0:T(8,128)(2,1)S(1)} %get-tuple-element.29), channel_id=1, source_target_pairs={{0,16},{2,18},{4,20},{6,22},{8,24},{10,26},{12,28},{14,30},{16,0},... | collective-permute-start | bytes 92168 | tf_op jit(solution)/shard_map/ppermute | solution.py:268
  26.6 1.0 %collective-permute-start.7 = (bf16[40,384]{1,0:T(8,128)(2,1)S(1)}, bf16[40,384]{1,0:T(8,128)(2,1)S(1)}, u32[]{:S(2)}, u32[]{:S(2)}) collective-permute-start(bf16[40,384]{1,0:T(8,128)(2,1)S(1)} %get-tuple-element.31), channel_id=1, source_target_pairs={{0,20},{2,22},{4,16},{6,18},{8,28},{10,30},{12,24},{14,26},{16,4},... | collective-permute-start | bytes 92168 | tf_op jit(solution)/shard_map/ppermute | solution.py:268
  27.6 1.6 %collective-permute-done.5.refs_5_ = bf16[40,384]{1,0:T(8,128)(2,1)S(1)} collective-permute-done((bf16[40,384]{1,0:T(8,128)(2,1)S(1)}, bf16[40,384]{1,0:T(8,128)(2,1)S(1)}, u32[]{:S(2)}, u32[]{:S(2)}) %collective-permute-start.5) | collective-permute-done | bytes 30752 | tf_op jit(solution)/shard_map/ppermute | solution.py:268
  29.3 4.2 %collective-permute-start.9 = (bf16[40,384]{1,0:T(8,128)(2,1)S(1)}, bf16[40,384]{1,0:T(8,128)(2,1)S(1)}, u32[]{:S(2)}, u32[]{:S(2)}) collective-permute-start(bf16[40,384]{1,0:T(8,128)(2,1)S(1)} %get-tuple-element.33), channel_id=1, source_target_pairs={{0,24},{2,26},{4,28},{6,30},{8,16},{10,18},{12,20},{14,22},{16,8},... | collective-permute-start | bytes 92168 | tf_op jit(solution)/shard_map/ppermute | solution.py:268
  33.4 0.6 collective-permute-start.1
  34.0 1.3 %collective-permute-done.9.refs_9_ = bf16[40,384]{1,0:T(8,128)(2,1)S(1)} collective-permute-done((bf16[40,384]{1,0:T(8,128)(2,1)S(1)}, bf16[40,384]{1,0:T(8,128)(2,1)S(1)}, u32[]{:S(2)}, u32[]{:S(2)}) %collective-permute-start.9) | collective-permute-done | bytes 30752 | tf_op jit(solution)/shard_map/ppermute | solution.py:268
  35.3 2.6 %collective-permute-start.3 = (bf16[40,1536]{1,0:T(8,128)(2,1)S(1)}, bf16[40,1536]{1,0:T(8,128)(2,1)S(1)}, u32[]{:S(2)}, u32[]{:S(2)}) collective-permute-start(bf16[40,1536]{1,0:T(8,128)(2,1)S(1)} %get-tuple-element.28), channel_id=1, source_target_pairs={{0,12},{2,14},{4,8},{6,10},{8,4},{10,6},{12,0},{14,2},{16,28},{18,... | collective-permute-start | bytes 368648 | tf_op jit(solution)/shard_map/ppermute | solution.py:268
  37.9 4.5 %collective-permute-start.10 = (bf16[40,1536]{1,0:T(8,128)(2,1)S(1)}, bf16[40,1536]{1,0:T(8,128)(2,1)S(1)}, u32[]{:S(2)}, u32[]{:S(2)}) collective-permute-start(bf16[40,1536]{1,0:T(8,128)(2,1)S(1)} %get-tuple-element.34), channel_id=1, source_target_pairs={{0,28},{2,30},{4,24},{6,26},{8,20},{10,22},{12,16},{14,18},{16,12}... | collective-permute-start | bytes 368648 | tf_op jit(solution)/shard_map/ppermute | solution.py:268
  42.4 1.2 %collective-permute-done.16.refs_16_ = bf16[40,384]{1,0:T(8,128)(2,1)S(1)} collective-permute-done((bf16[40,384]{1,0:T(8,128)(2,1)S(1)}, bf16[40,384]{1,0:T(8,128)(2,1)S(1)}, u32[]{:S(2)}, u32[]{:S(2)}) %collective-permute-start.16) | collective-permute-done | bytes 30752 | tf_op jit(solution)/shard_map/ppermute | solution.py:268
  43.8 1.0 %collective-permute-done.18.refs_18_ = bf16[40,384]{1,0:T(8,128)(2,1)S(1)} collective-permute-done((bf16[40,384]{1,0:T(8,128)(2,1)S(1)}, bf16[40,384]{1,0:T(8,128)(2,1)S(1)}, u32[]{:S(2)}, u32[]{:S(2)}) %collective-permute-start.18) | collective-permute-done | bytes 30752 | tf_op jit(solution)/shard_map/ppermute | solution.py:268
  45.0 1.0 %collective-permute-done.20.refs_20_ = bf16[40,384]{1,0:T(8,128)(2,1)S(1)} collective-permute-done((bf16[40,384]{1,0:T(8,128)(2,1)S(1)}, bf16[40,384]{1,0:T(8,128)(2,1)S(1)}, u32[]{:S(2)}, u32[]{:S(2)}) %collective-permute-start.20) | collective-permute-done | bytes 30752 | tf_op jit(solution)/shard_map/ppermute | solution.py:268
  46.2 0.3 collective-permute-start.12
  48.4 4.5 %shard_map.80 = (bf16[40,1152]{1,0:T(8,128)(2,1)S(1)}, bf16[40,1152]{1,0:T(8,128)(2,1)S(1)}, bf16[40,1152]{1,0:T(8,128)(2,1)S(1)}, bf16[40,1152]{1,0:T(8,128)(2,...) custom-call(bf16[40,1536]{1,0:T(8,128)(2,1)S(1)} %get-tuple-element., ...), custom_call_target="tpu_custom_call" | custom-call | flops 524288000 | bytes 2703360 | tf_op jit(solution)/shard_map/pallas_call | solution.py:35
  53.1 3.4 %collective-permute-start.24 = (bf16[40,1152]{1,0:T(8,128)(2,1)S(1)}, bf16[40,1152]{1,0:T(8,128)(2,1)S(1)}, u32[]{:S(2)}, u32[]{:S(2)}) collective-permute-start(bf16[40,1152]{1,0:T(8,128)(2,1)S(1)} %get-tuple-element.38), channel_id=1, source_target_pairs={{0,12},{2,14},{4,8},{6,10},{8,4},{10,6},{12,0},{14,2},{16,28},{18,... | collective-permute-start | bytes 276488 | tf_op jit(solution)/shard_map/ppermute | solution.py:268
  56.5 0.6 collective-permute-start.25
  57.1 1.9 %collective-permute-start.26 = (bf16[40,1152]{1,0:T(8,128)(2,1)S(1)}, bf16[40,1152]{1,0:T(8,128)(2,1)S(1)}, u32[]{:S(2)}, u32[]{:S(2)}) collective-permute-start(bf16[40,1152]{1,0:T(8,128)(2,1)S(1)} %get-tuple-element.40), channel_id=1, source_target_pairs={{0,20},{2,22},{4,16},{6,18},{8,28},{10,30},{12,24},{14,26},{16,4},... | collective-permute-start | bytes 276488 | tf_op jit(solution)/shard_map/ppermute | solution.py:268
  58.9 3.4 %collective-permute-start.27 = (bf16[40,1152]{1,0:T(8,128)(2,1)S(1)}, bf16[40,1152]{1,0:T(8,128)(2,1)S(1)}, u32[]{:S(2)}, u32[]{:S(2)}) collective-permute-start(bf16[40,1152]{1,0:T(8,128)(2,1)S(1)} %get-tuple-element.41), channel_id=1, source_target_pairs={{0,24},{2,26},{4,28},{6,30},{8,16},{10,18},{12,20},{14,22},{16,8},... | collective-permute-start | bytes 276488 | tf_op jit(solution)/shard_map/ppermute | solution.py:268
  62.4 1.8 %collective-permute-start.28 = (bf16[40,1152]{1,0:T(8,128)(2,1)S(1)}, bf16[40,1152]{1,0:T(8,128)(2,1)S(1)}, u32[]{:S(2)}, u32[]{:S(2)}) collective-permute-start(bf16[40,1152]{1,0:T(8,128)(2,1)S(1)} %get-tuple-element.42), channel_id=1, source_target_pairs={{0,28},{2,30},{4,24},{6,26},{8,20},{10,22},{12,16},{14,18},{16,12}... | collective-permute-start | bytes 276488 | tf_op jit(solution)/shard_map/ppermute | solution.py:268
  64.1 6.4 %collective-permute-done.25.refs_4_ = bf16[40,1152]{1,0:T(8,128)(2,1)S(1)} collective-permute-done((bf16[40,1152]{1,0:T(8,128)(2,1)S(1)}, bf16[40,1152]{1,0:T(8,128)(2,1)S(1)}, u32[]{:S(2)}, u32[]{:S(2)}) %collective-permute-start.25) | collective-permute-done | bytes 92192 | tf_op jit(solution)/shard_map/ppermute | solution.py:268
  70.6 1.6 %collective-permute-done.26.refs_5_ = bf16[40,1152]{1,0:T(8,128)(2,1)S(1)} collective-permute-done((bf16[40,1152]{1,0:T(8,128)(2,1)S(1)}, bf16[40,1152]{1,0:T(8,128)(2,1)S(1)}, u32[]{:S(2)}, u32[]{:S(2)}) %collective-permute-start.26) | collective-permute-done | bytes 92192 | tf_op jit(solution)/shard_map/ppermute | solution.py:268
  72.1 1.0 %shard_map.81 = (bf16[40,3072]{1,0:T(8,128)(2,1)}, bf16[40,3072]{1,0:T(8,128)(2,1)}, bf16[40,3072]{1,0:T(8,128)(2,1)}) custom-call(bf16[40,1152]{1,0:T(8,128)(2,1)S(1)} %get-tuple-element.35.refs_0_, bf16[40,1152]{1,0:T(8,128)(2,1)S(1)} %collective-permute-done.22.refs_1_, bf16[40,1152]{1,0:T(8,128)(2,1)S(1)} %collective-permute-done.23.refs_2_, ...), custom_call_target="tpu_custom_call" | custom-call | bytes 1474560 | tf_op jit(solution)/shard_map/pallas_call | solution.py:35
  (42 shorter events, 2.8 us)
Async XLA Ops:
  4.9 6.6 %copy-start.1 = (bf16[40,3072]{1,0:T(8,128)(2,1)S(1)}, bf16[40,3072]{1,0:T(8,128)(2,1)}, u32[]{:S(2)}) copy-start(bf16[40,3072]{1,0:T(8,128)(2,1)} %refs_0_.5) | copy-start | bytes 737284
  4.9 6.6 %copy-start.2 = (bf16[40,3072]{1,0:T(8,128)(2,1)S(1)}, bf16[40,3072]{1,0:T(8,128)(2,1)}, u32[]{:S(2)}) copy-start(bf16[40,3072]{1,0:T(8,128)(2,1)} %refs_1_.5) | copy-start | bytes 737284
  4.9 6.6 %copy-start.3 = (bf16[40,3072]{1,0:T(8,128)(2,1)S(1)}, bf16[40,3072]{1,0:T(8,128)(2,1)}, u32[]{:S(2)}) copy-start(bf16[40,3072]{1,0:T(8,128)(2,1)} %refs_2_.5) | copy-start | bytes 737284
  4.9 18.9 %collective-permute-start = (bf16[20,3072]{1,0:T(8,128)(2,1)S(1)}, bf16[20,3072]{1,0:T(8,128)(2,1)S(1)}, u32[]{:S(2)}, u32[]{:S(2)}) collective-permute-start(bf16[20,3072]{1,0:T(8,128)(2,1)S(1)} %get-tuple-element.24), channel_id=1, source_target_pairs={{0,1},{1,0},{2,3},{3,2},{4,5},{5,4},{6,7},{7,6},{8,9},{9,8},{10,11... | collective-permute-start | bytes 368648 | tf_op jit(solution)/shard_map/ppermute | solution.py:278
  8.8 11.6 %collective-permute-start.4 = (bf16[40,1152]{1,0:T(8,128)(2,1)S(1)}, bf16[40,1152]{1,0:T(8,128)(2,1)S(1)}, u32[]{:S(2)}, u32[]{:S(2)}) collective-permute-start(bf16[40,1152]{1,0:T(8,128)(2,1)S(1)} %shard_map.78), channel_id=1, source_target_pairs={{0,16},{2,18},{4,20},{6,22},{8,24},{10,26},{12,28},{14,30},{16,0},... | collective-permute-start | bytes 276488 | tf_op jit(solution)/shard_map/ppermute | solution.py:268
  11.5 11.8 %collective-permute-start.6 = (bf16[40,1152]{1,0:T(8,128)(2,1)S(1)}, bf16[40,1152]{1,0:T(8,128)(2,1)S(1)}, u32[]{:S(2)}, u32[]{:S(2)}) collective-permute-start(bf16[40,1152]{1,0:T(8,128)(2,1)S(1)} %get-tuple-element.30), channel_id=1, source_target_pairs={{0,20},{2,22},{4,16},{6,18},{8,28},{10,30},{12,24},{14,26},{16,4},... | collective-permute-start | bytes 276488 | tf_op jit(solution)/shard_map/ppermute | solution.py:268
  12.8 10.5 %collective-permute-start.8 = (bf16[40,1152]{1,0:T(8,128)(2,1)S(1)}, bf16[40,1152]{1,0:T(8,128)(2,1)S(1)}, u32[]{:S(2)}, u32[]{:S(2)}) collective-permute-start(bf16[40,1152]{1,0:T(8,128)(2,1)S(1)} %get-tuple-element.32), channel_id=1, source_target_pairs={{0,24},{2,26},{4,28},{6,30},{8,16},{10,18},{12,20},{14,22},{16,8},... | collective-permute-start | bytes 276488 | tf_op jit(solution)/shard_map/ppermute | solution.py:268
  20.4 14.9 %collective-permute-start.15 = (bf16[40,1152]{1,0:T(8,128)(2,1)S(1)}, bf16[40,1152]{1,0:T(8,128)(2,1)S(1)}, u32[]{:S(2)}, u32[]{:S(2)}) collective-permute-start(bf16[40,1152]{1,0:T(8,128)(2,1)S(1)} %collective-permute-done.4.refs_4_), channel_id=1, source_target_pairs={{0,2},{2,0},{4,6},{6,4},{8,10},{10,8},{12,14},{14,12},{16,18},{18,... | collective-permute-start | bytes 276488 | tf_op jit(solution)/shard_map/ppermute | solution.py:268
  23.3 14.6 %collective-permute-start.17 = (bf16[40,1152]{1,0:T(8,128)(2,1)S(1)}, bf16[40,1152]{1,0:T(8,128)(2,1)S(1)}, u32[]{:S(2)}, u32[]{:S(2)}) collective-permute-start(bf16[40,1152]{1,0:T(8,128)(2,1)S(1)} %collective-permute-done.6.refs_6_), channel_id=1, source_target_pairs={{0,2},{2,0},{4,6},{6,4},{8,10},{10,8},{12,14},{14,12},{16,18},{18,... | collective-permute-start | bytes 276488 | tf_op jit(solution)/shard_map/ppermute | solution.py:268
  23.3 19.1 %collective-permute-start.19 = (bf16[40,1152]{1,0:T(8,128)(2,1)S(1)}, bf16[40,1152]{1,0:T(8,128)(2,1)S(1)}, u32[]{:S(2)}, u32[]{:S(2)}) collective-permute-start(bf16[40,1152]{1,0:T(8,128)(2,1)S(1)} %collective-permute-done.8.refs_8_), channel_id=1, source_target_pairs={{0,2},{2,0},{4,6},{6,4},{8,10},{10,8},{12,14},{14,12},{16,18},{18,... | collective-permute-start | bytes 276488 | tf_op jit(solution)/shard_map/ppermute | solution.py:268
  24.0 5.3 %collective-permute-start.5 = (bf16[40,384]{1,0:T(8,128)(2,1)S(1)}, bf16[40,384]{1,0:T(8,128)(2,1)S(1)}, u32[]{:S(2)}, u32[]{:S(2)}) collective-permute-start(bf16[40,384]{1,0:T(8,128)(2,1)S(1)} %get-tuple-element.29), channel_id=1, source_target_pairs={{0,16},{2,18},{4,20},{6,22},{8,24},{10,26},{12,28},{14,30},{16,0},... | collective-permute-start | bytes 92168 | tf_op jit(solution)/shard_map/ppermute | solution.py:268
  26.6 6.9 %collective-permute-start.7 = (bf16[40,384]{1,0:T(8,128)(2,1)S(1)}, bf16[40,384]{1,0:T(8,128)(2,1)S(1)}, u32[]{:S(2)}, u32[]{:S(2)}) collective-permute-start(bf16[40,384]{1,0:T(8,128)(2,1)S(1)} %get-tuple-element.31), channel_id=1, source_target_pairs={{0,20},{2,22},{4,16},{6,18},{8,28},{10,30},{12,24},{14,26},{16,4},... | collective-permute-start | bytes 92168 | tf_op jit(solution)/shard_map/ppermute | solution.py:268
  29.3 6.0 %collective-permute-start.9 = (bf16[40,384]{1,0:T(8,128)(2,1)S(1)}, bf16[40,384]{1,0:T(8,128)(2,1)S(1)}, u32[]{:S(2)}, u32[]{:S(2)}) collective-permute-start(bf16[40,384]{1,0:T(8,128)(2,1)S(1)} %get-tuple-element.33), channel_id=1, source_target_pairs={{0,24},{2,26},{4,28},{6,30},{8,16},{10,18},{12,20},{14,22},{16,8},... | collective-permute-start | bytes 92168 | tf_op jit(solution)/shard_map/ppermute | solution.py:268
  33.4 12.7 %collective-permute-start.1 = (bf16[40,1536]{1,0:T(8,128)(2,1)S(1)}, bf16[40,1536]{1,0:T(8,128)(2,1)S(1)}, u32[]{:S(2)}, u32[]{:S(2)}) collective-permute-start(bf16[40,1536]{1,0:T(8,128)(2,1)S(1)} %get-tuple-element.26), channel_id=1, source_target_pairs={{0,4},{2,6},{4,0},{6,2},{8,12},{10,14},{12,8},{14,10},{16,20},{18,... | collective-permute-start | bytes 368648 | tf_op jit(solution)/shard_map/ppermute | solution.py:268
  35.3 11.2 %collective-permute-start.2 = (bf16[40,1536]{1,0:T(8,128)(2,1)S(1)}, bf16[40,1536]{1,0:T(8,128)(2,1)S(1)}, u32[]{:S(2)}, u32[]{:S(2)}) collective-permute-start(bf16[40,1536]{1,0:T(8,128)(2,1)S(1)} %get-tuple-element.27), channel_id=1, source_target_pairs={{0,8},{2,10},{4,12},{6,14},{8,0},{10,2},{12,4},{14,6},{16,24},{18,... | collective-permute-start | bytes 368648 | tf_op jit(solution)/shard_map/ppermute | solution.py:268
  35.3 11.4 %collective-permute-start.3 = (bf16[40,1536]{1,0:T(8,128)(2,1)S(1)}, bf16[40,1536]{1,0:T(8,128)(2,1)S(1)}, u32[]{:S(2)}, u32[]{:S(2)}) collective-permute-start(bf16[40,1536]{1,0:T(8,128)(2,1)S(1)} %get-tuple-element.28), channel_id=1, source_target_pairs={{0,12},{2,14},{4,8},{6,10},{8,4},{10,6},{12,0},{14,2},{16,28},{18,... | collective-permute-start | bytes 368648 | tf_op jit(solution)/shard_map/ppermute | solution.py:268
  37.9 9.1 %collective-permute-start.10 = (bf16[40,1536]{1,0:T(8,128)(2,1)S(1)}, bf16[40,1536]{1,0:T(8,128)(2,1)S(1)}, u32[]{:S(2)}, u32[]{:S(2)}) collective-permute-start(bf16[40,1536]{1,0:T(8,128)(2,1)S(1)} %get-tuple-element.34), channel_id=1, source_target_pairs={{0,28},{2,30},{4,24},{6,26},{8,20},{10,22},{12,16},{14,18},{16,12}... | collective-permute-start | bytes 368648 | tf_op jit(solution)/shard_map/ppermute | solution.py:268
  42.4 1.2 %collective-permute-start.16 = (bf16[40,384]{1,0:T(8,128)(2,1)S(1)}, bf16[40,384]{1,0:T(8,128)(2,1)S(1)}, u32[]{:S(2)}, u32[]{:S(2)}) collective-permute-start(bf16[40,384]{1,0:T(8,128)(2,1)S(1)} %collective-permute-done.5.refs_5_), channel_id=1, source_target_pairs={{0,2},{2,0},{4,6},{6,4},{8,10},{10,8},{12,14},{14,12},{16,18},{18,... | collective-permute-start | bytes 92168 | tf_op jit(solution)/shard_map/ppermute | solution.py:268
  43.6 1.2 %collective-permute-start.18 = (bf16[40,384]{1,0:T(8,128)(2,1)S(1)}, bf16[40,384]{1,0:T(8,128)(2,1)S(1)}, u32[]{:S(2)}, u32[]{:S(2)}) collective-permute-start(bf16[40,384]{1,0:T(8,128)(2,1)S(1)} %collective-permute-done.7.refs_7_), channel_id=1, source_target_pairs={{0,2},{2,0},{4,6},{6,4},{8,10},{10,8},{12,14},{14,12},{16,18},{18,... | collective-permute-start | bytes 92168 | tf_op jit(solution)/shard_map/ppermute | solution.py:268
  44.8 1.2 %collective-permute-start.20 = (bf16[40,384]{1,0:T(8,128)(2,1)S(1)}, bf16[40,384]{1,0:T(8,128)(2,1)S(1)}, u32[]{:S(2)}, u32[]{:S(2)}) collective-permute-start(bf16[40,384]{1,0:T(8,128)(2,1)S(1)} %collective-permute-done.9.refs_9_), channel_id=1, source_target_pairs={{0,2},{2,0},{4,6},{6,4},{8,10},{10,8},{12,14},{14,12},{16,18},{18,... | collective-permute-start | bytes 92168 | tf_op jit(solution)/shard_map/ppermute | solution.py:268
  46.0 1.3 %collective-permute-start.11 = (bf16[40,1536]{1,0:T(8,128)(2,1)S(1)}, bf16[40,1536]{1,0:T(8,128)(2,1)S(1)}, u32[]{:S(2)}, u32[]{:S(2)}) collective-permute-start(bf16[40,1536]{1,0:T(8,128)(2,1)S(1)} %get-tuple-element.25.refs_0_), channel_id=1, source_target_pairs={{0,2},{2,0},{4,6},{6,4},{8,10},{10,8},{12,14},{14,12},{16,18},{18,... | collective-permute-start | bytes 368648 | tf_op jit(solution)/shard_map/ppermute | solution.py:268
  46.2 1.3 %collective-permute-start.12 = (bf16[40,1536]{1,0:T(8,128)(2,1)S(1)}, bf16[40,1536]{1,0:T(8,128)(2,1)S(1)}, u32[]{:S(2)}, u32[]{:S(2)}) collective-permute-start(bf16[40,1536]{1,0:T(8,128)(2,1)S(1)} %collective-permute-done.1.refs_1_), channel_id=1, source_target_pairs={{0,2},{2,0},{4,6},{6,4},{8,10},{10,8},{12,14},{14,12},{16,18},{18,... | collective-permute-start | bytes 368648 | tf_op jit(solution)/shard_map/ppermute | solution.py:268
  46.5 1.3 %collective-permute-start.13 = (bf16[40,1536]{1,0:T(8,128)(2,1)S(1)}, bf16[40,1536]{1,0:T(8,128)(2,1)S(1)}, u32[]{:S(2)}, u32[]{:S(2)}) collective-permute-start(bf16[40,1536]{1,0:T(8,128)(2,1)S(1)} %collective-permute-done.2.refs_2_), channel_id=1, source_target_pairs={{0,2},{2,0},{4,6},{6,4},{8,10},{10,8},{12,14},{14,12},{16,18},{18,... | collective-permute-start | bytes 368648 | tf_op jit(solution)/shard_map/ppermute | solution.py:268
  46.7 1.3 %collective-permute-start.14 = (bf16[40,1536]{1,0:T(8,128)(2,1)S(1)}, bf16[40,1536]{1,0:T(8,128)(2,1)S(1)}, u32[]{:S(2)}, u32[]{:S(2)}) collective-permute-start(bf16[40,1536]{1,0:T(8,128)(2,1)S(1)} %collective-permute-done.3.refs_3_), channel_id=1, source_target_pairs={{0,2},{2,0},{4,6},{6,4},{8,10},{10,8},{12,14},{14,12},{16,18},{18,... | collective-permute-start | bytes 368648 | tf_op jit(solution)/shard_map/ppermute | solution.py:268
  47.0 1.3 %collective-permute-start.21 = (bf16[40,1536]{1,0:T(8,128)(2,1)S(1)}, bf16[40,1536]{1,0:T(8,128)(2,1)S(1)}, u32[]{:S(2)}, u32[]{:S(2)}) collective-permute-start(bf16[40,1536]{1,0:T(8,128)(2,1)S(1)} %collective-permute-done.10.refs_10_), channel_id=1, source_target_pairs={{0,2},{2,0},{4,6},{6,4},{8,10},{10,8},{12,14},{14,12},{16,18},{18,... | collective-permute-start | bytes 368648 | tf_op jit(solution)/shard_map/ppermute | solution.py:268
  52.9 6.0 %collective-permute-start.22 = (bf16[40,1152]{1,0:T(8,128)(2,1)S(1)}, bf16[40,1152]{1,0:T(8,128)(2,1)S(1)}, u32[]{:S(2)}, u32[]{:S(2)}) collective-permute-start(bf16[40,1152]{1,0:T(8,128)(2,1)S(1)} %get-tuple-element.36), channel_id=1, source_target_pairs={{0,4},{2,6},{4,0},{6,2},{8,12},{10,14},{12,8},{14,10},{16,20},{18,... | collective-permute-start | bytes 276488 | tf_op jit(solution)/shard_map/ppermute | solution.py:268
  53.1 9.3 %collective-permute-start.23 = (bf16[40,1152]{1,0:T(8,128)(2,1)S(1)}, bf16[40,1152]{1,0:T(8,128)(2,1)S(1)}, u32[]{:S(2)}, u32[]{:S(2)}) collective-permute-start(bf16[40,1152]{1,0:T(8,128)(2,1)S(1)} %get-tuple-element.37), channel_id=1, source_target_pairs={{0,8},{2,10},{4,12},{6,14},{8,0},{10,2},{12,4},{14,6},{16,24},{18,... | collective-permute-start | bytes 276488 | tf_op jit(solution)/shard_map/ppermute | solution.py:268
  53.1 11.0 %collective-permute-start.24 = (bf16[40,1152]{1,0:T(8,128)(2,1)S(1)}, bf16[40,1152]{1,0:T(8,128)(2,1)S(1)}, u32[]{:S(2)}, u32[]{:S(2)}) collective-permute-start(bf16[40,1152]{1,0:T(8,128)(2,1)S(1)} %get-tuple-element.38), channel_id=1, source_target_pairs={{0,12},{2,14},{4,8},{6,10},{8,4},{10,6},{12,0},{14,2},{16,28},{18,... | collective-permute-start | bytes 276488 | tf_op jit(solution)/shard_map/ppermute | solution.py:268
  56.5 14.1 %collective-permute-start.25 = (bf16[40,1152]{1,0:T(8,128)(2,1)S(1)}, bf16[40,1152]{1,0:T(8,128)(2,1)S(1)}, u32[]{:S(2)}, u32[]{:S(2)}) collective-permute-start(bf16[40,1152]{1,0:T(8,128)(2,1)S(1)} %get-tuple-element.39), channel_id=1, source_target_pairs={{0,16},{2,18},{4,20},{6,22},{8,24},{10,26},{12,28},{14,30},{16,0},... | collective-permute-start | bytes 276488 | tf_op jit(solution)/shard_map/ppermute | solution.py:268
  57.1 15.1 %collective-permute-start.26 = (bf16[40,1152]{1,0:T(8,128)(2,1)S(1)}, bf16[40,1152]{1,0:T(8,128)(2,1)S(1)}, u32[]{:S(2)}, u32[]{:S(2)}) collective-permute-start(bf16[40,1152]{1,0:T(8,128)(2,1)S(1)} %get-tuple-element.40), channel_id=1, source_target_pairs={{0,20},{2,22},{4,16},{6,18},{8,28},{10,30},{12,24},{14,26},{16,4},... | collective-permute-start | bytes 276488 | tf_op jit(solution)/shard_map/ppermute | solution.py:268
  58.9 13.2 %collective-permute-start.27 = (bf16[40,1152]{1,0:T(8,128)(2,1)S(1)}, bf16[40,1152]{1,0:T(8,128)(2,1)S(1)}, u32[]{:S(2)}, u32[]{:S(2)}) collective-permute-start(bf16[40,1152]{1,0:T(8,128)(2,1)S(1)} %get-tuple-element.41), channel_id=1, source_target_pairs={{0,24},{2,26},{4,28},{6,30},{8,16},{10,18},{12,20},{14,22},{16,8},... | collective-permute-start | bytes 276488 | tf_op jit(solution)/shard_map/ppermute | solution.py:268
  62.4 9.8 %collective-permute-start.28 = (bf16[40,1152]{1,0:T(8,128)(2,1)S(1)}, bf16[40,1152]{1,0:T(8,128)(2,1)S(1)}, u32[]{:S(2)}, u32[]{:S(2)}) collective-permute-start(bf16[40,1152]{1,0:T(8,128)(2,1)S(1)} %get-tuple-element.42), channel_id=1, source_target_pairs={{0,28},{2,30},{4,24},{6,26},{8,20},{10,22},{12,16},{14,18},{16,12}... | collective-permute-start | bytes 276488 | tf_op jit(solution)/shard_map/ppermute | solution.py:268
  (2 other events, 3.0 us)

commit v5 on v4

--- a/solution.py
+++ b/solution.py
@@ -148,7 +148,7 @@
 def attend(own, other, rows):
     chips = len(own)
     total = 2 * chips * rows
-    part = chips // 2 * rows
+    part = chips * rows
     scaling = 1.0 / math.sqrt(HD)
     grade = scaling * math.log2(math.e)
     operands = [block for part in (own, other) for blocks in part for block in blocks]
@@ -170,8 +170,7 @@
             return blocks[0][:, pl.ds(pl.multiple_of(at * HD, HD), HD)].astype(jnp.float32)
 
         def spots(step):
-            late = jnp.where((chip ^ step) >= chips // 2, 1, 0)
-            start = late * (2 * part) + ((chip ^ step) - late * (chips // 2)) * rows
+            start = (chip ^ step) * rows
             return (
                 pl.ds(pl.multiple_of(start, 8), rows),
                 pl.ds(pl.multiple_of(start + part, 8), rows),
@@ -185,8 +184,7 @@
             side = jnp.abs(others - jnp.where(core == 1, 1.0, 0.0))
             return which * (2 * rows) + side * rows + (inside - which * rows)
 
-        square = hidden.shape
-        hidden[...] = jnp.where(place(square, 0) <= place(square, 1), 0.0, lowest)
+        hidden[...] = jnp.where(place((total, 1), 0) <= place((1, total), 1), 0.0, lowest)
         last, first, plain = ((((x,), (y,)), ((), ())) for x, y in ((1, 1), (0, 0), (1, 0)))
         for head in range(3):
             for which in range(4):
@@ -197,30 +195,22 @@
             query, keys, values, grads = (
                 gathered[which].astype(jnp.bfloat16) for which in range(4)
             )
-            for low in range(0, total, 2 * part):
-                high = low + 2 * part
-                q, g = query[low:high], grads[low:high]
-                k, v = keys[:high], values[:high]
-                scores = lax.dot_general(k, q, last, preferred_element_type=jnp.float32)
-                below = scores[low:] + hidden[...]
-                scores = jnp.concatenate([scores[:low], below]) if low else below
-                expo = jnp.exp2((scores - jnp.max(scores, axis=0, keepdims=True)) * grade)
-                products = lax.dot_general(v, g, last, preferred_element_type=jnp.float32)
-                scale = 1.0 / jnp.sum(expo, axis=0, keepdims=True)
-                delta = jnp.sum(expo * products, axis=0, keepdims=True) * scale
-                weights = expo * scale
-                score_grad = (weights * (products - delta)).astype(jnp.bfloat16)
-                half = weights.astype(jnp.bfloat16)
-                query_sum[low : low + part] = lax.dot_general(
-                    score_grad[:, :part], k, first, preferred_element_type=jnp.float32
+            scores = lax.dot_general(keys, query, last, preferred_element_type=jnp.float32)
+            scores = scores + hidden[...]
+            expo = jnp.exp2((scores - jnp.max(scores, axis=0, keepdims=True)) * grade)
+            products = lax.dot_general(values, grads, last, preferred_element_type=jnp.float32)
+            scale = 1.0 / jnp.sum(expo, axis=0, keepdims=True)
+            delta = jnp.sum(expo * products, axis=0, keepdims=True) * scale
+            weights = expo * scale
+            score_grad = (weights * (products - delta)).astype(jnp.bfloat16)
+            half = weights.astype(jnp.bfloat16)
+            query_sum[...] = lax.dot_general(
+                score_grad[:, :part], keys, first, preferred_element_type=jnp.float32
+            )
+            for store, left, right in ((key_sum, score_grad, query), (value_sum, half, grads)):
+                store[...] = lax.dot_general(
+                    left[:part], right, plain, preferred_element_type=jnp.float32
                 )
-                for start in range(0, high, 2 * part):
-                    mine = slice(start, start + part)
-                    for store, left, right in ((key_sum, score_grad, q), (value_sum, half, g)):
-                        added = lax.dot_general(
-                            left[mine], right, plain, preferred_element_type=jnp.float32
-                        )
-                        store[mine] = added if start == low else store[mine] + added
             for which, (store, factor) in enumerate(
                 ((query_sum, scaling), (key_sum, scaling), (value_sum, 1.0))
             ):
@@ -228,7 +218,7 @@
                 for step in range(chips):
                     outs[step][:, at : at + HD] = (store[spots(step)[0]] * factor).astype(jnp.bfloat16)
 
-    big = pltpu.VMEM((total, HD), jnp.float32)
+    big = pltpu.VMEM((part, HD), jnp.float32)
     return local(
         kernel,
         operands,
@@ -238,7 +228,7 @@
             big,
             big,
             big,
-            pltpu.VMEM((2 * part, 2 * part), jnp.float32),
+            pltpu.VMEM((total, total), jnp.float32),
         ],
         10 * total * total * HD,
     )
@@ -299,7 +289,7 @@
         and lax.axis_size("narrow") == 2
         and columns == chips * 3 * HD
         and chips > 1
-        and (chips // 2 * rows) % 16 == 0
+        and (chips * rows) % 16 == 0
         and rows % 8 == 0
     )
     plan = by_heads if fits else by_rows

time: 74.3 us -> 74 us (level)
  no operation moved by 1% of the time
where the time goes in v5:
time: 74 us; the launch traced here: 72.9 us
  starting transfers between devices  39.3 us (53%)
  waiting for transfers between devices  22.3 us (30%)
  Pallas kernels  7.51 us (10%)
  local copies, waits for them, and re-layouts  2.99 us (4%)
    ppermute x28, starting transfers between devices, cross(): lax.ppermute(block, 'wide', [(i, i ^ step) for i in range(size)])  36.3 us
    ppermute x28, waiting for transfers between devices, cross(): lax.ppermute(block, 'wide', [(i, i ^ step) for i in range(size)])  22.3 us
    pallas_call x6, Pallas kernels, local(): pl.pallas_call(kernel, in_specs=[anywhere if i in afar else vmem for i in...  7.51 us
    ppermute x1, starting transfers between devices, by_heads(): came = held(lax.ppermute(leave, 'narrow', [(0, 1), (1, 0)]))  3.06 us
    unnamed x10, local copies, waits for them, and re-layouts  2.99 us
  transfers between devices with their start and end apart: 29, of which 14 were waited for; matrix products, arithmetic and copies ran while one was open for 0% of the time, Pallas kernels for 1%

profile of v5, /device:TPU:0, one launch (start us, length us, event | category | flops | bytes accessed | tf_op | source)
XLA Modules:
  0.0 72.9 jit_solution(1008902494245547202)
XLA Ops:
  0.6 1.9 %copy-done = bf16[768,2048]{1,0:T(8,128)(2,1)S(1)} copy-done((bf16[768,2048]{1,0:T(8,128)(2,1)S(1)}, bf16[768,2048]{1,0:T(8,128)(2,1)}, u32[]{:S(2)}) %copy-start) | copy-done | bytes 3145752
  2.5 1.1 %copy-done.4 = bf16[160,2048]{1,0:T(8,128)(2,1)S(1)} copy-done((bf16[160,2048]{1,0:T(8,128)(2,1)S(1)}, bf16[160,2048]{1,0:T(8,128)(2,1)}, u32[]{:S(2)}) %copy-start.4) | copy-done | bytes 655384
  3.6 1.3 %shard_map.76 = (bf16[20,3072]{1,0:T(8,128)(2,1)S(1)}, bf16[20,3072]{1,0:T(8,128)(2,1)S(1)}) custom-call(bf16[160,2048]{1,0:T(8,128)(2,1)S(1)} %copy-done.4, bf16[768,2048]{1,0:T(8,128)(2,1)S(1)} %copy-done), custom_call_target="tpu_custom_call" | custom-call | flops 503316480 | bytes 4046848 | tf_op jit(solution)/shard_map/pallas_call | solution.py:35
  4.9 3.1 %collective-permute-start = (bf16[20,3072]{1,0:T(8,128)(2,1)S(1)}, bf16[20,3072]{1,0:T(8,128)(2,1)S(1)}, u32[]{:S(2)}, u32[]{:S(2)}) collective-permute-start(bf16[20,3072]{1,0:T(8,128)(2,1)S(1)} %get-tuple-element.24), channel_id=1, source_target_pairs={{0,1},{1,0},{2,3},{3,2},{4,5},{5,4},{6,7},{7,6},{8,9},{9,8},{10,11... | collective-permute-start | bytes 368648 | tf_op jit(solution)/shard_map/ppermute | solution.py:268
  8.0 0.8 %shard_map.78 = bf16[40,1152]{1,0:T(8,128)(2,1)S(1)} custom-call(bf16[40,3072]{1,0:T(8,128)(2,1)} %refs_0_.5, bf16[40,3072]{1,0:T(8,128)(2,1)} %refs_1_.5, bf16[40,3072]{1,0:T(8,128)(2,1)} %refs_2_.5), custom_call_target="tpu_custom_call" | custom-call | flops 5000000000 | bytes 829440 | tf_op jit(solution)/shard_map/pallas_call | solution.py:35
  8.8 2.7 %collective-permute-start.4 = (bf16[40,1152]{1,0:T(8,128)(2,1)S(1)}, bf16[40,1152]{1,0:T(8,128)(2,1)S(1)}, u32[]{:S(2)}, u32[]{:S(2)}) collective-permute-start(bf16[40,1152]{1,0:T(8,128)(2,1)S(1)} %shard_map.78), channel_id=1, source_target_pairs={{0,16},{2,18},{4,20},{6,22},{8,24},{10,26},{12,28},{14,30},{16,0},... | collective-permute-start | bytes 276488 | tf_op jit(solution)/shard_map/ppermute | solution.py:258
  11.5 1.3 %collective-permute-start.6 = (bf16[40,1152]{1,0:T(8,128)(2,1)S(1)}, bf16[40,1152]{1,0:T(8,128)(2,1)S(1)}, u32[]{:S(2)}, u32[]{:S(2)}) collective-permute-start(bf16[40,1152]{1,0:T(8,128)(2,1)S(1)} %get-tuple-element.30), channel_id=1, source_target_pairs={{0,20},{2,22},{4,16},{6,18},{8,28},{10,30},{12,24},{14,26},{16,4},... | collective-permute-start | bytes 276488 | tf_op jit(solution)/shard_map/ppermute | solution.py:258
  12.8 3.6 %collective-permute-start.8 = (bf16[40,1152]{1,0:T(8,128)(2,1)S(1)}, bf16[40,1152]{1,0:T(8,128)(2,1)S(1)}, u32[]{:S(2)}, u32[]{:S(2)}) collective-permute-start(bf16[40,1152]{1,0:T(8,128)(2,1)S(1)} %get-tuple-element.32), channel_id=1, source_target_pairs={{0,24},{2,26},{4,28},{6,30},{8,16},{10,18},{12,20},{14,22},{16,8},... | collective-permute-start | bytes 276488 | tf_op jit(solution)/shard_map/ppermute | solution.py:258
  16.4 4.0 %collective-permute-done.4.refs_4_ = bf16[40,1152]{1,0:T(8,128)(2,1)S(1)} collective-permute-done((bf16[40,1152]{1,0:T(8,128)(2,1)S(1)}, bf16[40,1152]{1,0:T(8,128)(2,1)S(1)}, u32[]{:S(2)}, u32[]{:S(2)}) %collective-permute-start.4) | collective-permute-done | bytes 92192 | tf_op jit(solution)/shard_map/ppermute | solution.py:258
  20.4 2.9 %collective-permute-done.6.refs_6_ = bf16[40,1152]{1,0:T(8,128)(2,1)S(1)} collective-permute-done((bf16[40,1152]{1,0:T(8,128)(2,1)S(1)}, bf16[40,1152]{1,0:T(8,128)(2,1)S(1)}, u32[]{:S(2)}, u32[]{:S(2)}) %collective-permute-start.6) | collective-permute-done | bytes 92192 | tf_op jit(solution)/shard_map/ppermute | solution.py:258
  23.3 0.5 collective-permute-start.19
  24.0 2.6 %collective-permute-start.5 = (bf16[40,384]{1,0:T(8,128)(2,1)S(1)}, bf16[40,384]{1,0:T(8,128)(2,1)S(1)}, u32[]{:S(2)}, u32[]{:S(2)}) collective-permute-start(bf16[40,384]{1,0:T(8,128)(2,1)S(1)} %get-tuple-element.29), channel_id=1, source_target_pairs={{0,16},{2,18},{4,20},{6,22},{8,24},{10,26},{12,28},{14,30},{16,0},... | collective-permute-start | bytes 92168 | tf_op jit(solution)/shard_map/ppermute | solution.py:258
  26.6 1.0 %collective-permute-start.7 = (bf16[40,384]{1,0:T(8,128)(2,1)S(1)}, bf16[40,384]{1,0:T(8,128)(2,1)S(1)}, u32[]{:S(2)}, u32[]{:S(2)}) collective-permute-start(bf16[40,384]{1,0:T(8,128)(2,1)S(1)} %get-tuple-element.31), channel_id=1, source_target_pairs={{0,20},{2,22},{4,16},{6,18},{8,28},{10,30},{12,24},{14,26},{16,4},... | collective-permute-start | bytes 92168 | tf_op jit(solution)/shard_map/ppermute | solution.py:258
  27.6 1.6 %collective-permute-done.5.refs_5_ = bf16[40,384]{1,0:T(8,128)(2,1)S(1)} collective-permute-done((bf16[40,384]{1,0:T(8,128)(2,1)S(1)}, bf16[40,384]{1,0:T(8,128)(2,1)S(1)}, u32[]{:S(2)}, u32[]{:S(2)}) %collective-permute-start.5) | collective-permute-done | bytes 30752 | tf_op jit(solution)/shard_map/ppermute | solution.py:258
  29.3 4.2 %collective-permute-start.9 = (bf16[40,384]{1,0:T(8,128)(2,1)S(1)}, bf16[40,384]{1,0:T(8,128)(2,1)S(1)}, u32[]{:S(2)}, u32[]{:S(2)}) collective-permute-start(bf16[40,384]{1,0:T(8,128)(2,1)S(1)} %get-tuple-element.33), channel_id=1, source_target_pairs={{0,24},{2,26},{4,28},{6,30},{8,16},{10,18},{12,20},{14,22},{16,8},... | collective-permute-start | bytes 92168 | tf_op jit(solution)/shard_map/ppermute | solution.py:258
  33.4 0.6 collective-permute-start.1
  34.0 1.3 %collective-permute-done.9.refs_9_ = bf16[40,384]{1,0:T(8,128)(2,1)S(1)} collective-permute-done((bf16[40,384]{1,0:T(8,128)(2,1)S(1)}, bf16[40,384]{1,0:T(8,128)(2,1)S(1)}, u32[]{:S(2)}, u32[]{:S(2)}) %collective-permute-start.9) | collective-permute-done | bytes 30752 | tf_op jit(solution)/shard_map/ppermute | solution.py:258
  35.3 2.6 %collective-permute-start.3 = (bf16[40,1536]{1,0:T(8,128)(2,1)S(1)}, bf16[40,1536]{1,0:T(8,128)(2,1)S(1)}, u32[]{:S(2)}, u32[]{:S(2)}) collective-permute-start(bf16[40,1536]{1,0:T(8,128)(2,1)S(1)} %get-tuple-element.28), channel_id=1, source_target_pairs={{0,12},{2,14},{4,8},{6,10},{8,4},{10,6},{12,0},{14,2},{16,28},{18,... | collective-permute-start | bytes 368648 | tf_op jit(solution)/shard_map/ppermute | solution.py:258
  37.9 4.5 %collective-permute-start.10 = (bf16[40,1536]{1,0:T(8,128)(2,1)S(1)}, bf16[40,1536]{1,0:T(8,128)(2,1)S(1)}, u32[]{:S(2)}, u32[]{:S(2)}) collective-permute-start(bf16[40,1536]{1,0:T(8,128)(2,1)S(1)} %get-tuple-element.34), channel_id=1, source_target_pairs={{0,28},{2,30},{4,24},{6,26},{8,20},{10,22},{12,16},{14,18},{16,12}... | collective-permute-start | bytes 368648 | tf_op jit(solution)/shard_map/ppermute | solution.py:258
  42.4 1.2 %collective-permute-done.16.refs_16_ = bf16[40,384]{1,0:T(8,128)(2,1)S(1)} collective-permute-done((bf16[40,384]{1,0:T(8,128)(2,1)S(1)}, bf16[40,384]{1,0:T(8,128)(2,1)S(1)}, u32[]{:S(2)}, u32[]{:S(2)}) %collective-permute-start.16) | collective-permute-done | bytes 30752 | tf_op jit(solution)/shard_map/ppermute | solution.py:258
  43.8 1.0 %collective-permute-done.18.refs_18_ = bf16[40,384]{1,0:T(8,128)(2,1)S(1)} collective-permute-done((bf16[40,384]{1,0:T(8,128)(2,1)S(1)}, bf16[40,384]{1,0:T(8,128)(2,1)S(1)}, u32[]{:S(2)}, u32[]{:S(2)}) %collective-permute-start.18) | collective-permute-done | bytes 30752 | tf_op jit(solution)/shard_map/ppermute | solution.py:258
  45.0 1.0 %collective-permute-done.20.refs_20_ = bf16[40,384]{1,0:T(8,128)(2,1)S(1)} collective-permute-done((bf16[40,384]{1,0:T(8,128)(2,1)S(1)}, bf16[40,384]{1,0:T(8,128)(2,1)S(1)}, u32[]{:S(2)}, u32[]{:S(2)}) %collective-permute-start.20) | collective-permute-done | bytes 30752 | tf_op jit(solution)/shard_map/ppermute | solution.py:258
  46.2 0.3 collective-permute-start.12
  48.4 4.3 %shard_map.80 = (bf16[40,1152]{1,0:T(8,128)(2,1)S(1)}, bf16[40,1152]{1,0:T(8,128)(2,1)S(1)}, bf16[40,1152]{1,0:T(8,128)(2,1)S(1)}, bf16[40,1152]{1,0:T(8,128)(2,...) custom-call(bf16[40,1536]{1,0:T(8,128)(2,1)S(1)} %get-tuple-element., ...), custom_call_target="tpu_custom_call" | custom-call | flops 524288000 | bytes 2703360 | tf_op jit(solution)/shard_map/pallas_call | solution.py:35
  52.9 3.4 %collective-permute-start.24 = (bf16[40,1152]{1,0:T(8,128)(2,1)S(1)}, bf16[40,1152]{1,0:T(8,128)(2,1)S(1)}, u32[]{:S(2)}, u32[]{:S(2)}) collective-permute-start(bf16[40,1152]{1,0:T(8,128)(2,1)S(1)} %get-tuple-element.38), channel_id=1, source_target_pairs={{0,12},{2,14},{4,8},{6,10},{8,4},{10,6},{12,0},{14,2},{16,28},{18,... | collective-permute-start | bytes 276488 | tf_op jit(solution)/shard_map/ppermute | solution.py:258
  56.2 0.6 collective-permute-start.25
  56.8 1.9 %collective-permute-start.26 = (bf16[40,1152]{1,0:T(8,128)(2,1)S(1)}, bf16[40,1152]{1,0:T(8,128)(2,1)S(1)}, u32[]{:S(2)}, u32[]{:S(2)}) collective-permute-start(bf16[40,1152]{1,0:T(8,128)(2,1)S(1)} %get-tuple-element.40), channel_id=1, source_target_pairs={{0,20},{2,22},{4,16},{6,18},{8,28},{10,30},{12,24},{14,26},{16,4},... | collective-permute-start | bytes 276488 | tf_op jit(solution)/shard_map/ppermute | solution.py:258
  58.7 3.4 %collective-permute-start.27 = (bf16[40,1152]{1,0:T(8,128)(2,1)S(1)}, bf16[40,1152]{1,0:T(8,128)(2,1)S(1)}, u32[]{:S(2)}, u32[]{:S(2)}) collective-permute-start(bf16[40,1152]{1,0:T(8,128)(2,1)S(1)} %get-tuple-element.41), channel_id=1, source_target_pairs={{0,24},{2,26},{4,28},{6,30},{8,16},{10,18},{12,20},{14,22},{16,8},... | collective-permute-start | bytes 276488 | tf_op jit(solution)/shard_map/ppermute | solution.py:258
  62.1 1.8 %collective-permute-start.28 = (bf16[40,1152]{1,0:T(8,128)(2,1)S(1)}, bf16[40,1152]{1,0:T(8,128)(2,1)S(1)}, u32[]{:S(2)}, u32[]{:S(2)}) collective-permute-start(bf16[40,1152]{1,0:T(8,128)(2,1)S(1)} %get-tuple-element.42), channel_id=1, source_target_pairs={{0,28},{2,30},{4,24},{6,26},{8,20},{10,22},{12,16},{14,18},{16,12}... | collective-permute-start | bytes 276488 | tf_op jit(solution)/shard_map/ppermute | solution.py:258
  63.9 6.4 %collective-permute-done.25.refs_4_ = bf16[40,1152]{1,0:T(8,128)(2,1)S(1)} collective-permute-done((bf16[40,1152]{1,0:T(8,128)(2,1)S(1)}, bf16[40,1152]{1,0:T(8,128)(2,1)S(1)}, u32[]{:S(2)}, u32[]{:S(2)}) %collective-permute-start.25) | collective-permute-done | bytes 92192 | tf_op jit(solution)/shard_map/ppermute | solution.py:258
  70.3 1.6 %collective-permute-done.26.refs_5_ = bf16[40,1152]{1,0:T(8,128)(2,1)S(1)} collective-permute-done((bf16[40,1152]{1,0:T(8,128)(2,1)S(1)}, bf16[40,1152]{1,0:T(8,128)(2,1)S(1)}, u32[]{:S(2)}, u32[]{:S(2)}) %collective-permute-start.26) | collective-permute-done | bytes 92192 | tf_op jit(solution)/shard_map/ppermute | solution.py:258
  71.9 1.0 %shard_map.81 = (bf16[40,3072]{1,0:T(8,128)(2,1)}, bf16[40,3072]{1,0:T(8,128)(2,1)}, bf16[40,3072]{1,0:T(8,128)(2,1)}) custom-call(bf16[40,1152]{1,0:T(8,128)(2,1)S(1)} %get-tuple-element.35.refs_0_, bf16[40,1152]{1,0:T(8,128)(2,1)S(1)} %collective-permute-done.22.refs_1_, bf16[40,1152]{1,0:T(8,128)(2,1)S(1)} %collective-permute-done.23.refs_2_, ...), custom_call_target="tpu_custom_call" | custom-call | bytes 1474560 | tf_op jit(solution)/shard_map/pallas_call | solution.py:35
  (42 shorter events, 2.8 us)
Async XLA Ops:
  4.9 6.6 %copy-start.1 = (bf16[40,3072]{1,0:T(8,128)(2,1)S(1)}, bf16[40,3072]{1,0:T(8,128)(2,1)}, u32[]{:S(2)}) copy-start(bf16[40,3072]{1,0:T(8,128)(2,1)} %refs_0_.5) | copy-start | bytes 737284
  4.9 6.6 %copy-start.2 = (bf16[40,3072]{1,0:T(8,128)(2,1)S(1)}, bf16[40,3072]{1,0:T(8,128)(2,1)}, u32[]{:S(2)}) copy-start(bf16[40,3072]{1,0:T(8,128)(2,1)} %refs_1_.5) | copy-start | bytes 737284
  4.9 6.6 %copy-start.3 = (bf16[40,3072]{1,0:T(8,128)(2,1)S(1)}, bf16[40,3072]{1,0:T(8,128)(2,1)}, u32[]{:S(2)}) copy-start(bf16[40,3072]{1,0:T(8,128)(2,1)} %refs_2_.5) | copy-start | bytes 737284
  4.9 18.9 %collective-permute-start = (bf16[20,3072]{1,0:T(8,128)(2,1)S(1)}, bf16[20,3072]{1,0:T(8,128)(2,1)S(1)}, u32[]{:S(2)}, u32[]{:S(2)}) collective-permute-start(bf16[20,3072]{1,0:T(8,128)(2,1)S(1)} %get-tuple-element.24), channel_id=1, source_target_pairs={{0,1},{1,0},{2,3},{3,2},{4,5},{5,4},{6,7},{7,6},{8,9},{9,8},{10,11... | collective-permute-start | bytes 368648 | tf_op jit(solution)/shard_map/ppermute | solution.py:268
  8.8 11.6 %collective-permute-start.4 = (bf16[40,1152]{1,0:T(8,128)(2,1)S(1)}, bf16[40,1152]{1,0:T(8,128)(2,1)S(1)}, u32[]{:S(2)}, u32[]{:S(2)}) collective-permute-start(bf16[40,1152]{1,0:T(8,128)(2,1)S(1)} %shard_map.78), channel_id=1, source_target_pairs={{0,16},{2,18},{4,20},{6,22},{8,24},{10,26},{12,28},{14,30},{16,0},... | collective-permute-start | bytes 276488 | tf_op jit(solution)/shard_map/ppermute | solution.py:258
  11.5 11.8 %collective-permute-start.6 = (bf16[40,1152]{1,0:T(8,128)(2,1)S(1)}, bf16[40,1152]{1,0:T(8,128)(2,1)S(1)}, u32[]{:S(2)}, u32[]{:S(2)}) collective-permute-start(bf16[40,1152]{1,0:T(8,128)(2,1)S(1)} %get-tuple-element.30), channel_id=1, source_target_pairs={{0,20},{2,22},{4,16},{6,18},{8,28},{10,30},{12,24},{14,26},{16,4},... | collective-permute-start | bytes 276488 | tf_op jit(solution)/shard_map/ppermute | solution.py:258
  12.8 10.5 %collective-permute-start.8 = (bf16[40,1152]{1,0:T(8,128)(2,1)S(1)}, bf16[40,1152]{1,0:T(8,128)(2,1)S(1)}, u32[]{:S(2)}, u32[]{:S(2)}) collective-permute-start(bf16[40,1152]{1,0:T(8,128)(2,1)S(1)} %get-tuple-element.32), channel_id=1, source_target_pairs={{0,24},{2,26},{4,28},{6,30},{8,16},{10,18},{12,20},{14,22},{16,8},... | collective-permute-start | bytes 276488 | tf_op jit(solution)/shard_map/ppermute | solution.py:258
  20.4 14.9 %collective-permute-start.15 = (bf16[40,1152]{1,0:T(8,128)(2,1)S(1)}, bf16[40,1152]{1,0:T(8,128)(2,1)S(1)}, u32[]{:S(2)}, u32[]{:S(2)}) collective-permute-start(bf16[40,1152]{1,0:T(8,128)(2,1)S(1)} %collective-permute-done.4.refs_4_), channel_id=1, source_target_pairs={{0,2},{2,0},{4,6},{6,4},{8,10},{10,8},{12,14},{14,12},{16,18},{18,... | collective-permute-start | bytes 276488 | tf_op jit(solution)/shard_map/ppermute | solution.py:258
  23.3 14.6 %collective-permute-start.17 = (bf16[40,1152]{1,0:T(8,128)(2,1)S(1)}, bf16[40,1152]{1,0:T(8,128)(2,1)S(1)}, u32[]{:S(2)}, u32[]{:S(2)}) collective-permute-start(bf16[40,1152]{1,0:T(8,128)(2,1)S(1)} %collective-permute-done.6.refs_6_), channel_id=1, source_target_pairs={{0,2},{2,0},{4,6},{6,4},{8,10},{10,8},{12,14},{14,12},{16,18},{18,... | collective-permute-start | bytes 276488 | tf_op jit(solution)/shard_map/ppermute | solution.py:258
  23.3 19.1 %collective-permute-start.19 = (bf16[40,1152]{1,0:T(8,128)(2,1)S(1)}, bf16[40,1152]{1,0:T(8,128)(2,1)S(1)}, u32[]{:S(2)}, u32[]{:S(2)}) collective-permute-start(bf16[40,1152]{1,0:T(8,128)(2,1)S(1)} %collective-permute-done.8.refs_8_), channel_id=1, source_target_pairs={{0,2},{2,0},{4,6},{6,4},{8,10},{10,8},{12,14},{14,12},{16,18},{18,... | collective-permute-start | bytes 276488 | tf_op jit(solution)/shard_map/ppermute | solution.py:258
  24.0 5.3 %collective-permute-start.5 = (bf16[40,384]{1,0:T(8,128)(2,1)S(1)}, bf16[40,384]{1,0:T(8,128)(2,1)S(1)}, u32[]{:S(2)}, u32[]{:S(2)}) collective-permute-start(bf16[40,384]{1,0:T(8,128)(2,1)S(1)} %get-tuple-element.29), channel_id=1, source_target_pairs={{0,16},{2,18},{4,20},{6,22},{8,24},{10,26},{12,28},{14,30},{16,0},... | collective-permute-start | bytes 92168 | tf_op jit(solution)/shard_map/ppermute | solution.py:258
  26.6 6.9 %collective-permute-start.7 = (bf16[40,384]{1,0:T(8,128)(2,1)S(1)}, bf16[40,384]{1,0:T(8,128)(2,1)S(1)}, u32[]{:S(2)}, u32[]{:S(2)}) collective-permute-start(bf16[40,384]{1,0:T(8,128)(2,1)S(1)} %get-tuple-element.31), channel_id=1, source_target_pairs={{0,20},{2,22},{4,16},{6,18},{8,28},{10,30},{12,24},{14,26},{16,4},... | collective-permute-start | bytes 92168 | tf_op jit(solution)/shard_map/ppermute | solution.py:258
  29.3 6.0 %collective-permute-start.9 = (bf16[40,384]{1,0:T(8,128)(2,1)S(1)}, bf16[40,384]{1,0:T(8,128)(2,1)S(1)}, u32[]{:S(2)}, u32[]{:S(2)}) collective-permute-start(bf16[40,384]{1,0:T(8,128)(2,1)S(1)} %get-tuple-element.33), channel_id=1, source_target_pairs={{0,24},{2,26},{4,28},{6,30},{8,16},{10,18},{12,20},{14,22},{16,8},... | collective-permute-start | bytes 92168 | tf_op jit(solution)/shard_map/ppermute | solution.py:258
  33.4 12.7 %collective-permute-start.1 = (bf16[40,1536]{1,0:T(8,128)(2,1)S(1)}, bf16[40,1536]{1,0:T(8,128)(2,1)S(1)}, u32[]{:S(2)}, u32[]{:S(2)}) collective-permute-start(bf16[40,1536]{1,0:T(8,128)(2,1)S(1)} %get-tuple-element.26), channel_id=1, source_target_pairs={{0,4},{2,6},{4,0},{6,2},{8,12},{10,14},{12,8},{14,10},{16,20},{18,... | collective-permute-start | bytes 368648 | tf_op jit(solution)/shard_map/ppermute | solution.py:258
  35.3 11.2 %collective-permute-start.2 = (bf16[40,1536]{1,0:T(8,128)(2,1)S(1)}, bf16[40,1536]{1,0:T(8,128)(2,1)S(1)}, u32[]{:S(2)}, u32[]{:S(2)}) collective-permute-start(bf16[40,1536]{1,0:T(8,128)(2,1)S(1)} %get-tuple-element.27), channel_id=1, source_target_pairs={{0,8},{2,10},{4,12},{6,14},{8,0},{10,2},{12,4},{14,6},{16,24},{18,... | collective-permute-start | bytes 368648 | tf_op jit(solution)/shard_map/ppermute | solution.py:258
  35.3 11.4 %collective-permute-start.3 = (bf16[40,1536]{1,0:T(8,128)(2,1)S(1)}, bf16[40,1536]{1,0:T(8,128)(2,1)S(1)}, u32[]{:S(2)}, u32[]{:S(2)}) collective-permute-start(bf16[40,1536]{1,0:T(8,128)(2,1)S(1)} %get-tuple-element.28), channel_id=1, source_target_pairs={{0,12},{2,14},{4,8},{6,10},{8,4},{10,6},{12,0},{14,2},{16,28},{18,... | collective-permute-start | bytes 368648 | tf_op jit(solution)/shard_map/ppermute | solution.py:258
  37.9 9.1 %collective-permute-start.10 = (bf16[40,1536]{1,0:T(8,128)(2,1)S(1)}, bf16[40,1536]{1,0:T(8,128)(2,1)S(1)}, u32[]{:S(2)}, u32[]{:S(2)}) collective-permute-start(bf16[40,1536]{1,0:T(8,128)(2,1)S(1)} %get-tuple-element.34), channel_id=1, source_target_pairs={{0,28},{2,30},{4,24},{6,26},{8,20},{10,22},{12,16},{14,18},{16,12}... | collective-permute-start | bytes 368648 | tf_op jit(solution)/shard_map/ppermute | solution.py:258
  42.4 1.2 %collective-permute-start.16 = (bf16[40,384]{1,0:T(8,128)(2,1)S(1)}, bf16[40,384]{1,0:T(8,128)(2,1)S(1)}, u32[]{:S(2)}, u32[]{:S(2)}) collective-permute-start(bf16[40,384]{1,0:T(8,128)(2,1)S(1)} %collective-permute-done.5.refs_5_), channel_id=1, source_target_pairs={{0,2},{2,0},{4,6},{6,4},{8,10},{10,8},{12,14},{14,12},{16,18},{18,... | collective-permute-start | bytes 92168 | tf_op jit(solution)/shard_map/ppermute | solution.py:258
  43.6 1.2 %collective-permute-start.18 = (bf16[40,384]{1,0:T(8,128)(2,1)S(1)}, bf16[40,384]{1,0:T(8,128)(2,1)S(1)}, u32[]{:S(2)}, u32[]{:S(2)}) collective-permute-start(bf16[40,384]{1,0:T(8,128)(2,1)S(1)} %collective-permute-done.7.refs_7_), channel_id=1, source_target_pairs={{0,2},{2,0},{4,6},{6,4},{8,10},{10,8},{12,14},{14,12},{16,18},{18,... | collective-permute-start | bytes 92168 | tf_op jit(solution)/shard_map/ppermute | solution.py:258
  44.8 1.2 %collective-permute-start.20 = (bf16[40,384]{1,0:T(8,128)(2,1)S(1)}, bf16[40,384]{1,0:T(8,128)(2,1)S(1)}, u32[]{:S(2)}, u32[]{:S(2)}) collective-permute-start(bf16[40,384]{1,0:T(8,128)(2,1)S(1)} %collective-permute-done.9.refs_9_), channel_id=1, source_target_pairs={{0,2},{2,0},{4,6},{6,4},{8,10},{10,8},{12,14},{14,12},{16,18},{18,... | collective-permute-start | bytes 92168 | tf_op jit(solution)/shard_map/ppermute | solution.py:258
  46.0 1.3 %collective-permute-start.11 = (bf16[40,1536]{1,0:T(8,128)(2,1)S(1)}, bf16[40,1536]{1,0:T(8,128)(2,1)S(1)}, u32[]{:S(2)}, u32[]{:S(2)}) collective-permute-start(bf16[40,1536]{1,0:T(8,128)(2,1)S(1)} %get-tuple-element.25.refs_0_), channel_id=1, source_target_pairs={{0,2},{2,0},{4,6},{6,4},{8,10},{10,8},{12,14},{14,12},{16,18},{18,... | collective-permute-start | bytes 368648 | tf_op jit(solution)/shard_map/ppermute | solution.py:258
  46.2 1.3 %collective-permute-start.12 = (bf16[40,1536]{1,0:T(8,128)(2,1)S(1)}, bf16[40,1536]{1,0:T(8,128)(2,1)S(1)}, u32[]{:S(2)}, u32[]{:S(2)}) collective-permute-start(bf16[40,1536]{1,0:T(8,128)(2,1)S(1)} %collective-permute-done.1.refs_1_), channel_id=1, source_target_pairs={{0,2},{2,0},{4,6},{6,4},{8,10},{10,8},{12,14},{14,12},{16,18},{18,... | collective-permute-start | bytes 368648 | tf_op jit(solution)/shard_map/ppermute | solution.py:258
  46.5 1.3 %collective-permute-start.13 = (bf16[40,1536]{1,0:T(8,128)(2,1)S(1)}, bf16[40,1536]{1,0:T(8,128)(2,1)S(1)}, u32[]{:S(2)}, u32[]{:S(2)}) collective-permute-start(bf16[40,1536]{1,0:T(8,128)(2,1)S(1)} %collective-permute-done.2.refs_2_), channel_id=1, source_target_pairs={{0,2},{2,0},{4,6},{6,4},{8,10},{10,8},{12,14},{14,12},{16,18},{18,... | collective-permute-start | bytes 368648 | tf_op jit(solution)/shard_map/ppermute | solution.py:258
  46.7 1.3 %collective-permute-start.14 = (bf16[40,1536]{1,0:T(8,128)(2,1)S(1)}, bf16[40,1536]{1,0:T(8,128)(2,1)S(1)}, u32[]{:S(2)}, u32[]{:S(2)}) collective-permute-start(bf16[40,1536]{1,0:T(8,128)(2,1)S(1)} %collective-permute-done.3.refs_3_), channel_id=1, source_target_pairs={{0,2},{2,0},{4,6},{6,4},{8,10},{10,8},{12,14},{14,12},{16,18},{18,... | collective-permute-start | bytes 368648 | tf_op jit(solution)/shard_map/ppermute | solution.py:258
  47.0 1.3 %collective-permute-start.21 = (bf16[40,1536]{1,0:T(8,128)(2,1)S(1)}, bf16[40,1536]{1,0:T(8,128)(2,1)S(1)}, u32[]{:S(2)}, u32[]{:S(2)}) collective-permute-start(bf16[40,1536]{1,0:T(8,128)(2,1)S(1)} %collective-permute-done.10.refs_10_), channel_id=1, source_target_pairs={{0,2},{2,0},{4,6},{6,4},{8,10},{10,8},{12,14},{14,12},{16,18},{18,... | collective-permute-start | bytes 368648 | tf_op jit(solution)/shard_map/ppermute | solution.py:258
  52.7 6.0 %collective-permute-start.22 = (bf16[40,1152]{1,0:T(8,128)(2,1)S(1)}, bf16[40,1152]{1,0:T(8,128)(2,1)S(1)}, u32[]{:S(2)}, u32[]{:S(2)}) collective-permute-start(bf16[40,1152]{1,0:T(8,128)(2,1)S(1)} %get-tuple-element.36), channel_id=1, source_target_pairs={{0,4},{2,6},{4,0},{6,2},{8,12},{10,14},{12,8},{14,10},{16,20},{18,... | collective-permute-start | bytes 276488 | tf_op jit(solution)/shard_map/ppermute | solution.py:258
  52.9 9.3 %collective-permute-start.23 = (bf16[40,1152]{1,0:T(8,128)(2,1)S(1)}, bf16[40,1152]{1,0:T(8,128)(2,1)S(1)}, u32[]{:S(2)}, u32[]{:S(2)}) collective-permute-start(bf16[40,1152]{1,0:T(8,128)(2,1)S(1)} %get-tuple-element.37), channel_id=1, source_target_pairs={{0,8},{2,10},{4,12},{6,14},{8,0},{10,2},{12,4},{14,6},{16,24},{18,... | collective-permute-start | bytes 276488 | tf_op jit(solution)/shard_map/ppermute | solution.py:258
  52.9 11.0 %collective-permute-start.24 = (bf16[40,1152]{1,0:T(8,128)(2,1)S(1)}, bf16[40,1152]{1,0:T(8,128)(2,1)S(1)}, u32[]{:S(2)}, u32[]{:S(2)}) collective-permute-start(bf16[40,1152]{1,0:T(8,128)(2,1)S(1)} %get-tuple-element.38), channel_id=1, source_target_pairs={{0,12},{2,14},{4,8},{6,10},{8,4},{10,6},{12,0},{14,2},{16,28},{18,... | collective-permute-start | bytes 276488 | tf_op jit(solution)/shard_map/ppermute | solution.py:258
  56.2 14.1 %collective-permute-start.25 = (bf16[40,1152]{1,0:T(8,128)(2,1)S(1)}, bf16[40,1152]{1,0:T(8,128)(2,1)S(1)}, u32[]{:S(2)}, u32[]{:S(2)}) collective-permute-start(bf16[40,1152]{1,0:T(8,128)(2,1)S(1)} %get-tuple-element.39), channel_id=1, source_target_pairs={{0,16},{2,18},{4,20},{6,22},{8,24},{10,26},{12,28},{14,30},{16,0},... | collective-permute-start | bytes 276488 | tf_op jit(solution)/shard_map/ppermute | solution.py:258
  56.8 15.1 %collective-permute-start.26 = (bf16[40,1152]{1,0:T(8,128)(2,1)S(1)}, bf16[40,1152]{1,0:T(8,128)(2,1)S(1)}, u32[]{:S(2)}, u32[]{:S(2)}) collective-permute-start(bf16[40,1152]{1,0:T(8,128)(2,1)S(1)} %get-tuple-element.40), channel_id=1, source_target_pairs={{0,20},{2,22},{4,16},{6,18},{8,28},{10,30},{12,24},{14,26},{16,4},... | collective-permute-start | bytes 276488 | tf_op jit(solution)/shard_map/ppermute | solution.py:258
  58.7 13.2 %collective-permute-start.27 = (bf16[40,1152]{1,0:T(8,128)(2,1)S(1)}, bf16[40,1152]{1,0:T(8,128)(2,1)S(1)}, u32[]{:S(2)}, u32[]{:S(2)}) collective-permute-start(bf16[40,1152]{1,0:T(8,128)(2,1)S(1)} %get-tuple-element.41), channel_id=1, source_target_pairs={{0,24},{2,26},{4,28},{6,30},{8,16},{10,18},{12,20},{14,22},{16,8},... | collective-permute-start | bytes 276488 | tf_op jit(solution)/shard_map/ppermute | solution.py:258
  62.1 9.8 %collective-permute-start.28 = (bf16[40,1152]{1,0:T(8,128)(2,1)S(1)}, bf16[40,1152]{1,0:T(8,128)(2,1)S(1)}, u32[]{:S(2)}, u32[]{:S(2)}) collective-permute-start(bf16[40,1152]{1,0:T(8,128)(2,1)S(1)} %get-tuple-element.42), channel_id=1, source_target_pairs={{0,28},{2,30},{4,24},{6,26},{8,20},{10,22},{12,16},{14,18},{16,12}... | collective-permute-start | bytes 276488 | tf_op jit(solution)/shard_map/ppermute | solution.py:258
  (2 other events, 3.0 us)
